TPU v7x, 32 devices: a whole 2x2x4 slice. The times are simulated.
32 devices in a mesh: clip: 2 (over y), tile: 8 (over z, x), tm: 2 (over core).
Axes of the slice: x: 2, y: 2, z: 4, core: 2. Of those that a mesh axis runs over, the one named last changes fastest.
Arguments:
- frames_in: bfloat16 [16, 32, 128, 256], P(('clip', 'tm'), 'tile'), parts along dimension 0, may hold values from -6 to 6
- grad_out: bfloat16 [16, 32, 128, 256], P(('clip', 'tm'), 'tile'), parts along dimension 0, may hold values from -6 to 6
- gain_first: float32 [256], replicated, may hold values from 0.5 to 1.5
- gain_second: float32 [256], replicated, may hold values from 0.5 to 1.5
- spatial_first: bfloat16 [3, 3, 256, 256], replicated, may hold values from -0.125 to 0.125
- temporal_first: bfloat16 [3, 256, 256], replicated, may hold values from -0.21875 to 0.21875
- spatial_second: bfloat16 [3, 3, 256, 256], replicated, may hold values from -0.125 to 0.125
- temporal_second: bfloat16 [3, 256, 256], replicated, may hold values from -0.21875 to 0.21875
Outputs:
- grad_in: bfloat16 [16, 32, 128, 256], P(('clip', 'tm'), 'tile'), parts along dimension 0
There are 2 independent parts, one for each index of `clip`. A program takes and returns all parts, laid end to end along the dimension named above; an argument that names none is the same for every part. Nothing has to cross between parts.
All inputs are finite; a program needn't handle non-finite values.
Results may differ from a plain program's by a relative error of at most 0.0054.
Values may be sent and summed in bfloat16 or wider, within the bound.
No kernel may reach another device: no remote copies, remote signals or barrier semaphores. Data moves between devices by JAX's collectives and lax.ppermute only.
A program may use at most 64 MiB of HBM per device.

v0:
```python
import jax
import jax.numpy as jnp
from jax import lax
from jax.sharding import PartitionSpec as P

EPS = 1e-06


def padded_2(cells, sides, width):
    for axis, dim in sides:
        count = lax.axis_size(axis)
        ends = count - 1
        head = lax.slice_in_dim(cells, 0, width, axis=dim)
        tail = lax.slice_in_dim(cells, cells.shape[dim] - width, cells.shape[dim], axis=dim)
        cells = jnp.concatenate(
            [
                lax.ppermute(tail, axis, [(i, (i + 1) % count) for i in range(ends)]),
                cells,
                lax.ppermute(head, axis, [((i + 1) % count, i) for i in range(ends)]),
            ],
            axis=dim,
        )
    return cells


def passed_along(block, axis, distance):
    devices = range(lax.axis_size(axis))
    route = [(i - distance, i) for i in devices if i - distance in devices]
    return lax.ppermute(block, axis, route)


def rms_scale(values):
    return lax.rsqrt(jnp.mean(values * values, axis=-1, keepdims=True) + EPS)


def silu_slope(values):
    logistic = jax.nn.sigmoid(values)
    return logistic * (1.0 + values * (1.0 - logistic))


def norm_back(upstream, values, inv_scale, gain_vec):
    scaled = upstream * gain_vec
    unit_vals = values * inv_scale
    return inv_scale * (scaled - unit_vals * jnp.mean(scaled * unit_vals, axis=-1, keepdims=True))


def spatial_valid(inputs, kernel):
    return lax.conv_general_dilated(
        inputs,
        kernel,
        (1, 1),
        ((0, 0), (1, 1)),
        dimension_numbers=("NHWC", "HWIO", "NHWC"),
        preferred_element_type=jnp.float32,
    )


def flipped(kernel):
    return jnp.transpose(jnp.flip(kernel, (0, 1)), (0, 1, 3, 2))


def row_rims(inputs):
    return padded_2(inputs, (("tile", 1),), 1)


def time_taps(padded, kernel, frame_count):
    channels = padded.shape[-1]
    running = jnp.zeros((frame_count * padded.shape[1] * padded.shape[2], channels), jnp.float32)
    for k in range(3):
        running = running + jnp.dot(
            padded[k : k + frame_count].reshape(-1, channels),
            kernel[k],
            preferred_element_type=jnp.float32,
        )
    return running.reshape((frame_count,) + padded.shape[1:])


def time_back(upstream, kernel, at_start):
    frame_count = upstream.shape[0]
    later_rows = passed_along(upstream[:2], "tm", -1)
    zero_edge = jnp.zeros_like(later_rows)
    padded = jnp.concatenate([zero_edge, upstream, later_rows], 0)
    kernel_back = jnp.transpose(kernel[::-1], (0, 2, 1))
    all_taps = time_taps(padded, kernel_back, frame_count + 2)
    own_taps = all_taps[2:]
    head_tap = own_taps[:1] + jnp.where(at_start, all_taps[:1] + all_taps[1:2], 0.0)
    return jnp.concatenate([head_tap, own_taps[1:]], 0)


def on_device(
    frames_in,
    grad_out,
    gain_first,
    gain_second,
    spatial_first,
    temporal_first,
    spatial_second,
    temporal_second,
):
    frame_count = frames_in.shape[0]
    at_start = lax.axis_index("tm") == 0
    values_one = frames_in.astype(jnp.float32)
    scale_one = rms_scale(values_one)
    normed_one = values_one * scale_one * gain_first
    active_one = jax.nn.silu(normed_one).astype(jnp.bfloat16)
    active_wide = row_rims(active_one)
    spatial_out = spatial_valid(active_wide, spatial_first).astype(jnp.bfloat16)
    received = passed_along(spatial_out[-2:], "tm", 1)
    repeated = jnp.concatenate([spatial_out[:1], spatial_out[:1]], 0)
    earlier = jnp.where(at_start, repeated, received)
    hidden_one = time_taps(jnp.concatenate([earlier, spatial_out], 0), temporal_first, frame_count)
    scale_two = rms_scale(hidden_one)
    normed_two = hidden_one * scale_two * gain_second
    grad_space_two = time_back(grad_out, temporal_second, at_start).astype(jnp.bfloat16)
    space_wide = row_rims(grad_space_two)
    grad_act_two = spatial_valid(space_wide, flipped(spatial_second))
    grad_hidden = norm_back(
        grad_act_two * silu_slope(normed_two), hidden_one, scale_two, gain_second
    ).astype(jnp.bfloat16)
    grad_space_one = time_back(grad_hidden, temporal_first, at_start).astype(jnp.bfloat16)
    grad_act_one = spatial_valid(row_rims(grad_space_one), flipped(spatial_first))
    grad_input = norm_back(grad_act_one * silu_slope(normed_one), values_one, scale_one, gain_first)
    return (grad_out.astype(jnp.float32) + grad_input).astype(jnp.bfloat16)


def solution(mesh):
    return jax.shard_map(
        on_device,
        mesh=mesh,
        in_specs=(
            P(("clip", "tm"), "tile", None, None),
            P(("clip", "tm"), "tile", None, None),
            P(),
            P(),
            P(),
            P(),
            P(),
            P(),
        ),
        out_specs=P(("clip", "tm"), "tile", None, None),
        check_vma=False,
    )
```

profile of v0, /device:TPU:24, one launch (start us, length us, event | category | flops | bytes accessed | tf_op | source)
XLA Modules:
  0.0 103.9 jit_solution(3191551875071585499)
XLA Ops:
  0.0 1.7 %fusion.22 = f32[4,4,128]{2,1,0:T(4,128)S(1)} fusion(bf16[4,4,128,256]{3,2,1,0:T(8,128)(2,1)} %param.8), kind=kLoop, calls=%fused_computation.32 | loop fusion | flops 1570816 | bytes 1056768 | tf_op jit(solution)/shard_map/reduce_sum | solution.py:33
  1.8 1.9 %fusion.12 = bf16[4,4,128,256]{3,2,1,0:T(8,128)(2,1)S(1)} fusion(bf16[4,4,128,256]{3,2,1,0:T(8,128)(2,1)} %param.8, f32[256]{0:T(256)} %param.10, f32[4,4,128]{2,1,0:T(4,128)S(1)} %add_rsqrt_fusion.1), kind=kLoop, calls=%fused_computation.22 | loop fusion | flops 4194304 | bytes 2106368 | tf_op jit(solution)/shard_map/convert_element_type | solution.py:105
  4.5 3.4 %collective-permute-start = (bf16[4,1,128,256]{3,2,1,0:T(8,128)(2,1)}, bf16[4,1,128,256]{3,2,1,0:T(8,128)(2,1)S(1)}, u32[]{:S(2)}, u32[]{:S(2)}) collective-permute-start(bf16[4,1,128,256]{3,2,1,0:T(8,128)(2,1)} %get-tuple-element.17), channel_id=1, source_target_pairs={{0,2},{2,4},{4,6},{6,8},{8,10},{10,12},{12,14},{1,3},{3,5},{5,7},{... | collective-permute-start | bytes 786440 | tf_op jit(solution)/shard_map/ppermute | solution.py:17
  7.9 3.3 %collective-permute-start.1 = (bf16[4,1,128,256]{3,2,1,0:T(8,128)(2,1)}, bf16[4,1,128,256]{3,2,1,0:T(8,128)(2,1)}, u32[]{:S(2)}, u32[]{:S(2)}) collective-permute-start(bf16[4,1,128,256]{3,2,1,0:T(8,128)(2,1)} %get-tuple-element.18), channel_id=1, source_target_pairs={{2,0},{4,2},{6,4},{8,6},{10,8},{12,10},{14,12},{3,1},{5,3},{7,5},{... | collective-permute-start | bytes 786440 | tf_op jit(solution)/shard_map/ppermute | solution.py:19
  15.6 5.6 %collective-permute-done.1 = bf16[4,1,128,256]{3,2,1,0:T(8,128)(2,1)} collective-permute-done((bf16[4,1,128,256]{3,2,1,0:T(8,128)(2,1)}, bf16[4,1,128,256]{3,2,1,0:T(8,128)(2,1)}, u32[]{:S(2)}, u32[]{:S(2)}) %collective-permute-start.1) | collective-permute-done | bytes 262176 | tf_op jit(solution)/shard_map/ppermute | solution.py:19
  25.2 2.8 %select_convert_fusion = bf16[4,32,17,256]{3,1,2,0:T(8,128)(2,1)S(1)} fusion(bf16[3,3,256,256]{3,2,1,0:T(8,128)(2,1)S(1)} %copy-done, bf16[6,4,8,19,256]{4,1,3,2,0:T(4,128)(2,1)S(1)} %fusion.25, pred[32,17]{0,1:T(8,128)(4,1)S(1)} %copy-done.9), kind=kOutput, calls=%fused_computation.18 | convolution fusion | flops 2568028160 | bytes 4162080 | tf_op jit(solution)/shard_map/conv_general_dilated | solution.py:48
  28.9 1.5 %pad_maximum_fusion.4 = (bf16[6,4,128,256]{3,2,1,0:T(8,128)(2,1)S(1)}, bf16[6,4,128,256]{3,2,1,0:T(8,128)(2,1)S(1)}, bf16[6,4,128,256]{3,2,1,0:T(8,128)(2,1)S(1)}) fusion(bf16[2,4,128,256]{3,2,1,0:T(8,128)(2,1)} %collective-permute-done.3, bf16[4,4,128,256]{3,2,1,0:T(8,128)(2,1)S(1)} %copy-done.4, bf16[6]{0:T(256)(128)(2,1)S(1)} %pad_slice_fusion.2), kind=kLoop, calls=%fused_computation.61 | loop fusion | flops 2359296 | bytes 6291468 | tf_op jit(solution)/shard_map/concatenate | solution.py:82
  34.1 1.9 %collective-permute-start.4 = (bf16[4,1,128,256]{3,0,2,1:T(4,128)(2,1)S(1)}, bf16[4,1,128,256]{3,0,2,1:T(4,128)(2,1)S(1)}, u32[]{:S(2)}, u32[]{:S(2)}) collective-permute-start(bf16[4,1,128,256]{3,0,2,1:T(4,128)(2,1)S(1)} %get-tuple-element.9), channel_id=1, source_target_pairs={{0,2},{2,4},{4,6},{6,8},{8,10},{10,12},{12,14},{1,3},{3,5},{5,7},{... | collective-permute-start | bytes 786440 | tf_op jit(solution)/shard_map/ppermute | solution.py:17
  36.1 5.0 %collective-permute-start.5 = (bf16[4,1,128,256]{3,0,2,1:T(4,128)(2,1)S(1)}, bf16[4,1,128,256]{3,0,2,1:T(4,128)(2,1)S(1)}, u32[]{:S(2)}, u32[]{:S(2)}) collective-permute-start(bf16[4,1,128,256]{3,0,2,1:T(4,128)(2,1)S(1)} %get-tuple-element.10), channel_id=1, source_target_pairs={{2,0},{4,2},{6,4},{8,6},{10,8},{12,10},{14,12},{3,1},{5,3},{7,5},{... | collective-permute-start | bytes 786440 | tf_op jit(solution)/shard_map/ppermute | solution.py:19
  43.2 2.0 %collective-permute-done.4 = bf16[4,1,128,256]{3,0,2,1:T(4,128)(2,1)S(1)} collective-permute-done((bf16[4,1,128,256]{3,0,2,1:T(4,128)(2,1)S(1)}, bf16[4,1,128,256]{3,0,2,1:T(4,128)(2,1)S(1)}, u32[]{:S(2)}, u32[]{:S(2)}) %collective-permute-start.4) | collective-permute-done | bytes 262176 | tf_op jit(solution)/shard_map/ppermute | solution.py:17
  45.3 5.5 %collective-permute-done.5 = bf16[4,1,128,256]{3,0,2,1:T(4,128)(2,1)S(1)} collective-permute-done((bf16[4,1,128,256]{3,0,2,1:T(4,128)(2,1)S(1)}, bf16[4,1,128,256]{3,0,2,1:T(4,128)(2,1)S(1)}, u32[]{:S(2)}, u32[]{:S(2)}) %collective-permute-start.5) | collective-permute-done | bytes 262176 | tf_op jit(solution)/shard_map/ppermute | solution.py:19
  54.1 3.0 %fusion.37 = f32[4,32,17,256]{3,1,2,0:T(8,128)S(1)} fusion(bf16[3,3,256,256]{3,2,1,0:T(8,128)(2,1)S(1)} %copy-done.8, bf16[6,4,8,19,256]{4,1,3,2,0:T(4,128)(2,1)S(1)} %fusion.26, pred[32,17]{0,1:T(8,128)(4,1)S(1)} %copy-done.9), kind=kOutput, calls=%fused_computation.65 | convolution fusion | flops 2567471104 | bytes 5276192 | tf_op jit(solution)/shard_map/conv_general_dilated | solution.py:48
  57.0 1.4 %copy.63 = f32[4,32,17,256]{3,0,2,1:T(4,128)S(1)} copy(f32[4,32,17,256]{3,1,2,0:T(8,128)S(1)} %fusion.37) | data formatting | bytes 4456448 | tf_op jit(solution)/shard_map/conv_general_dilated | solution.py:48
  63.8 1.5 %multiply_reduce_fusion = f32[4,4,128]{2,1,0:T(4,128)S(1)} fusion(f32[4,4,128,256]{3,2,1,0:T(8,128)S(1)} %bitcast.108, f32[4,4,128]{2,1,0:T(4,128)S(1)} %bitcast.131, f32[256]{0:T(256)S(1)} %copy-done.7, f32[4,4,128,256]{3,0,2,1:T(4,128)S(1)} %slice.180), kind=kLoop, calls=%fused_computation.38 | loop fusion | flops 6813696 | bytes 4211712 | tf_op jit(solution)/shard_map/reduce_sum | solution.py:44
  65.2 1.4 %multiply_convert_fusion = bf16[4,4,128,256]{3,2,1,0:T(8,128)(2,1)S(1)} fusion(f32[4,4,128]{2,1,0:T(4,128)S(1)} %broadcast_multiply_fusion.1, f32[4,4,128]{2,1,0:T(4,128)S(1)} %bitcast.132, f32[256]{0:T(256)S(1)} %copy-done.7, f32[4,4,128,256]{3,0,2,1:T(4,128)S(1)} %slice.180, f32[2048,256]{1,0:T(8,128)S(1)} %get-tuple-element.20), kind=kLoop, calls=%fused_computation.37 | loop fusion | flops 7864320 | bytes 5260288 | tf_op jit(solution)/shard_map/convert_element_type | solution.py:119
  66.7 1.5 %collective-permute-start.6 = (bf16[2,4,128,256]{3,2,1,0:T(8,128)(2,1)S(1)}, bf16[2,4,128,256]{3,2,1,0:T(8,128)(2,1)S(1)}, u32[]{:S(2)}, u32[]{:S(2)}) collective-permute-start(bf16[2,4,128,256]{3,2,1,0:T(8,128)(2,1)S(1)} %slice.182), channel_id=1, source_target_pairs={{1,0},{3,2},{5,4},{7,6},{9,8},{11,10},{13,12},{15,14},{17,16},{19,... | collective-permute-start | bytes 1572872 | tf_op jit(solution)/shard_map/ppermute | solution.py:29
  68.3 2.2 %collective-permute-done.6 = bf16[2,4,128,256]{3,2,1,0:T(8,128)(2,1)S(1)} collective-permute-done((bf16[2,4,128,256]{3,2,1,0:T(8,128)(2,1)S(1)}, bf16[2,4,128,256]{3,2,1,0:T(8,128)(2,1)S(1)}, u32[]{:S(2)}, u32[]{:S(2)}) %collective-permute-start.6) | collective-permute-done | bytes 524320 | tf_op jit(solution)/shard_map/ppermute | solution.py:29
  74.7 1.9 %collective-permute-start.7 = (bf16[4,1,128,256]{3,0,2,1:T(4,128)(2,1)S(1)}, bf16[4,1,128,256]{3,0,2,1:T(4,128)(2,1)S(1)}, u32[]{:S(2)}, u32[]{:S(2)}) collective-permute-start(bf16[4,1,128,256]{3,0,2,1:T(4,128)(2,1)S(1)} %get-tuple-element.5), channel_id=1, source_target_pairs={{0,2},{2,4},{4,6},{6,8},{8,10},{10,12},{12,14},{1,3},{3,5},{5,7},{... | collective-permute-start | bytes 786440 | tf_op jit(solution)/shard_map/ppermute | solution.py:17
  76.6 4.8 %collective-permute-start.8 = (bf16[4,1,128,256]{3,0,2,1:T(4,128)(2,1)S(1)}, bf16[4,1,128,256]{3,0,2,1:T(4,128)(2,1)S(1)}, u32[]{:S(2)}, u32[]{:S(2)}) collective-permute-start(bf16[4,1,128,256]{3,0,2,1:T(4,128)(2,1)S(1)} %get-tuple-element.6), channel_id=1, source_target_pairs={{2,0},{4,2},{6,4},{8,6},{10,8},{12,10},{14,12},{3,1},{5,3},{7,5},{... | collective-permute-start | bytes 786440 | tf_op jit(solution)/shard_map/ppermute | solution.py:19
  81.4 4.5 %collective-permute-done.7 = bf16[4,1,128,256]{3,0,2,1:T(4,128)(2,1)S(1)} collective-permute-done((bf16[4,1,128,256]{3,0,2,1:T(4,128)(2,1)S(1)}, bf16[4,1,128,256]{3,0,2,1:T(4,128)(2,1)S(1)}, u32[]{:S(2)}, u32[]{:S(2)}) %collective-permute-start.7) | collective-permute-done | bytes 262176 | tf_op jit(solution)/shard_map/ppermute | solution.py:17
  85.9 5.5 %collective-permute-done.8 = bf16[4,1,128,256]{3,0,2,1:T(4,128)(2,1)S(1)} collective-permute-done((bf16[4,1,128,256]{3,0,2,1:T(4,128)(2,1)S(1)}, bf16[4,1,128,256]{3,0,2,1:T(4,128)(2,1)S(1)}, u32[]{:S(2)}, u32[]{:S(2)}) %collective-permute-start.8) | collective-permute-done | bytes 262176 | tf_op jit(solution)/shard_map/ppermute | solution.py:19
  94.4 3.0 %fusion.40 = f32[4,32,17,256]{3,1,2,0:T(8,128)S(1)} fusion(bf16[3,3,256,256]{3,2,1,0:T(8,128)(2,1)S(1)} %copy-done, bf16[6,4,8,19,256]{4,1,3,2,0:T(4,128)(2,1)S(1)} %fusion.27, pred[32,17]{0,1:T(8,128)(4,1)S(1)} %copy-done.9), kind=kOutput, calls=%fused_computation.66 | convolution fusion | flops 2567471104 | bytes 5276192 | tf_op jit(solution)/shard_map/conv_general_dilated | solution.py:48
  100.0 1.5 %fusion.17 = f32[4,4,128]{2,1,0:T(4,128)S(1)} fusion(bf16[4,4,128,256]{3,2,1,0:T(8,128)(2,1)S(1)} %copy-done.1, f32[4,4,128]{2,1,0:T(4,128)S(1)} %add_rsqrt_fusion.1, f32[256]{0:T(256)S(1)} %copy-done.6, f32[4,4,128,256]{3,0,2,1:T(4,128)S(1)} %slice.191), kind=kLoop, calls=%fused_computation.27 | loop fusion | flops 7337984 | bytes 3163136 | tf_op jit(solution)/shard_map/reduce_sum | solution.py:44
  101.5 2.4 %fusion.21 = bf16[4,4,128,256]{3,2,1,0:T(8,128)(2,1)} fusion(bf16[4,4,128,256]{3,2,1,0:T(8,128)(2,1)S(1)} %copy-done.1, bf16[4,4,128,256]{3,2,1,0:T(8,128)(2,1)S(1)} %copy-done.4, f32[4,4,128]{2,1,0:T(4,128)S(1)} %broadcast_multiply_fusion, f32[4,4,128]{2,1,0:T(4,128)S(1)} %add_rsqrt_fusion.1, f32[256]{0:T(256)S(1)} %copy-done.6, ...), kind=kLoop, calls=%fused_computation.31 | loop fusion | flops 9437184 | bytes 5260288 | tf_op jit(solution)/shard_map/convert_element_type | solution.py:123
  (82 shorter events, 33.9 us)
Async XLA Ops:
  0.0 25.2 %copy-start = (bf16[3,3,256,256]{3,2,1,0:T(8,128)(2,1)S(1)}, bf16[3,3,256,256]{3,2,1,0:T(8,128)(2,1)}, u32[]{:S(2)}) copy-start(bf16[3,3,256,256]{3,2,1,0:T(8,128)(2,1)} %param.12) | copy-start | bytes 3538948
  0.0 11.2 %copy-start.4 = (bf16[4,4,128,256]{3,2,1,0:T(8,128)(2,1)S(1)}, bf16[4,4,128,256]{3,2,1,0:T(8,128)(2,1)}, u32[]{:S(2)}) copy-start(bf16[4,4,128,256]{3,2,1,0:T(8,128)(2,1)} %param.9) | copy-start | bytes 3145732
  4.5 11.1 %collective-permute-start = (bf16[4,1,128,256]{3,2,1,0:T(8,128)(2,1)}, bf16[4,1,128,256]{3,2,1,0:T(8,128)(2,1)S(1)}, u32[]{:S(2)}, u32[]{:S(2)}) collective-permute-start(bf16[4,1,128,256]{3,2,1,0:T(8,128)(2,1)} %get-tuple-element.17), channel_id=1, source_target_pairs={{0,2},{2,4},{4,6},{6,8},{8,10},{10,12},{12,14},{1,3},{3,5},{5,7},{... | collective-permute-start | bytes 786440 | tf_op jit(solution)/shard_map/ppermute | solution.py:17
  7.9 13.4 %collective-permute-start.1 = (bf16[4,1,128,256]{3,2,1,0:T(8,128)(2,1)}, bf16[4,1,128,256]{3,2,1,0:T(8,128)(2,1)}, u32[]{:S(2)}, u32[]{:S(2)}) collective-permute-start(bf16[4,1,128,256]{3,2,1,0:T(8,128)(2,1)} %get-tuple-element.18), channel_id=1, source_target_pairs={{2,0},{4,2},{6,4},{8,6},{10,8},{12,10},{14,12},{3,1},{5,3},{7,5},{... | collective-permute-start | bytes 786440 | tf_op jit(solution)/shard_map/ppermute | solution.py:19
  12.1 16.8 %collective-permute-start.3 = (bf16[2,4,128,256]{3,2,1,0:T(8,128)(2,1)}, bf16[2,4,128,256]{3,2,1,0:T(8,128)(2,1)}, u32[]{:S(2)}, u32[]{:S(2)}) collective-permute-start(bf16[2,4,128,256]{3,2,1,0:T(8,128)(2,1)} %slice.134), channel_id=1, source_target_pairs={{1,0},{3,2},{5,4},{7,6},{9,8},{11,10},{13,12},{15,14},{17,16},{19,... | collective-permute-start | bytes 1572872 | tf_op jit(solution)/shard_map/ppermute | solution.py:29
  24.3 1.0 copy-start.9
  34.1 11.1 %collective-permute-start.4 = (bf16[4,1,128,256]{3,0,2,1:T(4,128)(2,1)S(1)}, bf16[4,1,128,256]{3,0,2,1:T(4,128)(2,1)S(1)}, u32[]{:S(2)}, u32[]{:S(2)}) collective-permute-start(bf16[4,1,128,256]{3,0,2,1:T(4,128)(2,1)S(1)} %get-tuple-element.9), channel_id=1, source_target_pairs={{0,2},{2,4},{4,6},{6,8},{8,10},{10,12},{12,14},{1,3},{3,5},{5,7},{... | collective-permute-start | bytes 786440 | tf_op jit(solution)/shard_map/ppermute | solution.py:17
  36.1 14.7 %collective-permute-start.5 = (bf16[4,1,128,256]{3,0,2,1:T(4,128)(2,1)S(1)}, bf16[4,1,128,256]{3,0,2,1:T(4,128)(2,1)S(1)}, u32[]{:S(2)}, u32[]{:S(2)}) collective-permute-start(bf16[4,1,128,256]{3,0,2,1:T(4,128)(2,1)S(1)} %get-tuple-element.10), channel_id=1, source_target_pairs={{2,0},{4,2},{6,4},{8,6},{10,8},{12,10},{14,12},{3,1},{5,3},{7,5},{... | collective-permute-start | bytes 786440 | tf_op jit(solution)/shard_map/ppermute | solution.py:19
  41.4 10.7 %copy-start.2 = (bf16[4,4,128,256]{3,1,2,0:T(4,128)(2,1)}, bf16[4,4,128,256]{3,1,2,0:T(4,128)(2,1)S(1)}, u32[]{:S(2)}) copy-start(bf16[4,4,128,256]{3,1,2,0:T(4,128)(2,1)S(1)} %slice_bitcast_fusion) | copy-start | bytes 3145732
  41.8 17.0 %collective-permute-start.2 = (bf16[2,4,128,256]{3,1,2,0:T(4,128)(2,1)S(1)}, bf16[2,4,128,256]{3,1,2,0:T(4,128)(2,1)S(1)}, u32[]{:S(2)}, u32[]{:S(2)}) collective-permute-start(bf16[2,4,128,256]{3,1,2,0:T(4,128)(2,1)S(1)} %slice.168), channel_id=1, source_target_pairs={{0,1},{2,3},{4,5},{6,7},{8,9},{10,11},{12,13},{14,15},{16,17},{18,... | collective-permute-start | bytes 1572872 | tf_op jit(solution)/shard_map/ppermute | solution.py:29
  52.8 1.3 %copy-start.8 = (bf16[3,3,256,256]{3,2,1,0:T(8,128)(2,1)S(1)}, bf16[3,3,256,256]{3,2,1,0:T(8,128)(2,1)}, u32[]{:S(2)}) copy-start(bf16[3,3,256,256]{3,2,1,0:T(8,128)(2,1)} %param.14) | copy-start | bytes 3538948
  58.5 1.0 slice-start
  58.5 1.3 %copy-start.3 = (bf16[4,4,128,256]{3,1,2,0:T(4,128)(2,1)S(1)}, bf16[4,4,128,256]{3,1,2,0:T(4,128)(2,1)}, u32[]{:S(2)}) copy-start(bf16[4,4,128,256]{3,1,2,0:T(4,128)(2,1)} %copy-done.2) | copy-start | bytes 3145732
  61.2 1.0 copy-start.5
  63.1 0.7 copy-start.7
  66.7 3.8 %collective-permute-start.6 = (bf16[2,4,128,256]{3,2,1,0:T(8,128)(2,1)S(1)}, bf16[2,4,128,256]{3,2,1,0:T(8,128)(2,1)S(1)}, u32[]{:S(2)}, u32[]{:S(2)}) collective-permute-start(bf16[2,4,128,256]{3,2,1,0:T(8,128)(2,1)S(1)} %slice.182), channel_id=1, source_target_pairs={{1,0},{3,2},{5,4},{7,6},{9,8},{11,10},{13,12},{15,14},{17,16},{19,... | collective-permute-start | bytes 1572872 | tf_op jit(solution)/shard_map/ppermute | solution.py:29
  74.7 11.2 %collective-permute-start.7 = (bf16[4,1,128,256]{3,0,2,1:T(4,128)(2,1)S(1)}, bf16[4,1,128,256]{3,0,2,1:T(4,128)(2,1)S(1)}, u32[]{:S(2)}, u32[]{:S(2)}) collective-permute-start(bf16[4,1,128,256]{3,0,2,1:T(4,128)(2,1)S(1)} %get-tuple-element.5), channel_id=1, source_target_pairs={{0,2},{2,4},{4,6},{6,8},{8,10},{10,12},{12,14},{1,3},{3,5},{5,7},{... | collective-permute-start | bytes 786440 | tf_op jit(solution)/shard_map/ppermute | solution.py:17
  76.6 14.8 %collective-permute-start.8 = (bf16[4,1,128,256]{3,0,2,1:T(4,128)(2,1)S(1)}, bf16[4,1,128,256]{3,0,2,1:T(4,128)(2,1)S(1)}, u32[]{:S(2)}, u32[]{:S(2)}) collective-permute-start(bf16[4,1,128,256]{3,0,2,1:T(4,128)(2,1)S(1)} %get-tuple-element.6), channel_id=1, source_target_pairs={{2,0},{4,2},{6,4},{8,6},{10,8},{12,10},{14,12},{3,1},{5,3},{7,5},{... | collective-permute-start | bytes 786440 | tf_op jit(solution)/shard_map/ppermute | solution.py:19
  98.8 1.2 %copy-start.1 = (bf16[4,4,128,256]{3,2,1,0:T(8,128)(2,1)S(1)}, bf16[4,4,128,256]{3,2,1,0:T(8,128)(2,1)}, u32[]{:S(2)}) copy-start(bf16[4,4,128,256]{3,2,1,0:T(8,128)(2,1)} %param.8) | copy-start | bytes 3145732
  98.8 1.2 %copy-start.6 = (f32[256]{0:T(256)S(1)}, f32[256]{0:T(256)}, u32[]{:S(2)}) copy-start(f32[256]{0:T(256)} %param.10) | copy-start | bytes 3076
where the time goes:
time: 105 us; the launch traced here: 104 us
  waiting for transfers between devices  26.6 us (25%)
  starting transfers between devices  24.6 us (23%)
  other arithmetic  21.7 us (21%)
  local copies, waits for them, and re-layouts  16.5 us (16%)
  matrix products  14 us (13%)
    ppermute x3, waiting for transfers between devices, padded_2(): lax.ppermute(head, axis, [((i + 1) % count, i) for i in range(ends)])  16.6 us
    ppermute x3, starting transfers between devices, padded_2(): lax.ppermute(head, axis, [((i + 1) % count, i) for i in range(ends)])  13.2 us
    conv_general_dilated x3, matrix products, spatial_valid(): lax.conv_general_dilated(inputs, kernel, (1, 1), ((0, 0), (1, 1)), dimens...  8.73 us
    ppermute x3, waiting for transfers between devices, padded_2(): lax.ppermute(tail, axis, [(i, (i + 1) % count) for i in range(ends)])  7.67 us
    ppermute x3, starting transfers between devices, padded_2(): lax.ppermute(tail, axis, [(i, (i + 1) % count) for i in range(ends)])  7.23 us
    dot_general x9, matrix products, time_taps(): jnp.dot(padded[k:k + frame_count].reshape(-1, channels), kernel[k], prefe...  5.24 us
    ppermute x3, starting transfers between devices, passed_along(): return lax.ppermute(block, axis, route)  4.18 us
    concatenate x3, other arithmetic, padded_2(): jnp.concatenate([lax.ppermute(tail, axis, [(i, (i + 1) % count) for i in...  3.84 us
  transfers between devices with their start and end apart: 9, of which 7 were waited for; matrix products, arithmetic and copies ran while one was open for 17% of the time, Pallas kernels for 0%

commit v1 on v0

v1 whole, which is shorter than its diff:
```python
import functools

import jax
import jax.numpy as jnp
from jax import lax
from jax.experimental import pallas as pl
from jax.experimental.pallas import tpu as pltpu
from jax.sharding import PartitionSpec as P

EPS = 1e-06
F32 = jnp.float32
BF16 = jnp.bfloat16
VMEM = pl.BlockSpec(memory_space=pltpu.VMEM)
SMEM = pl.BlockSpec(memory_space=pltpu.SMEM)


def shape_of(shape, dtype=BF16):
    return jax.ShapeDtypeStruct(shape, dtype)


def call(kernel, out_shape, flops, *args, scalars=0, aliases=None, name=None):
    outs = jax.tree.leaves(out_shape)
    moved = sum(a.size * a.dtype.itemsize for a in args) + sum(o.size * o.dtype.itemsize for o in outs)
    return pl.pallas_call(
        kernel,
        out_shape=out_shape,
        in_specs=[SMEM] * scalars + [VMEM] * (len(args) - scalars),
        out_specs=jax.tree.map(lambda _: VMEM, out_shape),
        input_output_aliases=aliases or {},
        compiler_params=pltpu.CompilerParams(vmem_limit_bytes=48 * 2**20),
        cost_estimate=pl.CostEstimate(flops=flops, bytes_accessed=moved, transcendentals=0),
        name=name,
    )(*args)


def dot_nn(lhs, rhs):
    return lax.dot_general(lhs, rhs, (((1,), (0,)), ((), ())), preferred_element_type=F32)


def dot_nt(lhs, rhs):
    return lax.dot_general(lhs, rhs, (((1,), (1,)), ((), ())), preferred_element_type=F32)


def flat(block):
    return block.reshape(-1, block.shape[-1])


def mean_last(values):
    return jnp.mean(values, axis=-1, keepdims=True)


def logistic(values):
    return 0.5 + 0.5 * jnp.tanh(0.5 * values)


def unit_of(values):
    inv = lax.rsqrt(mean_last(values * values) + EPS)
    return inv, values * inv


def silu_of(values, gain):
    _, unit = unit_of(values)
    normed = unit * gain
    return (normed * logistic(normed)).astype(BF16)


def back_of(upstream, values, gain):
    inv, unit = unit_of(values)
    normed = unit * gain
    sig = logistic(normed)
    scaled = upstream * (sig * (1.0 + normed * (1.0 - sig))) * gain
    return inv * (scaled - unit * mean_last(scaled * unit))


def mixed(sides, before, centre, after, cols):
    rows = before.shape[0]
    at = lax.broadcasted_iota(jnp.int32, (rows, 1), 0) & (cols - 1)
    down = jnp.where(at == 0, 0.0, pltpu.roll(before, 1, 0))
    up = jnp.where(at == cols - 1, 0.0, pltpu.roll(after, rows - 1, 0))
    return centre + down + up


def spatial(rows, kernel_ref, cols):
    lhs = jnp.concatenate(rows, axis=1)
    width = rows[0].shape[1]
    parts = [dot_nn(lhs, kernel_ref[:, dj].reshape(3 * width, -1)) for dj in range(3)]
    return mixed(None, parts[0], parts[1], parts[2], cols)


def spatial_back(rows, kernel_ref, cols):
    lhs = jnp.concatenate(rows, axis=1)
    parts = [
        dot_nt(lhs, jnp.concatenate([kernel_ref[2 - di, 2 - dj] for di in range(3)], axis=1))
        for dj in range(3)
    ]
    return mixed(None, parts[0], parts[1], parts[2], cols)


def time_back(padded, kernel_ref, head):
    weights = jnp.concatenate([kernel_ref[2], kernel_ref[1], kernel_ref[0]], axis=1)
    out = []
    for f in range(len(padded) - 2):
        part = dot_nt(jnp.concatenate(padded[f : f + 3], axis=1), weights)
        if f == 0:
            extra = jnp.concatenate([kernel_ref[0], kernel_ref[0], kernel_ref[1]], axis=1)
            part += head * dot_nt(jnp.concatenate([padded[0], padded[1], padded[0]], axis=1), extra)
        out.append(part.astype(BF16))
    return out


def act_kernel(x_ref, gain_ref, k_ref, a_ref, s_ref, tail_ref):
    frames, nrows, cols, width = x_ref.shape
    gain = gain_ref[...]
    for r in range(nrows):
        values = flat(x_ref[:, r]).astype(F32)
        a_ref[r] = silu_of(values, gain).reshape(frames, cols, width)
    for r in range(1, nrows - 1):
        rows = [flat(a_ref[r + d]) for d in (-1, 0, 1)]
        out = spatial(rows, k_ref, cols).astype(BF16).reshape(frames, cols, width)
        s_ref[r - 1] = out
        tail_ref[r - 1] = out[frames - 2 :]


def act_rim_kernel(up_ref, down_ref, a_ref, gain_ref, k_ref, s_ref, tail_ref):
    nrows, frames, cols, width = a_ref.shape
    gain = gain_ref[...]
    above = silu_of(flat(up_ref[...]).astype(F32), gain)
    below = silu_of(flat(down_ref[...]).astype(F32), gain)
    last = nrows - 1
    for at, rows in enumerate(
        [[above, flat(a_ref[0]), flat(a_ref[1])], [flat(a_ref[last - 1]), flat(a_ref[last]), below]]
    ):
        out = spatial(rows, k_ref, cols).astype(BF16).reshape(frames, cols, width)
        s_ref[at] = out
        tail_ref[at] = out[frames - 2 :]


def grad_time_kernel(flag_ref, g_ref, later_ref, k_ref, d_ref, top_ref, low_ref):
    frames, nrows, cols, width = g_ref.shape
    head = flag_ref[0].astype(F32)
    padded = [flat(g_ref[f]) for f in range(frames)] + [flat(later_ref[f]) for f in range(2)]
    for f, out in enumerate(time_back(padded, k_ref, head)):
        out = out.reshape(nrows, cols, width)
        d_ref[:, f] = out
        top_ref[f] = out[0]
        low_ref[f] = out[nrows - 1]


def hidden_kernel(which, flag_ref, s_ref, early_ref, d_ref, up_ref, down_ref, gain_ref, kt_ref, ks_ref, o_ref, head_ref):
    nrows, frames, cols, width = d_ref.shape
    gain = gain_ref[...]
    at_start = flag_ref[0] != 0

    def row_of(r):
        if r < 0:
            return flat(up_ref[...])
        if r == nrows:
            return flat(down_ref[...])
        return flat(d_ref[r])

    for at, r in enumerate(which):
        first = s_ref[at, 0]
        early = [jnp.where(at_start, first, early_ref[at, f]) for f in range(2)]
        line = early + [s_ref[at, f] for f in range(frames)]
        lhs = jnp.concatenate(
            [jnp.concatenate(line[k : k + frames], axis=0) for k in range(3)], axis=1
        )
        hidden = dot_nn(lhs, kt_ref[...].reshape(3 * width, width))
        grad = spatial_back([row_of(r + d) for d in (-1, 0, 1)], ks_ref, cols)
        out = back_of(grad, hidden, gain).astype(BF16).reshape(frames, cols, width)
        o_ref[at] = out
        head_ref[at] = out[:2]


def back_time_kernel(flag_ref, dh_ref, later_ref, k_ref, d_ref):
    rows, frames, cols, width = dh_ref.shape
    head = flag_ref[0].astype(F32)
    padded = [flat(dh_ref[:, f]) for f in range(frames)] + [flat(later_ref[:, f]) for f in range(2)]
    for f, out in enumerate(time_back(padded, k_ref, head)):
        d_ref[:, f] = out.reshape(rows, cols, width)


def finish(r, rows, x_ref, g_ref, gain, k_ref, o_ref):
    frames, _, cols, width = x_ref.shape
    grad = spatial_back(rows, k_ref, cols)
    out = back_of(grad, flat(x_ref[:, r]).astype(F32), gain)
    o_ref[:, r] = (flat(g_ref[:, r]).astype(F32) + out).astype(BF16).reshape(frames, cols, width)


def out_kernel(x_ref, g_ref, din_ref, drim_ref, gain_ref, k_ref, o_ref):
    nrows = x_ref.shape[1]
    lines = [flat(drim_ref[0])] + [flat(din_ref[r]) for r in range(nrows - 2)] + [flat(drim_ref[1])]
    for r in range(1, nrows - 1):
        finish(r, lines[r - 1 : r + 2], x_ref, g_ref, gain_ref[...], k_ref, o_ref)


def out_rim_kernel(x_ref, g_ref, din_ref, drim_ref, up_ref, down_ref, gain_ref, k_ref, part_ref, o_ref):
    nrows = x_ref.shape[1]
    o_ref[:, 1 : nrows - 1] = part_ref[:, 1 : nrows - 1]
    gain = gain_ref[...]
    finish(0, [flat(up_ref[...]), flat(drim_ref[0]), flat(din_ref[0])], x_ref, g_ref, gain, k_ref, o_ref)
    finish(
        nrows - 1,
        [flat(din_ref[nrows - 3]), flat(drim_ref[1]), flat(down_ref[...])],
        x_ref, g_ref, gain, k_ref, o_ref,
    )


def on_device(
    frames_in,
    grad_out,
    gain_first,
    gain_second,
    spatial_first,
    temporal_first,
    spatial_second,
    temporal_second,
):
    frames, nrows, cols, width = frames_in.shape
    tiles, spans = lax.axis_size("tile"), lax.axis_size("tm")
    flag = (lax.axis_index("tm") == 0).astype(jnp.int32).reshape(1)
    gain_first = gain_first.reshape(1, width)
    gain_second = gain_second.reshape(1, width)

    def to_next(block):
        return lax.ppermute(block, "tile", [(i, i + 1) for i in range(tiles - 1)])

    def to_previous(block):
        return lax.ppermute(block, "tile", [(i + 1, i) for i in range(tiles - 1)])

    def to_later(block):
        return lax.ppermute(block, "tm", [(i, i + 1) for i in range(spans - 1)])

    def to_earlier(block):
        return lax.ppermute(block, "tm", [(i + 1, i) for i in range(spans - 1)])

    inner, rims = list(range(1, nrows - 1)), [0, nrows - 1]
    per_tap = 2 * frames * cols * width * width
    row = (frames, cols, width)

    x_up = to_next(frames_in[:, nrows - 1])
    x_down = to_previous(frames_in[:, 0])
    g_later = to_earlier(grad_out[:2])

    d2, d2_top, d2_low = call(
        grad_time_kernel,
        (shape_of((nrows,) + row), shape_of(row), shape_of(row)),
        4 * nrows * per_tap,
        flag, grad_out, g_later, temporal_second, scalars=1, name="grad_time",
    )
    d2_up = to_next(d2_low)
    d2_down = to_previous(d2_top)

    a1, s_in, s_in_tail = call(
        act_kernel,
        (shape_of((nrows,) + row), shape_of((nrows - 2,) + row), shape_of((nrows - 2, 2, cols, width))),
        9 * (nrows - 2) * per_tap,
        frames_in, gain_first, spatial_first, name="act",
    )
    s_in_early = to_later(s_in_tail)

    def hidden(which, s, early, name):
        return call(
            functools.partial(hidden_kernel, which),
            (shape_of((len(which),) + row), shape_of((len(which), 2, cols, width))),
            12 * len(which) * per_tap,
            flag, s, early, d2, d2_up if which == rims else d2_top, d2_down if which == rims else d2_low,
            gain_second, temporal_first, spatial_second, scalars=1, name=name,
        )

    def back_time(dh, later, name):
        return call(
            back_time_kernel, shape_of(dh.shape), 4 * dh.shape[0] * per_tap,
            flag, dh, later, temporal_first, scalars=1, name=name,
        )

    dh_in, dh_in_head = hidden(inner, s_in, s_in_early, "hidden")
    dh_in_later = to_earlier(dh_in_head)

    s_rim, s_rim_tail = call(
        act_rim_kernel,
        (shape_of((2,) + row), shape_of((2, 2, cols, width))),
        18 * per_tap,
        x_up, x_down, a1, gain_first, spatial_first, name="act_rim",
    )
    s_rim_early = to_later(s_rim_tail)

    d1_in = back_time(dh_in, dh_in_later, "back_time")

    dh_rim, dh_rim_head = hidden(rims, s_rim, s_rim_early, "hidden_rim")
    dh_rim_later = to_earlier(dh_rim_head)
    d1_rim = back_time(dh_rim, dh_rim_later, "back_time_rim")
    d1_up = to_next(d1_rim[1])
    d1_down = to_previous(d1_rim[0])

    part = call(
        out_kernel, shape_of(frames_in.shape), 9 * (nrows - 2) * per_tap,
        frames_in, grad_out, d1_in, d1_rim, gain_first, spatial_first, name="out",
    )
    return call(
        out_rim_kernel, shape_of(frames_in.shape), 18 * per_tap,
        frames_in, grad_out, d1_in, d1_rim, d1_up, d1_down, gain_first, spatial_first, part,
        aliases={8: 0}, name="out_rim",
    )


def solution(mesh):
    return jax.shard_map(
        on_device,
        mesh=mesh,
        in_specs=(
            P(("clip", "tm"), "tile", None, None),
            P(("clip", "tm"), "tile", None, None),
            P(),
            P(),
            P(),
            P(),
            P(),
            P(),
        ),
        out_specs=P(("clip", "tm"), "tile", None, None),
        check_vma=False,
    )
```

time: 105 us -> 70.8 us (0.67)
  other arithmetic: 21.7 us -> 0 us
  Pallas kernels: 0 us -> 16.9 us
  matrix products: 14 us -> 0 us
  local copies, waits for them, and re-layouts: 16.5 us -> 2.54 us
  waiting for transfers between devices: 26.6 us -> 22.8 us
  starting transfers between devices: 24.6 us -> 27.6 us
    pallas_call x0 -> x9, Pallas kernels: none -> 16.9 us  [call(): pl.pallas_call(kernel, out_shape=out_shape, in_specs=[SMEM] * scalars + [...]
    conv_general_dilated x3 -> x0, matrix products: 8.73 us -> none  [spatial_valid(): lax.conv_general_dilated(inputs, kernel, (1, 1), ((0, 0), (1, 1)), dimens...]
    concatenate x6 -> x0, other arithmetic: 7.07 us -> none  [the longest x3 3.84 us: padded_2(): jnp.concatenate([lax.ppermute(tail, axis, [(i, (i + 1) % count) for i in...]
    convert_element_type x3 -> x0, other arithmetic: 5.72 us -> none  [the longest x1 2.38 us: on_device(): return (grad_out.astype(jnp.float32) + grad_input).astype(jnp.bfloat16)]
    dot_general x9 -> x0, matrix products: 5.24 us -> none  [time_taps(): jnp.dot(padded[k:k + frame_count].reshape(-1, channels), kernel[k], prefe...]
    reduce_sum x3 -> x0, other arithmetic: 4.67 us -> none  [the longest x2 2.95 us: norm_back(): jnp.mean(scaled * unit_vals, axis=-1, keepdims=True)]
    ppermute x9 -> x11, waiting for transfers between devices: 26.6 us -> 22.8 us  [the longest x3 16.9 us: to_previous(): return lax.ppermute(block, 'tile', [(i + 1, i) for i in range(tiles - 1)])]
    conv_general_dilated x7 -> x0, local copies, waits for them, and re-layouts: 3.78 us -> none  [spatial_valid(): lax.conv_general_dilated(inputs, kernel, (1, 1), ((0, 0), (1, 1)), dimens...]
  transfers between devices with their start and end apart: 9 -> 11, of which waited for: 7 -> 6; matrix products, arithmetic and copies ran while one was open for 17% -> 0% of each run, Pallas kernels for 0% -> 18%
where the time goes in v1:
time: 70.8 us; the launch traced here: 70.1 us
  starting transfers between devices  27.6 us (39%)
  waiting for transfers between devices  22.8 us (32%)
  Pallas kernels  16.9 us (24%)
  local copies, waits for them, and re-layouts  2.54 us (4%)
    pallas_call x9, Pallas kernels, call(): pl.pallas_call(kernel, out_shape=out_shape, in_specs=[SMEM] * scalars + [...  16.9 us
    ppermute x3, waiting for transfers between devices, to_previous(): return lax.ppermute(block, 'tile', [(i + 1, i) for i in range(tiles - 1)])  16.9 us
    ppermute x3, starting transfers between devices, to_previous(): return lax.ppermute(block, 'tile', [(i + 1, i) for i in range(tiles - 1)])  13.2 us
    ppermute x3, starting transfers between devices, to_next(): return lax.ppermute(block, 'tile', [(i, i + 1) for i in range(tiles - 1)])  7.24 us
    ppermute x3, waiting for transfers between devices, to_next(): return lax.ppermute(block, 'tile', [(i, i + 1) for i in range(tiles - 1)])  5.85 us
    ppermute x3, starting transfers between devices, to_earlier(): return lax.ppermute(block, 'tm', [(i + 1, i) for i in range(spans - 1)])  3.88 us
    ppermute x2, starting transfers between devices, to_later(): return lax.ppermute(block, 'tm', [(i, i + 1) for i in range(spans - 1)])  3.33 us
  transfers between devices with their start and end apart: 11, of which 6 were waited for; matrix products, arithmetic and copies ran while one was open for 0% of the time, Pallas kernels for 18%

profile of v1, /device:TPU:24, one launch (start us, length us, event | category | flops | bytes accessed | tf_op | source)
XLA Modules:
  0.0 70.1 jit_solution(4113848058220690375)
XLA Ops:
  1.2 1.3 %collective-permute-start.1 = (bf16[2,4,128,256]{3,2,1,0:T(8,128)(2,1)S(1)}, bf16[2,4,128,256]{3,2,1,0:T(8,128)(2,1)S(1)}, u32[]{:S(2)}, u32[]{:S(2)}) collective-permute-start(bf16[2,4,128,256]{3,2,1,0:T(8,128)(2,1)S(1)} %slice.15), channel_id=1, source_target_pairs={{1,0},{3,2},{5,4},{7,6},{9,8},{11,10},{13,12},{15,14},{17,16},{19,... | collective-permute-start | bytes 1572872 | tf_op jit(solution)/shard_map/ppermute | solution.py:235
  2.5 3.4 %collective-permute-start.3 = (bf16[4,128,256]{2,1,0:T(8,128)(2,1)S(1)}, bf16[4,128,256]{2,1,0:T(8,128)(2,1)S(1)}, u32[]{:S(2)}, u32[]{:S(2)}) collective-permute-start(bf16[4,128,256]{2,1,0:T(8,128)(2,1)S(1)} %get-tuple-element.30), channel_id=1, source_target_pairs={{0,2},{2,4},{4,6},{6,8},{8,10},{10,12},{12,14},{1,3},{3,5},{5,7},{... | collective-permute-start | bytes 786440 | tf_op jit(solution)/shard_map/ppermute | solution.py:226
  5.9 3.3 %collective-permute-start.4 = (bf16[4,128,256]{2,1,0:T(8,128)(2,1)S(1)}, bf16[4,128,256]{2,1,0:T(8,128)(2,1)S(1)}, u32[]{:S(2)}, u32[]{:S(2)}) collective-permute-start(bf16[4,128,256]{2,1,0:T(8,128)(2,1)S(1)} %get-tuple-element.29), channel_id=1, source_target_pairs={{2,0},{4,2},{6,4},{8,6},{10,8},{12,10},{14,12},{3,1},{5,3},{7,5},{... | collective-permute-start | bytes 786440 | tf_op jit(solution)/shard_map/ppermute | solution.py:229
  9.3 1.3 %copy-done.2 = bf16[3,3,256,256]{3,2,1,0:T(8,128)(2,1)S(1)} copy-done((bf16[3,3,256,256]{3,2,1,0:T(8,128)(2,1)S(1)}, bf16[3,3,256,256]{3,2,1,0:T(8,128)(2,1)}, u32[]{:S(2)}) %copy-start.2) | copy-done | bytes 1179672
  10.6 1.7 %act.1 = (bf16[4,4,128,256]{3,2,1,0:T(8,128)(2,1)S(1)}, bf16[2,4,128,256]{3,2,1,0:T(8,128)(2,1)S(1)}, bf16[2,2,128,256]{3,2,1,0:T(8,128)(2,1)S(1)}) custom-call(bf16[4,4,128,256]{3,2,1,0:T(8,128)(2,1)S(1)} %copy-done, f32[1,256]{1,0:T(1,128)S(1)} %bitcast.15, bf16[3,3,256,256]{3,2,1,0:T(8,128)(2,1)S(1)} %copy-done.2), custom_call_target="tpu_custom_call" | custom-call | flops 1207959552 | bytes 4064256 | tf_op jit(solution)/shard_map/act/pallas_call | solution.py:24
  12.3 2.1 %collective-permute-done.3.up_ref = bf16[4,128,256]{2,1,0:T(8,128)(2,1)S(1)} collective-permute-done((bf16[4,128,256]{2,1,0:T(8,128)(2,1)S(1)}, bf16[4,128,256]{2,1,0:T(8,128)(2,1)S(1)}, u32[]{:S(2)}, u32[]{:S(2)}) %collective-permute-start.3) | collective-permute-done | bytes 262176 | tf_op jit(solution)/shard_map/ppermute | solution.py:226
  14.4 5.7 %collective-permute-done.4.down_ref = bf16[4,128,256]{2,1,0:T(8,128)(2,1)S(1)} collective-permute-done((bf16[4,128,256]{2,1,0:T(8,128)(2,1)S(1)}, bf16[4,128,256]{2,1,0:T(8,128)(2,1)S(1)}, u32[]{:S(2)}, u32[]{:S(2)}) %collective-permute-start.4) | collective-permute-done | bytes 262176 | tf_op jit(solution)/shard_map/ppermute | solution.py:229
  20.1 1.5 %act_rim.1 = (bf16[2,4,128,256]{3,2,1,0:T(8,128)(2,1)S(1)}, bf16[2,2,128,256]{3,2,1,0:T(8,128)(2,1)S(1)}) custom-call(bf16[4,128,256]{2,1,0:T(8,128)(2,1)S(1)} %collective-permute-done.3.up_ref, bf16[4,128,256]{2,1,0:T(8,128)(2,1)S(1)} %collective-permute-done.4.down_ref, bf16[4,4,128,256]{3,2,1,0:T(8,128)(2,1)S(1)} %get-tuple-element.24.a_ref, ...), custom_call_target="tpu_custom_call" | custom-call | flops 1207959552 | bytes 3539968 | tf_op jit(solution)/shard_map/act_rim/pallas_call | solution.py:24
  21.6 2.0 %collective-permute-start.5 = (bf16[2,2,128,256]{3,2,1,0:T(8,128)(2,1)S(1)}, bf16[2,2,128,256]{3,2,1,0:T(8,128)(2,1)S(1)}, u32[]{:S(2)}, u32[]{:S(2)}) collective-permute-start(bf16[2,2,128,256]{3,2,1,0:T(8,128)(2,1)S(1)} %get-tuple-element.26), channel_id=1, source_target_pairs={{0,1},{2,3},{4,5},{6,7},{8,9},{10,11},{12,13},{14,15},{16,17},{18,... | collective-permute-start | bytes 786440 | tf_op jit(solution)/shard_map/ppermute | solution.py:232
  25.0 1.9 %collective-permute-start.6 = (bf16[4,128,256]{2,1,0:T(8,128)(2,1)S(1)}, bf16[4,128,256]{2,1,0:T(8,128)(2,1)S(1)}, u32[]{:S(2)}, u32[]{:S(2)}) collective-permute-start(bf16[4,128,256]{2,1,0:T(8,128)(2,1)S(1)} %get-tuple-element.21.down_ref), channel_id=1, source_target_pairs={{0,2},{2,4},{4,6},{6,8},{8,10},{10,12},{12,14},{1,3},{3,5},{5,7},{... | collective-permute-start | bytes 786440 | tf_op jit(solution)/shard_map/ppermute | solution.py:226
  26.9 4.8 %collective-permute-start.7 = (bf16[4,128,256]{2,1,0:T(8,128)(2,1)S(1)}, bf16[4,128,256]{2,1,0:T(8,128)(2,1)S(1)}, u32[]{:S(2)}, u32[]{:S(2)}) collective-permute-start(bf16[4,128,256]{2,1,0:T(8,128)(2,1)S(1)} %get-tuple-element.20.up_ref), channel_id=1, source_target_pairs={{2,0},{4,2},{6,4},{8,6},{10,8},{12,10},{14,12},{3,1},{5,3},{7,5},{... | collective-permute-start | bytes 786440 | tf_op jit(solution)/shard_map/ppermute | solution.py:229
  31.7 1.3 %collective-permute-start = (bf16[2,2,128,256]{3,2,1,0:T(8,128)(2,1)S(1)}, bf16[2,2,128,256]{3,2,1,0:T(8,128)(2,1)S(1)}, u32[]{:S(2)}, u32[]{:S(2)}) collective-permute-start(bf16[2,2,128,256]{3,2,1,0:T(8,128)(2,1)S(1)} %get-tuple-element.18), channel_id=1, source_target_pairs={{0,1},{2,3},{4,5},{6,7},{8,9},{10,11},{12,13},{14,15},{16,17},{18,... | collective-permute-start | bytes 786440 | tf_op jit(solution)/shard_map/ppermute | solution.py:232
  33.0 2.4 %collective-permute-done.6.up_ref = bf16[4,128,256]{2,1,0:T(8,128)(2,1)S(1)} collective-permute-done((bf16[4,128,256]{2,1,0:T(8,128)(2,1)S(1)}, bf16[4,128,256]{2,1,0:T(8,128)(2,1)S(1)}, u32[]{:S(2)}, u32[]{:S(2)}) %collective-permute-start.6) | collective-permute-done | bytes 262176 | tf_op jit(solution)/shard_map/ppermute | solution.py:226
  35.5 5.5 %collective-permute-done.7.down_ref = bf16[4,128,256]{2,1,0:T(8,128)(2,1)S(1)} collective-permute-done((bf16[4,128,256]{2,1,0:T(8,128)(2,1)S(1)}, bf16[4,128,256]{2,1,0:T(8,128)(2,1)S(1)}, u32[]{:S(2)}, u32[]{:S(2)}) %collective-permute-start.7) | collective-permute-done | bytes 262176 | tf_op jit(solution)/shard_map/ppermute | solution.py:229
  41.0 2.1 %hidden_rim.1 = (bf16[2,4,128,256]{3,2,1,0:T(8,128)(2,1)S(1)}, bf16[2,2,128,256]{3,2,1,0:T(8,128)(2,1)S(1)}) custom-call(s32[1]{0:T(128)} %bitcast.flag_ref, bf16[2,4,128,256]{3,2,1,0:T(8,128)(2,1)S(1)} %get-tuple-element.25.s_ref, bf16[2,2,128,256]{3,2,1,0:T(8,128)(2,1)S(1)} %collective-permute-done.5.early_ref, ...), custom_call_target="tpu_custom_call" | custom-call | flops 1610612736 | bytes 4719620 | tf_op jit(solution)/shard_map/hidden_rim/pallas_call | solution.py:24
  43.0 1.3 %collective-permute-start.8 = (bf16[2,2,128,256]{3,2,1,0:T(8,128)(2,1)S(1)}, bf16[2,2,128,256]{3,2,1,0:T(8,128)(2,1)S(1)}, u32[]{:S(2)}, u32[]{:S(2)}) collective-permute-start(bf16[2,2,128,256]{3,2,1,0:T(8,128)(2,1)S(1)} %get-tuple-element.28), channel_id=1, source_target_pairs={{1,0},{3,2},{5,4},{7,6},{9,8},{11,10},{13,12},{15,14},{17,16},{19,... | collective-permute-start | bytes 786440 | tf_op jit(solution)/shard_map/ppermute | solution.py:235
  44.3 2.0 %hidden.1 = (bf16[2,4,128,256]{3,2,1,0:T(8,128)(2,1)S(1)}, bf16[2,2,128,256]{3,2,1,0:T(8,128)(2,1)S(1)}) custom-call(s32[1]{0:T(128)} %bitcast.flag_ref, bf16[2,4,128,256]{3,2,1,0:T(8,128)(2,1)S(1)} %get-tuple-element.17.s_ref, bf16[2,2,128,256]{3,2,1,0:T(8,128)(2,1)S(1)} %collective-permute-done.early_ref, ...), custom_call_target="tpu_custom_call" | custom-call | flops 1610612736 | bytes 4719620 | tf_op jit(solution)/shard_map/hidden/pallas_call | solution.py:24
  46.4 1.3 %collective-permute-start.2 = (bf16[2,2,128,256]{3,2,1,0:T(8,128)(2,1)S(1)}, bf16[2,2,128,256]{3,2,1,0:T(8,128)(2,1)S(1)}, u32[]{:S(2)}, u32[]{:S(2)}) collective-permute-start(bf16[2,2,128,256]{3,2,1,0:T(8,128)(2,1)S(1)} %get-tuple-element.23), channel_id=1, source_target_pairs={{1,0},{3,2},{5,4},{7,6},{9,8},{11,10},{13,12},{15,14},{17,16},{19,... | collective-permute-start | bytes 786440 | tf_op jit(solution)/shard_map/ppermute | solution.py:235
  48.5 1.9 %collective-permute-start.9 = (bf16[4,128,256]{2,1,0:T(8,128)(2,1)S(1)}, bf16[4,128,256]{2,1,0:T(8,128)(2,1)S(1)}, u32[]{:S(2)}, u32[]{:S(2)}) collective-permute-start(bf16[4,128,256]{2,1,0:T(8,128)(2,1)S(1)} %get-tuple-element.32), channel_id=1, source_target_pairs={{0,2},{2,4},{4,6},{6,8},{8,10},{10,12},{12,14},{1,3},{3,5},{5,7},{... | collective-permute-start | bytes 786440 | tf_op jit(solution)/shard_map/ppermute | solution.py:226
  50.4 5.0 %collective-permute-start.10 = (bf16[4,128,256]{2,1,0:T(8,128)(2,1)S(1)}, bf16[4,128,256]{2,1,0:T(8,128)(2,1)S(1)}, u32[]{:S(2)}, u32[]{:S(2)}) collective-permute-start(bf16[4,128,256]{2,1,0:T(8,128)(2,1)S(1)} %get-tuple-element.31), channel_id=1, source_target_pairs={{2,0},{4,2},{6,4},{8,6},{10,8},{12,10},{14,12},{3,1},{5,3},{7,5},{... | collective-permute-start | bytes 786440 | tf_op jit(solution)/shard_map/ppermute | solution.py:229
  56.1 2.9 %out.1.part_ref = bf16[4,4,128,256]{3,2,1,0:T(8,128)(2,1)} custom-call(bf16[4,4,128,256]{3,2,1,0:T(8,128)(2,1)S(1)} %copy-done, bf16[4,4,128,256]{3,2,1,0:T(8,128)(2,1)S(1)} %copy-done.1, bf16[2,4,128,256]{3,2,1,0:T(8,128)(2,1)S(1)} %back_time.1.din_ref, bf16[2,4,128,256]{3,2,1,0:T(8,128)(2,1)S(1)} %back_time_rim.1.drim_ref, f32[1,256]{1,0:T(1,128)S(1)} %bitcast.17, ...), custom_call_target="tpu_custom_call" | custom-call | flops 1207959552 | bytes 5374976 | tf_op jit(solution)/shard_map/out/pallas_call | solution.py:24
  59.0 1.3 %collective-permute-done.9.up_ref = bf16[4,128,256]{2,1,0:T(8,128)(2,1)S(1)} collective-permute-done((bf16[4,128,256]{2,1,0:T(8,128)(2,1)S(1)}, bf16[4,128,256]{2,1,0:T(8,128)(2,1)S(1)}, u32[]{:S(2)}, u32[]{:S(2)}) %collective-permute-start.9) | collective-permute-done | bytes 262176 | tf_op jit(solution)/shard_map/ppermute | solution.py:226
  60.4 5.7 %collective-permute-done.10.down_ref = bf16[4,128,256]{2,1,0:T(8,128)(2,1)S(1)} collective-permute-done((bf16[4,128,256]{2,1,0:T(8,128)(2,1)S(1)}, bf16[4,128,256]{2,1,0:T(8,128)(2,1)S(1)}, u32[]{:S(2)}, u32[]{:S(2)}) %collective-permute-start.10) | collective-permute-done | bytes 262176 | tf_op jit(solution)/shard_map/ppermute | solution.py:229
  66.0 4.1 %out_rim.1 = bf16[4,4,128,256]{3,2,1,0:T(8,128)(2,1)} custom-call(bf16[4,4,128,256]{3,2,1,0:T(8,128)(2,1)S(1)} %copy-done, bf16[4,4,128,256]{3,2,1,0:T(8,128)(2,1)S(1)} %copy-done.1, bf16[2,4,128,256]{3,2,1,0:T(8,128)(2,1)S(1)} %back_time.1.din_ref, bf16[2,4,128,256]{3,2,1,0:T(8,128)(2,1)S(1)} %back_time_rim.1.drim_ref, ...), custom_call_target="tpu_custom_call", output_to_operand_aliasing={{}: (8, {})} | custom-call | flops 1207959552 | bytes 6947840 | tf_op jit(solution)/shard_map/out_rim/pallas_call | solution.py:24
  (28 shorter events, 3.9 us)
Async XLA Ops:
  0.0 2.5 %copy-start = (bf16[4,4,128,256]{3,2,1,0:T(8,128)(2,1)S(1)}, bf16[4,4,128,256]{3,2,1,0:T(8,128)(2,1)}, u32[]{:S(2)}) copy-start(bf16[4,4,128,256]{3,2,1,0:T(8,128)(2,1)} %x_ref.5) | copy-start | bytes 3145732
  0.0 9.3 %copy-start.4 = (f32[256]{0:T(256)S(1)}, f32[256]{0:T(256)}, u32[]{:S(2)}) copy-start(f32[256]{0:T(256)} %param.10) | copy-start | bytes 3076
  1.2 22.5 %collective-permute-start.1 = (bf16[2,4,128,256]{3,2,1,0:T(8,128)(2,1)S(1)}, bf16[2,4,128,256]{3,2,1,0:T(8,128)(2,1)S(1)}, u32[]{:S(2)}, u32[]{:S(2)}) collective-permute-start(bf16[2,4,128,256]{3,2,1,0:T(8,128)(2,1)S(1)} %slice.15), channel_id=1, source_target_pairs={{1,0},{3,2},{5,4},{7,6},{9,8},{11,10},{13,12},{15,14},{17,16},{19,... | collective-permute-start | bytes 1572872 | tf_op jit(solution)/shard_map/ppermute | solution.py:235
  2.5 11.9 %collective-permute-start.3 = (bf16[4,128,256]{2,1,0:T(8,128)(2,1)S(1)}, bf16[4,128,256]{2,1,0:T(8,128)(2,1)S(1)}, u32[]{:S(2)}, u32[]{:S(2)}) collective-permute-start(bf16[4,128,256]{2,1,0:T(8,128)(2,1)S(1)} %get-tuple-element.30), channel_id=1, source_target_pairs={{0,2},{2,4},{4,6},{6,8},{8,10},{10,12},{12,14},{1,3},{3,5},{5,7},{... | collective-permute-start | bytes 786440 | tf_op jit(solution)/shard_map/ppermute | solution.py:226
  5.9 14.2 %collective-permute-start.4 = (bf16[4,128,256]{2,1,0:T(8,128)(2,1)S(1)}, bf16[4,128,256]{2,1,0:T(8,128)(2,1)S(1)}, u32[]{:S(2)}, u32[]{:S(2)}) collective-permute-start(bf16[4,128,256]{2,1,0:T(8,128)(2,1)S(1)} %get-tuple-element.29), channel_id=1, source_target_pairs={{2,0},{4,2},{6,4},{8,6},{10,8},{12,10},{14,12},{3,1},{5,3},{7,5},{... | collective-permute-start | bytes 786440 | tf_op jit(solution)/shard_map/ppermute | solution.py:229
  9.3 1.3 %copy-start.2 = (bf16[3,3,256,256]{3,2,1,0:T(8,128)(2,1)S(1)}, bf16[3,3,256,256]{3,2,1,0:T(8,128)(2,1)}, u32[]{:S(2)}) copy-start(bf16[3,3,256,256]{3,2,1,0:T(8,128)(2,1)} %k_ref.13) | copy-start | bytes 3538948
  10.6 9.5 %copy-start.3 = (bf16[3,3,256,256]{3,2,1,0:T(8,128)(2,1)S(1)}, bf16[3,3,256,256]{3,2,1,0:T(8,128)(2,1)}, u32[]{:S(2)}) copy-start(bf16[3,3,256,256]{3,2,1,0:T(8,128)(2,1)} %k_ref.13) | copy-start | bytes 3538948
  20.1 3.6 %copy-start.1 = (bf16[4,4,128,256]{3,2,1,0:T(8,128)(2,1)S(1)}, bf16[4,4,128,256]{3,2,1,0:T(8,128)(2,1)}, u32[]{:S(2)}) copy-start(bf16[4,4,128,256]{3,2,1,0:T(8,128)(2,1)} %g_ref.5) | copy-start | bytes 3145732
  20.1 3.6 %copy-start.6 = (bf16[3,256,256]{2,1,0:T(8,128)(2,1)S(1)}, bf16[3,256,256]{2,1,0:T(8,128)(2,1)}, u32[]{:S(2)}) copy-start(bf16[3,256,256]{2,1,0:T(8,128)(2,1)} %k_ref.8) | copy-start | bytes 1179652
  21.6 11.4 %collective-permute-start.5 = (bf16[2,2,128,256]{3,2,1,0:T(8,128)(2,1)S(1)}, bf16[2,2,128,256]{3,2,1,0:T(8,128)(2,1)S(1)}, u32[]{:S(2)}, u32[]{:S(2)}) collective-permute-start(bf16[2,2,128,256]{3,2,1,0:T(8,128)(2,1)S(1)} %get-tuple-element.26), channel_id=1, source_target_pairs={{0,1},{2,3},{4,5},{6,7},{8,9},{10,11},{12,13},{14,15},{16,17},{18,... | collective-permute-start | bytes 786440 | tf_op jit(solution)/shard_map/ppermute | solution.py:232
  23.7 17.3 %copy-start.5 = (bf16[3,3,256,256]{3,2,1,0:T(8,128)(2,1)S(1)}, bf16[3,3,256,256]{3,2,1,0:T(8,128)(2,1)}, u32[]{:S(2)}) copy-start(bf16[3,3,256,256]{3,2,1,0:T(8,128)(2,1)} %ks_ref.3) | copy-start | bytes 3538948
  23.7 17.3 %copy-start.7 = (bf16[3,256,256]{2,1,0:T(8,128)(2,1)S(1)}, bf16[3,256,256]{2,1,0:T(8,128)(2,1)}, u32[]{:S(2)}) copy-start(bf16[3,256,256]{2,1,0:T(8,128)(2,1)} %k_ref.11) | copy-start | bytes 1179652
  23.7 17.3 %copy-start.8 = (f32[256]{0:T(256)S(1)}, f32[256]{0:T(256)}, u32[]{:S(2)}) copy-start(f32[256]{0:T(256)} %param.11) | copy-start | bytes 3076
  25.0 10.5 %collective-permute-start.6 = (bf16[4,128,256]{2,1,0:T(8,128)(2,1)S(1)}, bf16[4,128,256]{2,1,0:T(8,128)(2,1)S(1)}, u32[]{:S(2)}, u32[]{:S(2)}) collective-permute-start(bf16[4,128,256]{2,1,0:T(8,128)(2,1)S(1)} %get-tuple-element.21.down_ref), channel_id=1, source_target_pairs={{0,2},{2,4},{4,6},{6,8},{8,10},{10,12},{12,14},{1,3},{3,5},{5,7},{... | collective-permute-start | bytes 786440 | tf_op jit(solution)/shard_map/ppermute | solution.py:226
  26.9 14.1 %collective-permute-start.7 = (bf16[4,128,256]{2,1,0:T(8,128)(2,1)S(1)}, bf16[4,128,256]{2,1,0:T(8,128)(2,1)S(1)}, u32[]{:S(2)}, u32[]{:S(2)}) collective-permute-start(bf16[4,128,256]{2,1,0:T(8,128)(2,1)S(1)} %get-tuple-element.20.up_ref), channel_id=1, source_target_pairs={{2,0},{4,2},{6,4},{8,6},{10,8},{12,10},{14,12},{3,1},{5,3},{7,5},{... | collective-permute-start | bytes 786440 | tf_op jit(solution)/shard_map/ppermute | solution.py:229
  31.7 12.6 %collective-permute-start = (bf16[2,2,128,256]{3,2,1,0:T(8,128)(2,1)S(1)}, bf16[2,2,128,256]{3,2,1,0:T(8,128)(2,1)S(1)}, u32[]{:S(2)}, u32[]{:S(2)}) collective-permute-start(bf16[2,2,128,256]{3,2,1,0:T(8,128)(2,1)S(1)} %get-tuple-element.18), channel_id=1, source_target_pairs={{0,1},{2,3},{4,5},{6,7},{8,9},{10,11},{12,13},{14,15},{16,17},{18,... | collective-permute-start | bytes 786440 | tf_op jit(solution)/shard_map/ppermute | solution.py:232
  43.0 4.7 %collective-permute-start.8 = (bf16[2,2,128,256]{3,2,1,0:T(8,128)(2,1)S(1)}, bf16[2,2,128,256]{3,2,1,0:T(8,128)(2,1)S(1)}, u32[]{:S(2)}, u32[]{:S(2)}) collective-permute-start(bf16[2,2,128,256]{3,2,1,0:T(8,128)(2,1)S(1)} %get-tuple-element.28), channel_id=1, source_target_pairs={{1,0},{3,2},{5,4},{7,6},{9,8},{11,10},{13,12},{15,14},{17,16},{19,... | collective-permute-start | bytes 786440 | tf_op jit(solution)/shard_map/ppermute | solution.py:235
  46.4 9.0 %collective-permute-start.2 = (bf16[2,2,128,256]{3,2,1,0:T(8,128)(2,1)S(1)}, bf16[2,2,128,256]{3,2,1,0:T(8,128)(2,1)S(1)}, u32[]{:S(2)}, u32[]{:S(2)}) collective-permute-start(bf16[2,2,128,256]{3,2,1,0:T(8,128)(2,1)S(1)} %get-tuple-element.23), channel_id=1, source_target_pairs={{1,0},{3,2},{5,4},{7,6},{9,8},{11,10},{13,12},{15,14},{17,16},{19,... | collective-permute-start | bytes 786440 | tf_op jit(solution)/shard_map/ppermute | solution.py:235
  48.5 11.9 %collective-permute-start.9 = (bf16[4,128,256]{2,1,0:T(8,128)(2,1)S(1)}, bf16[4,128,256]{2,1,0:T(8,128)(2,1)S(1)}, u32[]{:S(2)}, u32[]{:S(2)}) collective-permute-start(bf16[4,128,256]{2,1,0:T(8,128)(2,1)S(1)} %get-tuple-element.32), channel_id=1, source_target_pairs={{0,2},{2,4},{4,6},{6,8},{8,10},{10,12},{12,14},{1,3},{3,5},{5,7},{... | collective-permute-start | bytes 786440 | tf_op jit(solution)/shard_map/ppermute | solution.py:226
  50.4 15.6 %collective-permute-start.10 = (bf16[4,128,256]{2,1,0:T(8,128)(2,1)S(1)}, bf16[4,128,256]{2,1,0:T(8,128)(2,1)S(1)}, u32[]{:S(2)}, u32[]{:S(2)}) collective-permute-start(bf16[4,128,256]{2,1,0:T(8,128)(2,1)S(1)} %get-tuple-element.31), channel_id=1, source_target_pairs={{2,0},{4,2},{6,4},{8,6},{10,8},{12,10},{14,12},{3,1},{5,3},{7,5},{... | collective-permute-start | bytes 786440 | tf_op jit(solution)/shard_map/ppermute | solution.py:229

commit v2 on v1

--- a/solution.py
+++ b/solution.py
@@ -8,6 +8,7 @@
 from jax.sharding import PartitionSpec as P
 
 EPS = 1e-06
+START, END, ODD, TOP, LOW = range(5)
 F32 = jnp.float32
 BF16 = jnp.bfloat16
 VMEM = pl.BlockSpec(memory_space=pltpu.VMEM)
@@ -72,7 +73,7 @@
     return inv * (scaled - unit * mean_last(scaled * unit))
 
 
-def mixed(sides, before, centre, after, cols):
+def mixed(before, centre, after, cols):
     rows = before.shape[0]
     at = lax.broadcasted_iota(jnp.int32, (rows, 1), 0) & (cols - 1)
     down = jnp.where(at == 0, 0.0, pltpu.roll(before, 1, 0))
@@ -84,7 +85,7 @@
     lhs = jnp.concatenate(rows, axis=1)
     width = rows[0].shape[1]
     parts = [dot_nn(lhs, kernel_ref[:, dj].reshape(3 * width, -1)) for dj in range(3)]
-    return mixed(None, parts[0], parts[1], parts[2], cols)
+    return mixed(parts[0], parts[1], parts[2], cols)
 
 
 def spatial_back(rows, kernel_ref, cols):
@@ -93,7 +94,7 @@
         dot_nt(lhs, jnp.concatenate([kernel_ref[2 - di, 2 - dj] for di in range(3)], axis=1))
         for dj in range(3)
     ]
-    return mixed(None, parts[0], parts[1], parts[2], cols)
+    return mixed(parts[0], parts[1], parts[2], cols)
 
 
 def time_back(padded, kernel_ref, head):
@@ -121,11 +122,19 @@
         tail_ref[r - 1] = out[frames - 2 :]
 
 
-def act_rim_kernel(up_ref, down_ref, a_ref, gain_ref, k_ref, s_ref, tail_ref):
+def neighbours(flag_ref, own, other):
+    odd, top, low = flag_ref[ODD] != 0, flag_ref[TOP] != 0, flag_ref[LOW] != 0
+    above = jnp.where(top, jnp.zeros_like(own), jnp.where(odd, own, other))
+    below = jnp.where(low, jnp.zeros_like(own), jnp.where(odd, other, own))
+    return above, below
+
+
+def act_rim_kernel(flag_ref, own_ref, other_ref, a_ref, gain_ref, k_ref, s_ref, tail_ref):
     nrows, frames, cols, width = a_ref.shape
     gain = gain_ref[...]
-    above = silu_of(flat(up_ref[...]).astype(F32), gain)
-    below = silu_of(flat(down_ref[...]).astype(F32), gain)
+    above, below = neighbours(flag_ref, flat(own_ref[...]), flat(other_ref[...]))
+    above = silu_of(above.astype(F32), gain)
+    below = silu_of(below.astype(F32), gain)
     last = nrows - 1
     for at, rows in enumerate(
         [[above, flat(a_ref[0]), flat(a_ref[1])], [flat(a_ref[last - 1]), flat(a_ref[last]), below]]
@@ -135,28 +144,31 @@
         tail_ref[at] = out[frames - 2 :]
 
 
-def grad_time_kernel(flag_ref, g_ref, later_ref, k_ref, d_ref, top_ref, low_ref):
+def later_of(flag_ref, block):
+    return jnp.where(flag_ref[END] != 0, jnp.zeros_like(block), block)
+
+
+def grad_time_kernel(flag_ref, g_ref, later_ref, k_ref, d_ref, own_ref, other_ref):
     frames, nrows, cols, width = g_ref.shape
-    head = flag_ref[0].astype(F32)
-    padded = [flat(g_ref[f]) for f in range(frames)] + [flat(later_ref[f]) for f in range(2)]
+    head = flag_ref[START].astype(F32)
+    odd = flag_ref[ODD] != 0
+    padded = [flat(g_ref[f]) for f in range(frames)]
+    padded += [later_of(flag_ref, flat(later_ref[f])) for f in range(2)]
     for f, out in enumerate(time_back(padded, k_ref, head)):
         out = out.reshape(nrows, cols, width)
         d_ref[:, f] = out
-        top_ref[f] = out[0]
-        low_ref[f] = out[nrows - 1]
-
-
-def hidden_kernel(which, flag_ref, s_ref, early_ref, d_ref, up_ref, down_ref, gain_ref, kt_ref, ks_ref, o_ref, head_ref):
+        own_ref[f] = jnp.where(odd, out[0], out[nrows - 1])
+        other_ref[f] = jnp.where(odd, out[nrows - 1], out[0])
+
+
+def hidden_kernel(which, flag_ref, s_ref, early_ref, d_ref, *refs):
+    *rim_refs, gain_ref, kt_ref, ks_ref, o_ref, head_ref = refs
     nrows, frames, cols, width = d_ref.shape
     gain = gain_ref[...]
-    at_start = flag_ref[0] != 0
-
-    def row_of(r):
-        if r < 0:
-            return flat(up_ref[...])
-        if r == nrows:
-            return flat(down_ref[...])
-        return flat(d_ref[r])
+    at_start = flag_ref[START] != 0
+    rows = {r: flat(d_ref[r]) for r in range(nrows)}
+    if rim_refs:
+        rows[-1], rows[nrows] = neighbours(flag_ref, *[flat(ref[...]) for ref in rim_refs])
 
     for at, r in enumerate(which):
         first = s_ref[at, 0]
@@ -166,18 +178,25 @@
             [jnp.concatenate(line[k : k + frames], axis=0) for k in range(3)], axis=1
         )
         hidden = dot_nn(lhs, kt_ref[...].reshape(3 * width, width))
-        grad = spatial_back([row_of(r + d) for d in (-1, 0, 1)], ks_ref, cols)
+        grad = spatial_back([rows[r + d] for d in (-1, 0, 1)], ks_ref, cols)
         out = back_of(grad, hidden, gain).astype(BF16).reshape(frames, cols, width)
         o_ref[at] = out
         head_ref[at] = out[:2]
 
 
-def back_time_kernel(flag_ref, dh_ref, later_ref, k_ref, d_ref):
+def back_time_kernel(flag_ref, dh_ref, later_ref, k_ref, d_ref, *send_refs):
     rows, frames, cols, width = dh_ref.shape
-    head = flag_ref[0].astype(F32)
-    padded = [flat(dh_ref[:, f]) for f in range(frames)] + [flat(later_ref[:, f]) for f in range(2)]
+    head = flag_ref[START].astype(F32)
+    odd = flag_ref[ODD] != 0
+    padded = [flat(dh_ref[:, f]) for f in range(frames)]
+    padded += [later_of(flag_ref, flat(later_ref[:, f])) for f in range(2)]
     for f, out in enumerate(time_back(padded, k_ref, head)):
-        d_ref[:, f] = out.reshape(rows, cols, width)
+        out = out.reshape(rows, cols, width)
+        d_ref[:, f] = out
+        if send_refs:
+            own_ref, other_ref = send_refs
+            own_ref[f] = jnp.where(odd, out[0], out[1])
+            other_ref[f] = jnp.where(odd, out[1], out[0])
 
 
 def finish(r, rows, x_ref, g_ref, gain, k_ref, o_ref):
@@ -194,16 +213,21 @@
         finish(r, lines[r - 1 : r + 2], x_ref, g_ref, gain_ref[...], k_ref, o_ref)
 
 
-def out_rim_kernel(x_ref, g_ref, din_ref, drim_ref, up_ref, down_ref, gain_ref, k_ref, part_ref, o_ref):
+def out_rim_kernel(flag_ref, x_ref, g_ref, din_ref, drim_ref, own_ref, other_ref, gain_ref, k_ref, part_ref, o_ref):
     nrows = x_ref.shape[1]
     o_ref[:, 1 : nrows - 1] = part_ref[:, 1 : nrows - 1]
     gain = gain_ref[...]
-    finish(0, [flat(up_ref[...]), flat(drim_ref[0]), flat(din_ref[0])], x_ref, g_ref, gain, k_ref, o_ref)
+    above, below = neighbours(flag_ref, flat(own_ref[...]), flat(other_ref[...]))
+    finish(0, [above, flat(drim_ref[0]), flat(din_ref[0])], x_ref, g_ref, gain, k_ref, o_ref)
     finish(
         nrows - 1,
-        [flat(din_ref[nrows - 3]), flat(drim_ref[1]), flat(down_ref[...])],
+        [flat(din_ref[nrows - 3]), flat(drim_ref[1]), below],
         x_ref, g_ref, gain, k_ref, o_ref,
     )
+
+
+def after(value, *earlier):
+    return lax.optimization_barrier((value,) + earlier)[0]
 
 
 def on_device(
@@ -218,80 +242,79 @@
 ):
     frames, nrows, cols, width = frames_in.shape
     tiles, spans = lax.axis_size("tile"), lax.axis_size("tm")
-    flag = (lax.axis_index("tm") == 0).astype(jnp.int32).reshape(1)
+    tile, span = lax.axis_index("tile"), lax.axis_index("tm")
+    odd = tile % 2
+    flag = jnp.stack([span == 0, span == spans - 1, odd == 1, tile == 0, tile == tiles - 1]).astype(jnp.int32)
     gain_first = gain_first.reshape(1, width)
     gain_second = gain_second.reshape(1, width)
 
-    def to_next(block):
-        return lax.ppermute(block, "tile", [(i, i + 1) for i in range(tiles - 1)])
-
-    def to_previous(block):
-        return lax.ppermute(block, "tile", [(i + 1, i) for i in range(tiles - 1)])
+    def swap(block, first):
+        pairs = [(i, i + 1) for i in range(first, tiles - 1, 2)]
+        route = dict(pairs + [(b, a) for a, b in pairs])
+        return lax.ppermute(block, "tile", [(i, route.get(i, i)) for i in range(tiles)])
+
+    def exchange(own, other):
+        return swap(own, 0), swap(other, 1)
 
     def to_later(block):
-        return lax.ppermute(block, "tm", [(i, i + 1) for i in range(spans - 1)])
+        return lax.ppermute(block, "tm", [(i, (i + 1) % spans) for i in range(spans)])
 
     def to_earlier(block):
-        return lax.ppermute(block, "tm", [(i + 1, i) for i in range(spans - 1)])
+        return lax.ppermute(block, "tm", [((i + 1) % spans, i) for i in range(spans)])
 
     inner, rims = list(range(1, nrows - 1)), [0, nrows - 1]
     per_tap = 2 * frames * cols * width * width
     row = (frames, cols, width)
 
-    x_up = to_next(frames_in[:, nrows - 1])
-    x_down = to_previous(frames_in[:, 0])
     g_later = to_earlier(grad_out[:2])
-
-    d2, d2_top, d2_low = call(
+    x_rims = exchange(
+        *[lax.dynamic_index_in_dim(frames_in, at, 1, keepdims=False) for at in ((1 - odd) * (nrows - 1), odd * (nrows - 1))]
+    )
+
+    d2, *d2_send = call(
         grad_time_kernel,
         (shape_of((nrows,) + row), shape_of(row), shape_of(row)),
         4 * nrows * per_tap,
         flag, grad_out, g_later, temporal_second, scalars=1, name="grad_time",
     )
-    d2_up = to_next(d2_low)
-    d2_down = to_previous(d2_top)
+    d2_rims = exchange(*d2_send)
 
     a1, s_in, s_in_tail = call(
         act_kernel,
         (shape_of((nrows,) + row), shape_of((nrows - 2,) + row), shape_of((nrows - 2, 2, cols, width))),
         9 * (nrows - 2) * per_tap,
-        frames_in, gain_first, spatial_first, name="act",
+        frames_in, after(gain_first, d2), spatial_first, name="act",
     )
     s_in_early = to_later(s_in_tail)
 
-    def hidden(which, s, early, name):
+    def hidden(which, s, early, extra, gain, name):
         return call(
             functools.partial(hidden_kernel, which),
             (shape_of((len(which),) + row), shape_of((len(which), 2, cols, width))),
             12 * len(which) * per_tap,
-            flag, s, early, d2, d2_up if which == rims else d2_top, d2_down if which == rims else d2_low,
-            gain_second, temporal_first, spatial_second, scalars=1, name=name,
+            flag, s, early, d2, *extra, gain, temporal_first, spatial_second, scalars=1, name=name,
         )
 
-    def back_time(dh, later, name):
+    def back_time(dh, later, name, sends):
         return call(
-            back_time_kernel, shape_of(dh.shape), 4 * dh.shape[0] * per_tap,
+            back_time_kernel, (shape_of(dh.shape),) + (shape_of(row),) * sends, 4 * dh.shape[0] * per_tap,
             flag, dh, later, temporal_first, scalars=1, name=name,
         )
-
-    dh_in, dh_in_head = hidden(inner, s_in, s_in_early, "hidden")
-    dh_in_later = to_earlier(dh_in_head)
 
     s_rim, s_rim_tail = call(
         act_rim_kernel,
         (shape_of((2,) + row), shape_of((2, 2, cols, width))),
         18 * per_tap,
-        x_up, x_down, a1, gain_first, spatial_first, name="act_rim",
+        flag, *x_rims, a1, gain_first, spatial_first, scalars=1, name="act_rim",
     )
     s_rim_early = to_later(s_rim_tail)
 
-    d1_in = back_time(dh_in, dh_in_later, "back_time")
-
-    dh_rim, dh_rim_head = hidden(rims, s_rim, s_rim_early, "hidden_rim")
-    dh_rim_later = to_earlier(dh_rim_head)
-    d1_rim = back_time(dh_rim, dh_rim_later, "back_time_rim")
-    d1_up = to_next(d1_rim[1])
-    d1_down = to_previous(d1_rim[0])
+    dh_in, dh_in_head = hidden(inner, s_in, s_in_early, (), after(gain_second, s_rim), "hidden")
+    (d1_in,) = back_time(dh_in, to_earlier(dh_in_head), "back_time", 0)
+
+    dh_rim, dh_rim_head = hidden(rims, s_rim, s_rim_early, d2_rims, after(gain_second, dh_in), "hidden_rim")
+    d1_rim, *d1_send = back_time(dh_rim, to_earlier(dh_rim_head), "back_time_rim", 2)
+    d1_rims = exchange(*d1_send)
 
     part = call(
         out_kernel, shape_of(frames_in.shape), 9 * (nrows - 2) * per_tap,
@@ -299,8 +322,8 @@
     )
     return call(
         out_rim_kernel, shape_of(frames_in.shape), 18 * per_tap,
-        frames_in, grad_out, d1_in, d1_rim, d1_up, d1_down, gain_first, spatial_first, part,
-        aliases={8: 0}, name="out_rim",
+        flag, frames_in, grad_out, d1_in, d1_rim, *d1_rims, gain_first, spatial_first, part,
+        scalars=1, aliases={9: 0}, name="out_rim",
     )
 
 

time: 70.8 us -> 55.7 us (0.79)
  starting transfers between devices: 27.6 us -> 13.6 us
  waiting for transfers between devices: 22.8 us -> 16.8 us
  Pallas kernels: 16.9 us -> 20.4 us
  local copies, waits for them, and re-layouts: 2.54 us -> 3.97 us
    ppermute x11, starting transfers between devices: 27.6 us -> 13.6 us  [the longest x6 12.7 us: swap(): lax.ppermute(block, 'tile', [(i, route.get(i, i)) for i in range(tiles)])]
    ppermute x11, waiting for transfers between devices: 22.8 us -> 16.8 us  [the longest x6 15.7 us: swap(): lax.ppermute(block, 'tile', [(i, route.get(i, i)) for i in range(tiles)])]
    pallas_call x9, Pallas kernels: 16.9 us -> 20.4 us  [call(): pl.pallas_call(kernel, out_shape=out_shape, in_specs=[SMEM] * scalars + [...]
    slice x1, local copies, waits for them, and re-layouts: 1.16 us -> 2.02 us  [on_device(): g_later = to_earlier(grad_out[:2])]
  transfers between devices with their start and end apart: 11 -> 11, of which waited for: 6 -> 4; matrix products, arithmetic and copies ran while one was open for 0% -> 2% of each run, Pallas kernels for 18% -> 25%
where the time goes in v2:
time: 55.7 us; the launch traced here: 55 us
  Pallas kernels  20.4 us (37%)
  waiting for transfers between devices  16.8 us (30%)
  starting transfers between devices  13.6 us (24%)
  local copies, waits for them, and re-layouts  3.97 us (7%)
    pallas_call x9, Pallas kernels, call(): pl.pallas_call(kernel, out_shape=out_shape, in_specs=[SMEM] * scalars + [...  20.4 us
    ppermute x6, waiting for transfers between devices, swap(): lax.ppermute(block, 'tile', [(i, route.get(i, i)) for i in range(tiles)])  15.7 us
    ppermute x6, starting transfers between devices, swap(): lax.ppermute(block, 'tile', [(i, route.get(i, i)) for i in range(tiles)])  12.7 us
    slice x1, local copies, waits for them, and re-layouts, on_device(): g_later = to_earlier(grad_out[:2])  2.02 us
  transfers between devices with their start and end apart: 11, of which 4 were waited for; matrix products, arithmetic and copies ran while one was open for 2% of the time, Pallas kernels for 25%

profile of v2, /device:TPU:24, one launch (start us, length us, event | category | flops | bytes accessed | tf_op | source)
XLA Modules:
  0.0 55.0 jit_solution(9069930008357086347)
XLA Ops:
  0.0 2.0 %slice.3 = bf16[2,4,128,256]{3,2,1,0:T(8,128)(2,1)} slice(bf16[4,4,128,256]{3,2,1,0:T(8,128)(2,1)} %g_ref.5), slice={[0:2], [0:4], [0:128], [0:256]} | slice | bytes 1048576 | tf_op jit(solution)/shard_map/slice | solution.py:269
  2.0 0.7 %dynamic-slice_bitcast_fusion = (bf16[4,128,256]{2,1,0:T(8,128)(2,1)}, bf16[4,128,256]{2,1,0:T(8,128)(2,1)S(1)}) fusion(bf16[4,4,128,256]{3,2,1,0:T(8,128)(2,1)S(1)} %copy-done, s32[]{:T(128)S(6)} %select_n.16, s32[]{:T(128)S(6)} %select_n.15), kind=kLoop, calls=%fused_computation | loop fusion | bytes 1048584 | tf_op jit(solution)/shard_map/jit(dynamic_index_in_dim)/squeeze | solution.py:271
  2.8 3.3 %collective-permute-start.3 = (bf16[4,128,256]{2,1,0:T(8,128)(2,1)}, bf16[4,128,256]{2,1,0:T(8,128)(2,1)S(1)}, u32[]{:S(2)}, u32[]{:S(2)}) collective-permute-start(bf16[4,128,256]{2,1,0:T(8,128)(2,1)} %get-tuple-element.41), channel_id=1, source_target_pairs={{0,0},{2,4},{4,2},{6,8},{8,6},{10,12},{12,10},{14,14},{1,1},{3,5},... | collective-permute-start | bytes 786440 | tf_op jit(solution)/shard_map/ppermute | solution.py:254
  6.1 0.1 stack.23
  6.3 1.1 %copy-done.5 = bf16[3,256,256]{2,1,0:T(8,128)(2,1)S(1)} copy-done((bf16[3,256,256]{2,1,0:T(8,128)(2,1)S(1)}, bf16[3,256,256]{2,1,0:T(8,128)(2,1)}, u32[]{:S(2)}) %copy-start.5) | copy-done | bytes 393240
  7.4 1.8 %grad_time.1 = (bf16[4,4,128,256]{3,2,1,0:T(8,128)(2,1)S(1)}, bf16[4,128,256]{2,1,0:T(8,128)(2,1)S(1)}, bf16[4,128,256]{2,1,0:T(8,128)(2,1)S(1)}) custom-call(s32[5]{0:T(128)S(1)} %convert_element_type.3.flag_ref, bf16[4,4,128,256]{3,2,1,0:T(8,128)(2,1)S(1)} %copy-done.1, bf16[2,4,128,256]{3,2,1,0:T(8,128)(2,1)S(1)} %collective-permute-done.later_ref, ...), custom_call_target="tpu_custom_call" | custom-call | flops 1073741824 | bytes 3538964 | tf_op jit(solution)/shard_map/grad_time/pallas_call | solution.py:25
  9.2 1.8 %act.1 = (bf16[4,4,128,256]{3,2,1,0:T(8,128)(2,1)S(1)}, bf16[2,4,128,256]{3,2,1,0:T(8,128)(2,1)S(1)}, bf16[2,2,128,256]{3,2,1,0:T(8,128)(2,1)S(1)}) custom-call(bf16[4,4,128,256]{3,2,1,0:T(8,128)(2,1)S(1)} %copy-done, f32[1,256]{1,0:T(1,128)S(1)} %bitcast.11, bf16[3,3,256,256]{3,2,1,0:T(8,128)(2,1)S(1)} %copy-done.2), custom_call_target="tpu_custom_call" | custom-call | flops 1207959552 | bytes 4064256 | tf_op jit(solution)/shard_map/act/pallas_call | solution.py:25
  11.0 0.3 collective-permute-start.1
  11.2 1.9 %collective-permute-start.6 = (bf16[4,128,256]{2,1,0:T(8,128)(2,1)S(1)}, bf16[4,128,256]{2,1,0:T(8,128)(2,1)S(1)}, u32[]{:S(2)}, u32[]{:S(2)}) collective-permute-start(bf16[4,128,256]{2,1,0:T(8,128)(2,1)S(1)} %get-tuple-element.33), channel_id=1, source_target_pairs={{0,2},{2,0},{4,6},{6,4},{8,10},{10,8},{12,14},{14,12},{1,3},{3,1},... | collective-permute-start | bytes 786440 | tf_op jit(solution)/shard_map/ppermute | solution.py:254
  13.1 3.4 %collective-permute-start.7 = (bf16[4,128,256]{2,1,0:T(8,128)(2,1)S(1)}, bf16[4,128,256]{2,1,0:T(8,128)(2,1)S(1)}, u32[]{:S(2)}, u32[]{:S(2)}) collective-permute-start(bf16[4,128,256]{2,1,0:T(8,128)(2,1)S(1)} %get-tuple-element.34), channel_id=1, source_target_pairs={{0,0},{2,4},{4,2},{6,8},{8,6},{10,12},{12,10},{14,14},{1,1},{3,5},... | collective-permute-start | bytes 786440 | tf_op jit(solution)/shard_map/ppermute | solution.py:254
  16.6 9.2 %collective-permute-done.2.own_ref = bf16[4,128,256]{2,1,0:T(8,128)(2,1)S(1)} collective-permute-done((bf16[4,128,256]{2,1,0:T(8,128)(2,1)S(1)}, bf16[4,128,256]{2,1,0:T(8,128)(2,1)S(1)}, u32[]{:S(2)}, u32[]{:S(2)}) %collective-permute-start.2) | collective-permute-done | bytes 262176 | tf_op jit(solution)/shard_map/ppermute | solution.py:254
  25.8 2.1 %act_rim.1 = (bf16[2,4,128,256]{3,2,1,0:T(8,128)(2,1)S(1)}, bf16[2,2,128,256]{3,2,1,0:T(8,128)(2,1)S(1)}) custom-call(s32[5]{0:T(128)S(1)} %convert_element_type.3.flag_ref, bf16[4,128,256]{2,1,0:T(8,128)(2,1)S(1)} %collective-permute-done.2.own_ref, bf16[4,128,256]{2,1,0:T(8,128)(2,1)S(1)} %collective-permute-done.3.other_ref, ...), custom_call_target="tpu_custom_call" | custom-call | flops 1207959552 | bytes 3539988 | tf_op jit(solution)/shard_map/act_rim/pallas_call | solution.py:25
  28.0 2.6 %hidden.1 = (bf16[2,4,128,256]{3,2,1,0:T(8,128)(2,1)S(1)}, bf16[2,2,128,256]{3,2,1,0:T(8,128)(2,1)S(1)}) custom-call(s32[5]{0:T(128)S(1)} %convert_element_type.3.flag_ref, bf16[2,4,128,256]{3,2,1,0:T(8,128)(2,1)S(1)} %get-tuple-element.25.s_ref, bf16[2,2,128,256]{3,2,1,0:T(8,128)(2,1)S(1)} %collective-permute-done.1.early_ref, ...), custom_call_target="tpu_custom_call" | custom-call | flops 1610612736 | bytes 4195348 | tf_op jit(solution)/shard_map/hidden/pallas_call | solution.py:25
  30.6 0.7 %collective-permute-done.6.refs_0_ = bf16[4,128,256]{2,1,0:T(8,128)(2,1)S(1)} collective-permute-done((bf16[4,128,256]{2,1,0:T(8,128)(2,1)S(1)}, bf16[4,128,256]{2,1,0:T(8,128)(2,1)S(1)}, u32[]{:S(2)}, u32[]{:S(2)}) %collective-permute-start.6) | collective-permute-done | bytes 262176 | tf_op jit(solution)/shard_map/ppermute | solution.py:254
  31.3 2.7 %hidden_rim.1 = (bf16[2,4,128,256]{3,2,1,0:T(8,128)(2,1)S(1)}, bf16[2,2,128,256]{3,2,1,0:T(8,128)(2,1)S(1)}) custom-call(s32[5]{0:T(128)S(1)} %convert_element_type.3.flag_ref, bf16[2,4,128,256]{3,2,1,0:T(8,128)(2,1)S(1)} %get-tuple-element.28.s_ref, bf16[2,2,128,256]{3,2,1,0:T(8,128)(2,1)S(1)} %collective-permute-done.5.early_ref, ...), custom_call_target="tpu_custom_call" | custom-call | flops 1610612736 | bytes 4719636 | tf_op jit(solution)/shard_map/hidden_rim/pallas_call | solution.py:25
  34.0 0.1 collective-permute-start.8
  34.1 0.5 collective-permute-start.4
  34.6 1.0 %collective-permute-done.8.later_ref = bf16[2,2,128,256]{3,2,1,0:T(8,128)(2,1)S(1)} collective-permute-done((bf16[2,2,128,256]{3,2,1,0:T(8,128)(2,1)S(1)}, bf16[2,2,128,256]{3,2,1,0:T(8,128)(2,1)S(1)}, u32[]{:S(2)}, u32[]{:S(2)}) %collective-permute-start.8) | collective-permute-done | bytes 262176 | tf_op jit(solution)/shard_map/ppermute | solution.py:263
  35.6 1.3 %back_time_rim.1 = (bf16[2,4,128,256]{3,2,1,0:T(8,128)(2,1)S(1)}, bf16[4,128,256]{2,1,0:T(8,128)(2,1)S(1)}, bf16[4,128,256]{2,1,0:T(8,128)(2,1)S(1)}) custom-call(s32[5]{0:T(128)S(1)} %convert_element_type.3.flag_ref, bf16[2,4,128,256]{3,2,1,0:T(8,128)(2,1)S(1)} %get-tuple-element.36.dh_ref, bf16[2,2,128,256]{3,2,1,0:T(8,128)(2,1)S(1)} %collective-permute-done.8.later_ref, ...), custom_call_target="tpu_custom_call" | custom-call | flops 536870912 | bytes 2228244 | tf_op jit(solution)/shard_map/back_time_rim/pallas_call | solution.py:25
  36.9 4.0 %collective-permute-start.10 = (bf16[4,128,256]{2,1,0:T(8,128)(2,1)S(1)}, bf16[4,128,256]{2,1,0:T(8,128)(2,1)S(1)}, u32[]{:S(2)}, u32[]{:S(2)}) collective-permute-start(bf16[4,128,256]{2,1,0:T(8,128)(2,1)S(1)} %get-tuple-element.40), channel_id=1, source_target_pairs={{0,0},{2,4},{4,2},{6,8},{8,6},{10,12},{12,10},{14,14},{1,1},{3,5},... | collective-permute-start | bytes 786440 | tf_op jit(solution)/shard_map/ppermute | solution.py:254
  40.9 1.3 %back_time.1.din_ref = bf16[2,4,128,256]{3,2,1,0:T(8,128)(2,1)S(1)} custom-call(s32[5]{0:T(128)S(1)} %convert_element_type.3.flag_ref, bf16[2,4,128,256]{3,2,1,0:T(8,128)(2,1)S(1)} %get-tuple-element.30.dh_ref, bf16[2,2,128,256]{3,2,1,0:T(8,128)(2,1)S(1)} %collective-permute-done.4.later_ref, bf16[3,256,256]{2,1,0:T(8,128)(2,1)S(1)} %copy-done.6), custom_call_target="tpu_custom_call" | custom-call | flops 536870912 | bytes 1703956 | tf_op jit(solution)/shard_map/back_time/pallas_call | solution.py:25
  42.2 2.9 %out.1.part_ref = bf16[4,4,128,256]{3,2,1,0:T(8,128)(2,1)} custom-call(bf16[4,4,128,256]{3,2,1,0:T(8,128)(2,1)S(1)} %copy-done, bf16[4,4,128,256]{3,2,1,0:T(8,128)(2,1)S(1)} %copy-done.1, bf16[2,4,128,256]{3,2,1,0:T(8,128)(2,1)S(1)} %back_time.1.din_ref, bf16[2,4,128,256]{3,2,1,0:T(8,128)(2,1)S(1)} %get-tuple-element.38.drim_ref, f32[1,256]{1,0:T(1,128)S(1)} %bitcast.13, ...), custom_call_target="tpu_custom_call" | custom-call | flops 1207959552 | bytes 5374976 | tf_op jit(solution)/shard_map/out/pallas_call | solution.py:25
  45.1 5.8 %collective-permute-done.9.own_ref = bf16[4,128,256]{2,1,0:T(8,128)(2,1)S(1)} collective-permute-done((bf16[4,128,256]{2,1,0:T(8,128)(2,1)S(1)}, bf16[4,128,256]{2,1,0:T(8,128)(2,1)S(1)}, u32[]{:S(2)}, u32[]{:S(2)}) %collective-permute-start.9) | collective-permute-done | bytes 262176 | tf_op jit(solution)/shard_map/ppermute | solution.py:254
  50.9 4.1 %out_rim.1 = bf16[4,4,128,256]{3,2,1,0:T(8,128)(2,1)} custom-call(s32[5]{0:T(128)S(1)} %convert_element_type.3.flag_ref, bf16[4,4,128,256]{3,2,1,0:T(8,128)(2,1)S(1)} %copy-done, bf16[4,4,128,256]{3,2,1,0:T(8,128)(2,1)S(1)} %copy-done.1, bf16[2,4,128,256]{3,2,1,0:T(8,128)(2,1)S(1)} %back_time.1.din_ref, ...), custom_call_target="tpu_custom_call", output_to_operand_aliasing={{}: (9, {})} | custom-call | flops 1207959552 | bytes 6947860 | tf_op jit(solution)/shard_map/out_rim/pallas_call | solution.py:25
  (27 shorter events, 0.3 us)
Async XLA Ops:
  0.0 2.0 %copy-start = (bf16[4,4,128,256]{3,2,1,0:T(8,128)(2,1)S(1)}, bf16[4,4,128,256]{3,2,1,0:T(8,128)(2,1)}, u32[]{:S(2)}) copy-start(bf16[4,4,128,256]{3,2,1,0:T(8,128)(2,1)} %x_ref.5) | copy-start | bytes 3145732
  0.0 6.3 %copy-start.1 = (bf16[4,4,128,256]{3,2,1,0:T(8,128)(2,1)S(1)}, bf16[4,4,128,256]{3,2,1,0:T(8,128)(2,1)}, u32[]{:S(2)}) copy-start(bf16[4,4,128,256]{3,2,1,0:T(8,128)(2,1)} %g_ref.5) | copy-start | bytes 3145732
  2.0 4.2 %collective-permute-start = (bf16[2,4,128,256]{3,2,1,0:T(8,128)(2,1)}, bf16[2,4,128,256]{3,2,1,0:T(8,128)(2,1)S(1)}, u32[]{:S(2)}, u32[]{:S(2)}) collective-permute-start(bf16[2,4,128,256]{3,2,1,0:T(8,128)(2,1)} %slice.3), channel_id=1, source_target_pairs={{1,0},{0,1},{3,2},{2,3},{5,4},{4,5},{7,6},{6,7},{9,8},{8,9},{11,10... | collective-permute-start | bytes 1572872 | tf_op jit(solution)/shard_map/ppermute | solution.py:263
  2.8 13.8 %collective-permute-start.3 = (bf16[4,128,256]{2,1,0:T(8,128)(2,1)}, bf16[4,128,256]{2,1,0:T(8,128)(2,1)S(1)}, u32[]{:S(2)}, u32[]{:S(2)}) collective-permute-start(bf16[4,128,256]{2,1,0:T(8,128)(2,1)} %get-tuple-element.41), channel_id=1, source_target_pairs={{0,0},{2,4},{4,2},{6,8},{8,6},{10,12},{12,10},{14,14},{1,1},{3,5},... | collective-permute-start | bytes 786440 | tf_op jit(solution)/shard_map/ppermute | solution.py:254
  6.0 19.7 %collective-permute-start.2 = (bf16[4,128,256]{2,1,0:T(8,128)(2,1)S(1)}, bf16[4,128,256]{2,1,0:T(8,128)(2,1)S(1)}, u32[]{:S(2)}, u32[]{:S(2)}) collective-permute-start(bf16[4,128,256]{2,1,0:T(8,128)(2,1)S(1)} %get-tuple-element.42), channel_id=1, source_target_pairs={{0,2},{2,0},{4,6},{6,4},{8,10},{10,8},{12,14},{14,12},{1,3},{3,1},... | collective-permute-start | bytes 786440 | tf_op jit(solution)/shard_map/ppermute | solution.py:254
  6.3 2.9 %copy-start.2 = (bf16[3,3,256,256]{3,2,1,0:T(8,128)(2,1)S(1)}, bf16[3,3,256,256]{3,2,1,0:T(8,128)(2,1)}, u32[]{:S(2)}) copy-start(bf16[3,3,256,256]{3,2,1,0:T(8,128)(2,1)} %k_ref.13) | copy-start | bytes 3538948
  6.3 2.9 %copy-start.3 = (f32[256]{0:T(256)S(1)}, f32[256]{0:T(256)}, u32[]{:S(2)}) copy-start(f32[256]{0:T(256)} %param.10) | copy-start | bytes 3076
  6.3 1.1 %copy-start.5 = (bf16[3,256,256]{2,1,0:T(8,128)(2,1)S(1)}, bf16[3,256,256]{2,1,0:T(8,128)(2,1)}, u32[]{:S(2)}) copy-start(bf16[3,256,256]{2,1,0:T(8,128)(2,1)} %k_ref.7) | copy-start | bytes 1179652
  11.0 17.0 %collective-permute-start.1 = (bf16[2,2,128,256]{3,2,1,0:T(8,128)(2,1)S(1)}, bf16[2,2,128,256]{3,2,1,0:T(8,128)(2,1)S(1)}, u32[]{:S(2)}, u32[]{:S(2)}) collective-permute-start(bf16[2,2,128,256]{3,2,1,0:T(8,128)(2,1)S(1)} %get-tuple-element.26), channel_id=1, source_target_pairs={{0,1},{1,0},{2,3},{3,2},{4,5},{5,4},{6,7},{7,6},{8,9},{9,8},{10,11... | collective-permute-start | bytes 786440 | tf_op jit(solution)/shard_map/ppermute | solution.py:260
  11.2 20.1 %collective-permute-start.6 = (bf16[4,128,256]{2,1,0:T(8,128)(2,1)S(1)}, bf16[4,128,256]{2,1,0:T(8,128)(2,1)S(1)}, u32[]{:S(2)}, u32[]{:S(2)}) collective-permute-start(bf16[4,128,256]{2,1,0:T(8,128)(2,1)S(1)} %get-tuple-element.33), channel_id=1, source_target_pairs={{0,2},{2,0},{4,6},{6,4},{8,10},{10,8},{12,14},{14,12},{1,3},{3,1},... | collective-permute-start | bytes 786440 | tf_op jit(solution)/shard_map/ppermute | solution.py:254
  13.1 18.2 %collective-permute-start.7 = (bf16[4,128,256]{2,1,0:T(8,128)(2,1)S(1)}, bf16[4,128,256]{2,1,0:T(8,128)(2,1)S(1)}, u32[]{:S(2)}, u32[]{:S(2)}) collective-permute-start(bf16[4,128,256]{2,1,0:T(8,128)(2,1)S(1)} %get-tuple-element.34), channel_id=1, source_target_pairs={{0,0},{2,4},{4,2},{6,8},{8,6},{10,12},{12,10},{14,14},{1,1},{3,5},... | collective-permute-start | bytes 786440 | tf_op jit(solution)/shard_map/ppermute | solution.py:254
  25.8 2.2 %copy-start.4 = (bf16[3,3,256,256]{3,2,1,0:T(8,128)(2,1)S(1)}, bf16[3,3,256,256]{3,2,1,0:T(8,128)(2,1)}, u32[]{:S(2)}) copy-start(bf16[3,3,256,256]{3,2,1,0:T(8,128)(2,1)} %refs_4_.1) | copy-start | bytes 3538948
  25.8 2.2 %copy-start.6 = (bf16[3,256,256]{2,1,0:T(8,128)(2,1)S(1)}, bf16[3,256,256]{2,1,0:T(8,128)(2,1)}, u32[]{:S(2)}) copy-start(bf16[3,256,256]{2,1,0:T(8,128)(2,1)} %k_ref.11) | copy-start | bytes 1179652
  25.8 2.2 %copy-start.7 = (f32[256]{0:T(256)S(1)}, f32[256]{0:T(256)}, u32[]{:S(2)}) copy-start(f32[256]{0:T(256)} %param.11) | copy-start | bytes 3076
  27.9 3.5 %collective-permute-start.5 = (bf16[2,2,128,256]{3,2,1,0:T(8,128)(2,1)S(1)}, bf16[2,2,128,256]{3,2,1,0:T(8,128)(2,1)S(1)}, u32[]{:S(2)}, u32[]{:S(2)}) collective-permute-start(bf16[2,2,128,256]{3,2,1,0:T(8,128)(2,1)S(1)} %get-tuple-element.32), channel_id=1, source_target_pairs={{0,1},{1,0},{2,3},{3,2},{4,5},{5,4},{6,7},{7,6},{8,9},{9,8},{10,11... | collective-permute-start | bytes 786440 | tf_op jit(solution)/shard_map/ppermute | solution.py:260
  34.0 1.6 %collective-permute-start.8 = (bf16[2,2,128,256]{3,2,1,0:T(8,128)(2,1)S(1)}, bf16[2,2,128,256]{3,2,1,0:T(8,128)(2,1)S(1)}, u32[]{:S(2)}, u32[]{:S(2)}) collective-permute-start(bf16[2,2,128,256]{3,2,1,0:T(8,128)(2,1)S(1)} %get-tuple-element.37), channel_id=1, source_target_pairs={{1,0},{0,1},{3,2},{2,3},{5,4},{4,5},{7,6},{6,7},{9,8},{8,9},{11,10... | collective-permute-start | bytes 786440 | tf_op jit(solution)/shard_map/ppermute | solution.py:263
  34.1 6.8 %collective-permute-start.4 = (bf16[2,2,128,256]{3,2,1,0:T(8,128)(2,1)S(1)}, bf16[2,2,128,256]{3,2,1,0:T(8,128)(2,1)S(1)}, u32[]{:S(2)}, u32[]{:S(2)}) collective-permute-start(bf16[2,2,128,256]{3,2,1,0:T(8,128)(2,1)S(1)} %get-tuple-element.31), channel_id=1, source_target_pairs={{1,0},{0,1},{3,2},{2,3},{5,4},{4,5},{7,6},{6,7},{9,8},{8,9},{11,10... | collective-permute-start | bytes 786440 | tf_op jit(solution)/shard_map/ppermute | solution.py:263
  36.9 14.0 %collective-permute-start.9 = (bf16[4,128,256]{2,1,0:T(8,128)(2,1)S(1)}, bf16[4,128,256]{2,1,0:T(8,128)(2,1)S(1)}, u32[]{:S(2)}, u32[]{:S(2)}) collective-permute-start(bf16[4,128,256]{2,1,0:T(8,128)(2,1)S(1)} %get-tuple-element.39), channel_id=1, source_target_pairs={{0,2},{2,0},{4,6},{6,4},{8,10},{10,8},{12,14},{14,12},{1,3},{3,1},... | collective-permute-start | bytes 786440 | tf_op jit(solution)/shard_map/ppermute | solution.py:254
  36.9 14.0 %collective-permute-start.10 = (bf16[4,128,256]{2,1,0:T(8,128)(2,1)S(1)}, bf16[4,128,256]{2,1,0:T(8,128)(2,1)S(1)}, u32[]{:S(2)}, u32[]{:S(2)}) collective-permute-start(bf16[4,128,256]{2,1,0:T(8,128)(2,1)S(1)} %get-tuple-element.40), channel_id=1, source_target_pairs={{0,0},{2,4},{4,2},{6,8},{8,6},{10,12},{12,10},{14,14},{1,1},{3,5},... | collective-permute-start | bytes 786440 | tf_op jit(solution)/shard_map/ppermute | solution.py:254

commit v3 on v2

v3 whole, which is shorter than its diff:
```python
import functools

import jax
import jax.numpy as jnp
from jax import lax
from jax.experimental import pallas as pl
from jax.experimental.pallas import tpu as pltpu
from jax.sharding import PartitionSpec as P

EPS = 1e-06
F32 = jnp.float32
BF16 = jnp.bfloat16
VMEM = pl.BlockSpec(memory_space=pltpu.VMEM)
ANY = pl.BlockSpec(memory_space=pl.ANY)
RIM = 16


def shape_of(*shape):
    return jax.ShapeDtypeStruct(shape, BF16)


def call(kernel, outs, flops, *args, aliases=None, scratch=(), any_in=(), any_out=(), vmem=40, name=None):
    moved = sum(a.size * a.dtype.itemsize for a in (*args, *outs))
    return pl.pallas_call(
        kernel,
        out_shape=tuple(outs),
        in_specs=[ANY if i in any_in else VMEM for i in range(len(args))],
        out_specs=tuple(ANY if i in any_out else VMEM for i in range(len(outs))),
        scratch_shapes=scratch,
        input_output_aliases=aliases or {},
        compiler_params=pltpu.CompilerParams(vmem_limit_bytes=vmem * 2**20),
        cost_estimate=pl.CostEstimate(flops=flops, bytes_accessed=moved, transcendentals=0),
        name=name,
    )(*args)


def dot_nn(lhs, rhs):
    return lax.dot_general(lhs, rhs, (((1,), (0,)), ((), ())), preferred_element_type=F32)


def dot_nt(lhs, rhs):
    return lax.dot_general(lhs, rhs, (((1,), (1,)), ((), ())), preferred_element_type=F32)


def flat(block):
    return block.reshape(-1, block.shape[-1])


def mean_last(values):
    return jnp.mean(values, axis=-1, keepdims=True)


def logistic(values):
    return 0.5 + 0.5 * jnp.tanh(0.5 * values)


def unit_of(values):
    inv = lax.rsqrt(mean_last(values * values) + EPS)
    return inv, values * inv


def silu_of(values, gain):
    _, unit = unit_of(values)
    normed = unit * gain
    return (normed * logistic(normed)).astype(BF16)


def back_of(upstream, values, gain):
    inv, unit = unit_of(values)
    normed = unit * gain
    sig = logistic(normed)
    scaled = upstream * (sig * (1.0 + normed * (1.0 - sig))) * gain
    return inv * (scaled - unit * mean_last(scaled * unit))


def mixed(before, centre, after_it, lo, hi, cols):
    rows, span = before.shape[0], hi - lo
    at = lax.rem(lax.broadcasted_iota(jnp.int32, (rows, 1), 0), span) + lo
    down = pltpu.roll(before, 1, 0)
    up = pltpu.roll(after_it, rows - 1, 0)
    if lo == 0:
        down = jnp.where(at == 0, 0.0, down)
    if hi == cols:
        up = jnp.where(at == cols - 1, 0.0, up)
    return centre + down + up


def spatial(rows, kernel_ref, cols):
    lhs = jnp.concatenate(rows, axis=1)
    width = rows[0].shape[1]
    parts = [dot_nn(lhs, kernel_ref[:, dj].reshape(3 * width, -1)) for dj in range(3)]
    return mixed(*parts, 0, cols, cols)


def spatial_back(rows, kernel_ref, lo, hi, cols):
    lhs = jnp.concatenate(rows, axis=1)
    parts = [
        dot_nt(lhs, jnp.concatenate([kernel_ref[2 - di, 2 - dj] for di in range(3)], axis=1))
        for dj in range(3)
    ]
    return mixed(*parts, lo, hi, cols)


def time_back(padded, kernel_ref):
    head = (lax.axis_index("tm") == 0).astype(F32)
    weights = jnp.concatenate([kernel_ref[2], kernel_ref[1], kernel_ref[0]], axis=1)
    out = []
    for f in range(len(padded) - 2):
        part = dot_nt(jnp.concatenate(padded[f : f + 3], axis=1), weights)
        if f == 0:
            extra = jnp.concatenate([kernel_ref[0], kernel_ref[0], kernel_ref[1]], axis=1)
            part += head * dot_nt(jnp.concatenate([padded[0], padded[1], padded[0]], axis=1), extra)
        out.append(part.astype(BF16))
    return out


def later_of(block):
    last = lax.axis_index("tm") == lax.axis_size("tm") - 1
    return jnp.where(last, jnp.zeros_like(block), block)


def is_odd():
    return lax.rem(lax.axis_index("tile"), 2) == 1


def to_send(top, low):
    odd = is_odd()
    return jnp.where(odd, top, low), jnp.where(odd, low, top)


def neighbours(own, other):
    tile, odd = lax.axis_index("tile"), is_odd()
    above = jnp.where(tile == 0, jnp.zeros_like(own), jnp.where(odd, own, other))
    below = jnp.where(tile == lax.axis_size("tile") - 1, jnp.zeros_like(own), jnp.where(odd, other, own))
    return above, below


def spans_of(bounds):
    return list(zip(bounds[:-1], bounds[1:]))


def window(refs, bounds, lo, hi, pick=lambda ref: ref):
    parts = []
    for ref, (a, b) in zip(refs, spans_of(bounds)):
        if max(a, lo) < min(b, hi):
            parts.append(pick(ref)[:, max(a, lo) - a : min(b, hi) - a])
    return flat(parts[0] if len(parts) == 1 else jnp.concatenate(parts, axis=1))


def run_all(copies):
    for copy in copies:
        copy.start()
    for copy in copies:
        copy.wait()


def rims_kernel(x_ref, own_ref, other_ref, sems):
    nrows = x_ref.shape[1]
    odd = lax.rem(lax.axis_index("tile"), 2)
    run_all(
        [
            pltpu.make_async_copy(x_ref.at[:, (1 - odd) * (nrows - 1)], own_ref, sems.at[0]),
            pltpu.make_async_copy(x_ref.at[:, odd * (nrows - 1)], other_ref, sems.at[1]),
        ]
    )


def head_kernel(g_ref, head_ref, sems):
    run_all([pltpu.make_async_copy(g_ref.at[pl.ds(0, 2)], head_ref, sems.at[0])])


def act_kernel(x_ref, gain_ref, k_ref, a_ref, s_ref, tail_ref):
    frames, nrows, cols, width = x_ref.shape
    gain = gain_ref[...]
    for r in range(nrows):
        values = flat(x_ref[:, r]).astype(F32)
        a_ref[r] = silu_of(values, gain).reshape(frames, cols, width)
    for r in range(1, nrows - 1):
        rows = [flat(a_ref[r + d]) for d in (-1, 0, 1)]
        out = spatial(rows, k_ref, cols).astype(BF16).reshape(frames, cols, width)
        s_ref[r - 1] = out
        tail_ref[r - 1] = out[frames - 2 :]


def act_rim_kernel(own_ref, other_ref, a_ref, gain_ref, k_ref, s_ref, tail_ref):
    nrows, frames, cols, width = a_ref.shape
    gain = gain_ref[...]
    above, below = neighbours(flat(own_ref[...]), flat(other_ref[...]))
    above = silu_of(above.astype(F32), gain)
    below = silu_of(below.astype(F32), gain)
    last = nrows - 1
    for at, rows in enumerate(
        [[above, flat(a_ref[0]), flat(a_ref[1])], [flat(a_ref[last - 1]), flat(a_ref[last]), below]]
    ):
        out = spatial(rows, k_ref, cols).astype(BF16).reshape(frames, cols, width)
        s_ref[at] = out
        tail_ref[at] = out[frames - 2 :]


def grad_time_kernel(bounds, g_ref, later_ref, k_ref, d_ref, *send_refs):
    frames, nrows, cols, width = g_ref.shape
    padded = [flat(g_ref[f]) for f in range(frames)] + [later_of(flat(later_ref[f])) for f in range(2)]
    for f, out in enumerate(time_back(padded, k_ref)):
        out = out.reshape(nrows, cols, width)
        d_ref[:, f] = out
        own, other = to_send(out[0], out[nrows - 1])
        for i, (a, b) in enumerate(spans_of(bounds)):
            send_refs[2 * i][f] = own[a:b]
            send_refs[2 * i + 1][f] = other[a:b]


def hidden_kernel(which, lo, hi, bounds, s_ref, early_ref, d_ref, *refs):
    *rim_refs, gain_ref, kt_ref, ks_ref, o_ref, head_ref = refs
    nrows, frames, cols, width = d_ref.shape
    gain = gain_ref[...]
    at_start = lax.axis_index("tm") == 0
    a, b = max(0, lo - RIM), min(cols, hi + RIM)
    rows = {r: flat(d_ref[r, :, a:b]) for r in range(nrows)}
    if rim_refs:
        rows[-1], rows[nrows] = neighbours(*[window(rim_refs[i::2], bounds, a, b) for i in range(2)])

    for at, r in enumerate(which):
        first = s_ref[at, 0, lo:hi]
        early = [jnp.where(at_start, first, early_ref[at, f, lo:hi]) for f in range(2)]
        line = early + [s_ref[at, f, lo:hi] for f in range(frames)]
        lhs = jnp.concatenate(
            [jnp.concatenate(line[k : k + frames], axis=0) for k in range(3)], axis=1
        )
        hidden = dot_nn(lhs, kt_ref[...].reshape(3 * width, width))
        grad = spatial_back([rows[r + d] for d in (-1, 0, 1)], ks_ref, a, b, cols)
        if (a, b) != (lo, hi):
            grad = flat(grad.reshape(frames, b - a, width)[:, lo - a : hi - a])
        out = back_of(grad, hidden, gain).astype(BF16).reshape(frames, hi - lo, width)
        o_ref[at] = out
        head_ref[at] = out[:2]


def back_time_kernel(dh_ref, later_ref, k_ref, d_ref, *send_refs):
    rows, frames, cols, width = dh_ref.shape
    padded = [flat(dh_ref[:, f]) for f in range(frames)] + [later_of(flat(later_ref[:, f])) for f in range(2)]
    for f, out in enumerate(time_back(padded, k_ref)):
        out = out.reshape(rows, cols, width)
        d_ref[:, f] = out
        if send_refs:
            send_refs[0][f], send_refs[1][f] = to_send(out[0], out[1])


def finish(r, lo, hi, a, b, rows, x_ref, g_ref, gain, k_ref):
    frames, _, cols, width = x_ref.shape
    grad = spatial_back(rows, k_ref, a, b, cols)
    if (a, b) != (lo, hi):
        grad = flat(grad.reshape(frames, b - a, width)[:, lo - a : hi - a])
    out = back_of(grad, flat(x_ref[:, r, lo:hi]).astype(F32), gain)
    return (flat(g_ref[:, r, lo:hi]).astype(F32) + out).astype(BF16).reshape(frames, hi - lo, width)


def out_kernel(bounds, x_ref, g_ref, din_ref, *refs):
    *drim_refs, gain_ref, k_ref, o_ref, held, sems = refs
    frames, nrows, cols, width = x_ref.shape
    lines = [window(drim_refs, bounds, 0, cols, lambda ref, i=i: ref[i]) for i in range(2)]
    lines = lines[:1] + [flat(din_ref[r]) for r in range(nrows - 2)] + lines[1:]
    copies = []
    for r in range(1, nrows - 1):
        held[r - 1] = finish(r, 0, cols, 0, cols, lines[r - 1 : r + 2], x_ref, g_ref, gain_ref[...], k_ref)
        copies.append(pltpu.make_async_copy(held.at[r - 1], o_ref.at[:, r], sems.at[r - 1]))
        copies[-1].start()
    for copy in copies:
        copy.wait()


def out_rim_kernel(lo, hi, bounds, x_ref, g_ref, din_ref, *refs):
    *d_refs, gain_ref, k_ref, _, o_ref, held, sems = refs
    frames, nrows, cols, width = x_ref.shape
    count = len(bounds) - 1
    drim_refs, rim_refs = d_refs[:count], d_refs[count:]
    gain = gain_ref[...]
    a, b = max(0, lo - RIM), min(cols, hi + RIM)
    above, below = neighbours(*[window(rim_refs[i::2], bounds, a, b) for i in range(2)])
    top, low = [window(drim_refs, bounds, a, b, lambda ref, i=i: ref[i]) for i in range(2)]
    near, far = [flat(din_ref[r, :, a:b]) for r in (0, nrows - 3)]
    copies = []
    for at, (r, rows) in enumerate([(0, [above, top, near]), (nrows - 1, [far, low, below])]):
        held[at] = finish(r, lo, hi, a, b, rows, x_ref, g_ref, gain, k_ref)
        copies.append(pltpu.make_async_copy(held.at[at], o_ref.at[:, r, lo:hi], sems.at[at]))
        copies[-1].start()
    for copy in copies:
        copy.wait()


def after(value, *earlier):
    return lax.optimization_barrier((value,) + earlier)[0]


def on_device(
    frames_in,
    grad_out,
    gain_first,
    gain_second,
    spatial_first,
    temporal_first,
    spatial_second,
    temporal_second,
):
    frames, nrows, cols, width = frames_in.shape
    tiles, spans = lax.axis_size("tile"), lax.axis_size("tm")
    gain_first = gain_first.reshape(1, width)
    gain_second = gain_second.reshape(1, width)

    def swap(block, first):
        pairs = [(i, i + 1) for i in range(first, tiles - 1, 2)]
        route = dict(pairs + [(b, a) for a, b in pairs])
        return lax.ppermute(block, "tile", [(i, route.get(i, i)) for i in range(tiles)])

    def exchange(own, other):
        return [swap(own, 0), swap(other, 1)]

    def to_later(block):
        return lax.ppermute(block, "tm", [(i, (i + 1) % spans) for i in range(spans)])

    def to_earlier(block):
        return lax.ppermute(block, "tm", [((i + 1) % spans, i) for i in range(spans)])

    inner, rims = list(range(1, nrows - 1)), [0, nrows - 1]
    per_tap = 2 * frames * cols * width * width
    row = (frames, cols, width)
    d2_bounds = [0, cols]
    dh_bounds = [0, cols]
    out_bounds = [0, cols]

    x_send = call(
        rims_kernel, [shape_of(*row), shape_of(*row)], 1, frames_in,
        any_in=(0,), scratch=[pltpu.SemaphoreType.DMA((2,))], name="rims",
    )
    (g_head,) = call(
        head_kernel, [shape_of(2, nrows, cols, width)], 1, after(grad_out, *x_send),
        any_in=(0,), scratch=[pltpu.SemaphoreType.DMA((1,))], name="head",
    )
    g_later = to_earlier(g_head)
    x_rims = exchange(*x_send)

    d2, *d2_send = call(
        functools.partial(grad_time_kernel, d2_bounds),
        [shape_of(nrows, *row)] + [shape_of(frames, b - a, width) for a, b in spans_of(d2_bounds) for _ in range(2)],
        4 * nrows * per_tap,
        grad_out, g_later, temporal_second, name="grad_time",
    )

    a1, s_in, s_in_tail = call(
        act_kernel,
        [shape_of(nrows, *row), shape_of(nrows - 2, *row), shape_of(nrows - 2, 2, cols, width)],
        9 * (nrows - 2) * per_tap,
        frames_in, after(gain_first, d2), spatial_first, name="act",
    )

    def hidden(which, lo, hi, s, early, extra, gain, name):
        return call(
            functools.partial(hidden_kernel, which, lo, hi, d2_bounds),
            [shape_of(len(which), n, hi - lo, width) for n in (frames, 2)],
            12 * len(which) * per_tap * (hi - lo) // cols,
            s, early, d2, *extra, gain, temporal_first, spatial_second, name=name,
        )

    def back_time(dh, later, name, sends):
        return call(
            back_time_kernel,
            [shape_of(*dh.shape)] + [shape_of(*dh.shape[1:])] * sends,
            4 * dh.shape[0] * per_tap * dh.shape[2] // cols,
            dh, later, temporal_first, name=name,
        )

    s_rim, s_rim_tail = call(
        act_rim_kernel,
        [shape_of(2, *row), shape_of(2, 2, cols, width)],
        18 * per_tap,
        *x_rims, a1, gain_first, spatial_first, name="act_rim",
    )
    s_rim_early = to_later(s_rim_tail)

    dh_in, dh_in_head = hidden(inner, 0, cols, s_in, to_later(s_in_tail), (), after(gain_second, s_rim), "hidden")
    (d1_in,) = back_time(dh_in, to_earlier(dh_in_head), "back_time", 0)

    d2_rims = []
    for i in range(len(d2_bounds) - 1):
        d2_rims += exchange(*[after(block, s_rim) if i else block for block in d2_send[2 * i : 2 * i + 2]])

    d1_rim, d1_rims = [], []
    for i, (lo, hi) in enumerate(spans_of(dh_bounds)):
        dh, head = hidden(rims, lo, hi, s_rim, s_rim_early, d2_rims[: 2 * i + 2], after(gain_second, dh_in), "hidden_rim")
        part, *d1_send = back_time(dh, to_earlier(head), "back_time_rim", 2)
        d1_rim.append(part)
        d1_rims += exchange(*d1_send)

    held = lambda n, w: [pltpu.VMEM((n, frames, w, width), BF16), pltpu.SemaphoreType.DMA((n,))]
    (out,) = call(
        functools.partial(out_kernel, dh_bounds),
        [shape_of(*frames_in.shape)],
        9 * (nrows - 2) * per_tap,
        frames_in, grad_out, d1_in, *d1_rim, gain_first, spatial_first,
        any_out=(0,), scratch=held(nrows - 2, cols), name="out",
    )
    for i, (lo, hi) in enumerate(spans_of(out_bounds)):
        operands = [frames_in, grad_out, d1_in, *d1_rim[: i + 1], *d1_rims[: 2 * i + 2], gain_first, spatial_first, out]
        last = len(operands) - 1
        (out,) = call(
            functools.partial(out_rim_kernel, lo, hi, dh_bounds[: i + 2]),
            [shape_of(*frames_in.shape)],
            18 * per_tap * (hi - lo) // cols,
            *operands,
            any_in=(last,), any_out=(0,), aliases={last: 0}, scratch=held(2, hi - lo), name="out_rim",
        )
    return out


def solution(mesh):
    return jax.shard_map(
        on_device,
        mesh=mesh,
        in_specs=(
            P(("clip", "tm"), "tile", None, None),
            P(("clip", "tm"), "tile", None, None),
            P(),
            P(),
            P(),
            P(),
            P(),
            P(),
        ),
        out_specs=P(("clip", "tm"), "tile", None, None),
        check_vma=False,
    )
```

time: 55.7 us -> 50.1 us (0.90)
  Pallas kernels: 20.4 us -> 15.3 us
  local copies, waits for them, and re-layouts: 3.97 us -> 2.42 us
  waiting for transfers between devices: 16.8 us -> 18.1 us
    pallas_call x9 -> x11, Pallas kernels: 20.4 us -> 15.3 us  [call(): pl.pallas_call(kernel, out_shape=tuple(outs), in_specs=[ANY if i in any_i...]
    slice x1 -> x0, local copies, waits for them, and re-layouts: 2.02 us -> none  [on_device(): g_later = to_earlier(grad_out[:2])]
    unnamed x16 -> x18, local copies, waits for them, and re-layouts: 1.11 us -> 2.42 us
    ppermute x6, waiting for transfers between devices: 15.7 us -> 17 us  [swap(): lax.ppermute(block, 'tile', [(i, route.get(i, i)) for i in range(tiles)])]
    squeeze x1 -> x0, local copies, waits for them, and re-layouts: 0.74 us -> none  [on_device(): lax.dynamic_index_in_dim(frames_in, at, 1, keepdims=False)]
  transfers between devices with their start and end apart: 11 -> 11, of which waited for: 4 -> 4; matrix products, arithmetic and copies ran while one was open for 2% -> 0% of each run, Pallas kernels for 25% -> 21%
where the time goes in v3:
time: 50.1 us; the launch traced here: 49.4 us
  waiting for transfers between devices  18.1 us (36%)
  Pallas kernels  15.3 us (31%)
  starting transfers between devices  13.2 us (26%)
  local copies, waits for them, and re-layouts  2.42 us (5%)
    ppermute x6, waiting for transfers between devices, swap(): lax.ppermute(block, 'tile', [(i, route.get(i, i)) for i in range(tiles)])  17 us
    pallas_call x11, Pallas kernels, call(): pl.pallas_call(kernel, out_shape=tuple(outs), in_specs=[ANY if i in any_i...  15.3 us
    ppermute x6, starting transfers between devices, swap(): lax.ppermute(block, 'tile', [(i, route.get(i, i)) for i in range(tiles)])  12.4 us
    unnamed x18, local copies, waits for them, and re-layouts  2.42 us
    ppermute x3, waiting for transfers between devices, to_earlier(): lax.ppermute(block, 'tm', [((i + 1) % spans, i) for i in range(spans)])  1.03 us
  transfers between devices with their start and end apart: 11, of which 4 were waited for; matrix products, arithmetic and copies ran while one was open for 0% of the time, Pallas kernels for 21%

profile of v3, /device:TPU:24, one launch (start us, length us, event | category | flops | bytes accessed | tf_op | source)
XLA Modules:
  0.0 49.4 jit_solution(463947421588233287)
XLA Ops:
  0.0 1.2 %copy-done = bf16[4,4,128,256]{3,2,1,0:T(8,128)(2,1)S(1)} copy-done((bf16[4,4,128,256]{3,2,1,0:T(8,128)(2,1)S(1)}, bf16[4,4,128,256]{3,2,1,0:T(8,128)(2,1)}, u32[]{:S(2)}) %copy-start) | copy-done | bytes 1048600
  1.3 1.2 %copy-done.2 = bf16[4,4,128,256]{3,2,1,0:T(8,128)(2,1)S(1)} copy-done((bf16[4,4,128,256]{3,2,1,0:T(8,128)(2,1)S(1)}, bf16[4,4,128,256]{3,2,1,0:T(8,128)(2,1)}, u32[]{:S(2)}) %copy-start.2) | copy-done | bytes 1048600
  2.5 0.1 collective-permute-start
  2.6 1.6 %collective-permute-start.2 = (bf16[4,128,256]{2,1,0:T(8,128)(2,1)S(1)}, bf16[4,128,256]{2,1,0:T(8,128)(2,1)S(1)}, u32[]{:S(2)}, u32[]{:S(2)}) collective-permute-start(bf16[4,128,256]{2,1,0:T(8,128)(2,1)S(1)} %get-tuple-element.26), channel_id=1, source_target_pairs={{0,2},{2,0},{4,6},{6,4},{8,10},{10,8},{12,14},{14,12},{1,3},{3,1},... | collective-permute-start | bytes 786440 | tf_op jit(solution)/shard_map/ppermute | solution.py:312
  4.2 2.3 %collective-permute-start.3 = (bf16[4,128,256]{2,1,0:T(8,128)(2,1)S(1)}, bf16[4,128,256]{2,1,0:T(8,128)(2,1)S(1)}, u32[]{:S(2)}, u32[]{:S(2)}) collective-permute-start(bf16[4,128,256]{2,1,0:T(8,128)(2,1)S(1)} %get-tuple-element.27), channel_id=1, source_target_pairs={{0,0},{2,4},{4,2},{6,8},{8,6},{10,12},{12,10},{14,14},{1,1},{3,5},... | collective-permute-start | bytes 786440 | tf_op jit(solution)/shard_map/ppermute | solution.py:312
  6.5 1.2 %grad_time.1 = (bf16[4,4,128,256]{3,2,1,0:T(8,128)(2,1)S(1)}, bf16[4,128,256]{2,1,0:T(8,128)(2,1)S(1)}, bf16[4,128,256]{2,1,0:T(8,128)(2,1)S(1)}) custom-call(bf16[4,4,128,256]{3,2,1,0:T(8,128)(2,1)S(1)} %copy-done.2, bf16[2,4,128,256]{3,2,1,0:T(8,128)(2,1)S(1)} %collective-permute-done.later_ref, bf16[3,256,256]{2,1,0:T(8,128)(2,1)S(1)} %copy-done.6), custom_call_target="tpu_custom_call" | custom-call | flops 1073741824 | bytes 3538944 | tf_op jit(solution)/shard_map/grad_time/pallas_call | solution.py:24
  7.8 1.7 %act.1 = (bf16[4,4,128,256]{3,2,1,0:T(8,128)(2,1)S(1)}, bf16[2,4,128,256]{3,2,1,0:T(8,128)(2,1)S(1)}, bf16[2,2,128,256]{3,2,1,0:T(8,128)(2,1)S(1)}) custom-call(bf16[4,4,128,256]{3,2,1,0:T(8,128)(2,1)S(1)} %copy-done.1, f32[1,256]{1,0:T(1,128)S(1)} %bitcast.2, bf16[3,3,256,256]{3,2,1,0:T(8,128)(2,1)S(1)} %copy-done.3), custom_call_target="tpu_custom_call" | custom-call | flops 1207959552 | bytes 4064256 | tf_op jit(solution)/shard_map/act/pallas_call | solution.py:24
  9.5 0.1 collective-permute-start.1
  9.7 4.4 %collective-permute-start.7 = (bf16[4,128,256]{2,1,0:T(8,128)(2,1)S(1)}, bf16[4,128,256]{2,1,0:T(8,128)(2,1)S(1)}, u32[]{:S(2)}, u32[]{:S(2)}) collective-permute-start(bf16[4,128,256]{2,1,0:T(8,128)(2,1)S(1)} %get-tuple-element.40), channel_id=1, source_target_pairs={{0,0},{2,4},{4,2},{6,8},{8,6},{10,12},{12,10},{14,14},{1,1},{3,5},... | collective-permute-start | bytes 786440 | tf_op jit(solution)/shard_map/ppermute | solution.py:312
  14.1 8.9 %collective-permute-done.2.own_ref = bf16[4,128,256]{2,1,0:T(8,128)(2,1)S(1)} collective-permute-done((bf16[4,128,256]{2,1,0:T(8,128)(2,1)S(1)}, bf16[4,128,256]{2,1,0:T(8,128)(2,1)S(1)}, u32[]{:S(2)}, u32[]{:S(2)}) %collective-permute-start.2) | collective-permute-done | bytes 262176 | tf_op jit(solution)/shard_map/ppermute | solution.py:312
  23.0 1.5 %act_rim.1 = (bf16[2,4,128,256]{3,2,1,0:T(8,128)(2,1)S(1)}, bf16[2,2,128,256]{3,2,1,0:T(8,128)(2,1)S(1)}) custom-call(bf16[4,128,256]{2,1,0:T(8,128)(2,1)S(1)} %collective-permute-done.2.own_ref, bf16[4,128,256]{2,1,0:T(8,128)(2,1)S(1)} %collective-permute-done.3.other_ref, bf16[4,4,128,256]{3,2,1,0:T(8,128)(2,1)S(1)} %get-tuple-element.33.a_ref, ...), custom_call_target="tpu_custom_call" | custom-call | flops 1207959552 | bytes 3539968 | tf_op jit(solution)/shard_map/act_rim/pallas_call | solution.py:24
  24.7 2.0 %hidden.1 = (bf16[2,4,128,256]{3,2,1,0:T(8,128)(2,1)S(1)}, bf16[2,2,128,256]{3,2,1,0:T(8,128)(2,1)S(1)}) custom-call(bf16[2,4,128,256]{3,2,1,0:T(8,128)(2,1)S(1)} %get-tuple-element.31.s_ref, bf16[2,2,128,256]{3,2,1,0:T(8,128)(2,1)S(1)} %collective-permute-done.1.early_ref, bf16[4,4,128,256]{3,2,1,0:T(8,128)(2,1)S(1)} %get-tuple-element.29.d_ref, ...), custom_call_target="tpu_custom_call" | custom-call | flops 1610612736 | bytes 4195328 | tf_op jit(solution)/shard_map/hidden/pallas_call | solution.py:24
  26.7 1.4 %collective-permute-done.6.refs_0_ = bf16[4,128,256]{2,1,0:T(8,128)(2,1)S(1)} collective-permute-done((bf16[4,128,256]{2,1,0:T(8,128)(2,1)S(1)}, bf16[4,128,256]{2,1,0:T(8,128)(2,1)S(1)}, u32[]{:S(2)}, u32[]{:S(2)}) %collective-permute-start.6) | collective-permute-done | bytes 262176 | tf_op jit(solution)/shard_map/ppermute | solution.py:312
  28.2 2.1 %hidden_rim.1 = (bf16[2,4,128,256]{3,2,1,0:T(8,128)(2,1)S(1)}, bf16[2,2,128,256]{3,2,1,0:T(8,128)(2,1)S(1)}) custom-call(bf16[2,4,128,256]{3,2,1,0:T(8,128)(2,1)S(1)} %get-tuple-element.34.s_ref, bf16[2,2,128,256]{3,2,1,0:T(8,128)(2,1)S(1)} %collective-permute-done.5.early_ref, bf16[4,4,128,256]{3,2,1,0:T(8,128)(2,1)S(1)} %get-tuple-element.29.d_ref, ...), custom_call_target="tpu_custom_call" | custom-call | flops 1610612736 | bytes 4719616 | tf_op jit(solution)/shard_map/hidden_rim/pallas_call | solution.py:24
  30.3 0.1 collective-permute-start.8
  30.3 0.5 %collective-permute-start.4 = (bf16[2,2,128,256]{3,2,1,0:T(8,128)(2,1)S(1)}, bf16[2,2,128,256]{3,2,1,0:T(8,128)(2,1)S(1)}, u32[]{:S(2)}, u32[]{:S(2)}) collective-permute-start(bf16[2,2,128,256]{3,2,1,0:T(8,128)(2,1)S(1)} %get-tuple-element.37), channel_id=1, source_target_pairs={{1,0},{0,1},{3,2},{2,3},{5,4},{4,5},{7,6},{6,7},{9,8},{8,9},{11,10... | collective-permute-start | bytes 786440 | tf_op jit(solution)/shard_map/ppermute | solution.py:321
  30.8 1.0 %collective-permute-done.8.later_ref = bf16[2,2,128,256]{3,2,1,0:T(8,128)(2,1)S(1)} collective-permute-done((bf16[2,2,128,256]{3,2,1,0:T(8,128)(2,1)S(1)}, bf16[2,2,128,256]{3,2,1,0:T(8,128)(2,1)S(1)}, u32[]{:S(2)}, u32[]{:S(2)}) %collective-permute-start.8) | collective-permute-done | bytes 262176 | tf_op jit(solution)/shard_map/ppermute | solution.py:321
  31.9 0.7 %back_time_rim.1 = (bf16[2,4,128,256]{3,2,1,0:T(8,128)(2,1)S(1)}, bf16[4,128,256]{2,1,0:T(8,128)(2,1)S(1)}, bf16[4,128,256]{2,1,0:T(8,128)(2,1)S(1)}) custom-call(bf16[2,4,128,256]{3,2,1,0:T(8,128)(2,1)S(1)} %get-tuple-element.42.dh_ref, bf16[2,2,128,256]{3,2,1,0:T(8,128)(2,1)S(1)} %collective-permute-done.8.later_ref, bf16[3,256,256]{2,1,0:T(8,128)(2,1)S(1)} %copy-done.7), custom_call_target="tpu_custom_call" | custom-call | flops 536870912 | bytes 2228224 | tf_op jit(solution)/shard_map/back_time_rim/pallas_call | solution.py:24
  32.6 0.1 collective-permute-start.9
  32.7 4.0 %collective-permute-start.10 = (bf16[4,128,256]{2,1,0:T(8,128)(2,1)S(1)}, bf16[4,128,256]{2,1,0:T(8,128)(2,1)S(1)}, u32[]{:S(2)}, u32[]{:S(2)}) collective-permute-start(bf16[4,128,256]{2,1,0:T(8,128)(2,1)S(1)} %get-tuple-element.46), channel_id=1, source_target_pairs={{0,0},{2,4},{4,2},{6,8},{8,6},{10,12},{12,10},{14,14},{1,1},{3,5},... | collective-permute-start | bytes 786440 | tf_op jit(solution)/shard_map/ppermute | solution.py:312
  36.7 0.7 %back_time.1.din_ref = bf16[2,4,128,256]{3,2,1,0:T(8,128)(2,1)S(1)} custom-call(bf16[2,4,128,256]{3,2,1,0:T(8,128)(2,1)S(1)} %get-tuple-element.36.dh_ref, bf16[2,2,128,256]{3,2,1,0:T(8,128)(2,1)S(1)} %collective-permute-done.4.later_ref, bf16[3,256,256]{2,1,0:T(8,128)(2,1)S(1)} %copy-done.7), custom_call_target="tpu_custom_call" | custom-call | flops 536870912 | bytes 1703936 | tf_op jit(solution)/shard_map/back_time/pallas_call | solution.py:24
  37.4 2.6 %out.1.refs_5_ = bf16[4,4,128,256]{3,2,1,0:T(8,128)(2,1)} custom-call(bf16[4,4,128,256]{3,2,1,0:T(8,128)(2,1)S(1)} %copy-done.1, bf16[4,4,128,256]{3,2,1,0:T(8,128)(2,1)S(1)} %copy-done.2, bf16[2,4,128,256]{3,2,1,0:T(8,128)(2,1)S(1)} %back_time.1.din_ref, bf16[2,4,128,256]{3,2,1,0:T(8,128)(2,1)S(1)} %get-tuple-element.44.refs_0_, f32[1,256]{1,0:T(1,128)S(1)} %bitcast.4, ...), custom_call_target="tpu_custom_call" | custom-call | flops 1207959552 | bytes 5374976 | tf_op jit(solution)/shard_map/out/pallas_call | solution.py:24
  40.0 6.6 %collective-permute-done.9.refs_1_ = bf16[4,128,256]{2,1,0:T(8,128)(2,1)S(1)} collective-permute-done((bf16[4,128,256]{2,1,0:T(8,128)(2,1)S(1)}, bf16[4,128,256]{2,1,0:T(8,128)(2,1)S(1)}, u32[]{:S(2)}, u32[]{:S(2)}) %collective-permute-start.9) | collective-permute-done | bytes 262176 | tf_op jit(solution)/shard_map/ppermute | solution.py:312
  46.6 2.6 %out_rim.1 = bf16[4,4,128,256]{3,2,1,0:T(8,128)(2,1)} custom-call(bf16[4,4,128,256]{3,2,1,0:T(8,128)(2,1)S(1)} %copy-done.1, bf16[4,4,128,256]{3,2,1,0:T(8,128)(2,1)S(1)} %copy-done.2, bf16[2,4,128,256]{3,2,1,0:T(8,128)(2,1)S(1)} %back_time.1.din_ref, bf16[2,4,128,256]{3,2,1,0:T(8,128)(2,1)S(1)} %get-tuple-element.44.refs_0_, ...), custom_call_target="tpu_custom_call", output_to_operand_aliasing={{}: (8, {})} | custom-call | flops 1207959552 | bytes 6947840 | tf_op jit(solution)/shard_map/out_rim/pallas_call | solution.py:24
  (27 shorter events, 0.3 us)
Async XLA Ops:
  0.0 1.2 %copy-start = (bf16[4,4,128,256]{3,2,1,0:T(8,128)(2,1)S(1)}, bf16[4,4,128,256]{3,2,1,0:T(8,128)(2,1)}, u32[]{:S(2)}) copy-start(bf16[4,4,128,256]{3,2,1,0:T(8,128)(2,1)} %x_ref.7) | copy-start | bytes 3145732
  1.2 1.2 %copy-start.2 = (bf16[4,4,128,256]{3,2,1,0:T(8,128)(2,1)S(1)}, bf16[4,4,128,256]{3,2,1,0:T(8,128)(2,1)}, u32[]{:S(2)}) copy-start(bf16[4,4,128,256]{3,2,1,0:T(8,128)(2,1)} %g_ref.6) | copy-start | bytes 3145732
  1.2 5.3 %copy-start.6 = (bf16[3,256,256]{2,1,0:T(8,128)(2,1)S(1)}, bf16[3,256,256]{2,1,0:T(8,128)(2,1)}, u32[]{:S(2)}) copy-start(bf16[3,256,256]{2,1,0:T(8,128)(2,1)} %k_ref.5) | copy-start | bytes 1179652
  2.5 5.3 %copy-start.1 = (bf16[4,4,128,256]{3,2,1,0:T(8,128)(2,1)S(1)}, bf16[4,4,128,256]{3,2,1,0:T(8,128)(2,1)}, u32[]{:S(2)}) copy-start(bf16[4,4,128,256]{3,2,1,0:T(8,128)(2,1)} %x_ref.7) | copy-start | bytes 3145732
  2.5 5.3 %copy-start.3 = (bf16[3,3,256,256]{3,2,1,0:T(8,128)(2,1)S(1)}, bf16[3,3,256,256]{3,2,1,0:T(8,128)(2,1)}, u32[]{:S(2)}) copy-start(bf16[3,3,256,256]{3,2,1,0:T(8,128)(2,1)} %refs_4_.3) | copy-start | bytes 3538948
  2.5 5.3 %copy-start.4 = (f32[256]{0:T(256)S(1)}, f32[256]{0:T(256)}, u32[]{:S(2)}) copy-start(f32[256]{0:T(256)} %param.10) | copy-start | bytes 3076
  2.5 4.0 %collective-permute-start = (bf16[2,4,128,256]{3,2,1,0:T(8,128)(2,1)S(1)}, bf16[2,4,128,256]{3,2,1,0:T(8,128)(2,1)S(1)}, u32[]{:S(2)}, u32[]{:S(2)}) collective-permute-start(bf16[2,4,128,256]{3,2,1,0:T(8,128)(2,1)S(1)} %head.1), channel_id=1, source_target_pairs={{1,0},{0,1},{3,2},{2,3},{5,4},{4,5},{7,6},{6,7},{9,8},{8,9},{11,10... | collective-permute-start | bytes 1572872 | tf_op jit(solution)/shard_map/ppermute | solution.py:321
  2.6 20.4 %collective-permute-start.2 = (bf16[4,128,256]{2,1,0:T(8,128)(2,1)S(1)}, bf16[4,128,256]{2,1,0:T(8,128)(2,1)S(1)}, u32[]{:S(2)}, u32[]{:S(2)}) collective-permute-start(bf16[4,128,256]{2,1,0:T(8,128)(2,1)S(1)} %get-tuple-element.26), channel_id=1, source_target_pairs={{0,2},{2,0},{4,6},{6,4},{8,10},{10,8},{12,14},{14,12},{1,3},{3,1},... | collective-permute-start | bytes 786440 | tf_op jit(solution)/shard_map/ppermute | solution.py:312
  4.2 18.9 %collective-permute-start.3 = (bf16[4,128,256]{2,1,0:T(8,128)(2,1)S(1)}, bf16[4,128,256]{2,1,0:T(8,128)(2,1)S(1)}, u32[]{:S(2)}, u32[]{:S(2)}) collective-permute-start(bf16[4,128,256]{2,1,0:T(8,128)(2,1)S(1)} %get-tuple-element.27), channel_id=1, source_target_pairs={{0,0},{2,4},{4,2},{6,8},{8,6},{10,12},{12,10},{14,14},{1,1},{3,5},... | collective-permute-start | bytes 786440 | tf_op jit(solution)/shard_map/ppermute | solution.py:312
  9.5 15.1 %collective-permute-start.1 = (bf16[2,2,128,256]{3,2,1,0:T(8,128)(2,1)S(1)}, bf16[2,2,128,256]{3,2,1,0:T(8,128)(2,1)S(1)}, u32[]{:S(2)}, u32[]{:S(2)}) collective-permute-start(bf16[2,2,128,256]{3,2,1,0:T(8,128)(2,1)S(1)} %get-tuple-element.32), channel_id=1, source_target_pairs={{0,1},{1,0},{2,3},{3,2},{4,5},{5,4},{6,7},{7,6},{8,9},{9,8},{10,11... | collective-permute-start | bytes 786440 | tf_op jit(solution)/shard_map/ppermute | solution.py:318
  9.6 18.6 %collective-permute-start.6 = (bf16[4,128,256]{2,1,0:T(8,128)(2,1)S(1)}, bf16[4,128,256]{2,1,0:T(8,128)(2,1)S(1)}, u32[]{:S(2)}, u32[]{:S(2)}) collective-permute-start(bf16[4,128,256]{2,1,0:T(8,128)(2,1)S(1)} %get-tuple-element.39), channel_id=1, source_target_pairs={{0,2},{2,0},{4,6},{6,4},{8,10},{10,8},{12,14},{14,12},{1,3},{3,1},... | collective-permute-start | bytes 786440 | tf_op jit(solution)/shard_map/ppermute | solution.py:312
  9.7 18.5 %collective-permute-start.7 = (bf16[4,128,256]{2,1,0:T(8,128)(2,1)S(1)}, bf16[4,128,256]{2,1,0:T(8,128)(2,1)S(1)}, u32[]{:S(2)}, u32[]{:S(2)}) collective-permute-start(bf16[4,128,256]{2,1,0:T(8,128)(2,1)S(1)} %get-tuple-element.40), channel_id=1, source_target_pairs={{0,0},{2,4},{4,2},{6,8},{8,6},{10,12},{12,10},{14,14},{1,1},{3,5},... | collective-permute-start | bytes 786440 | tf_op jit(solution)/shard_map/ppermute | solution.py:312
  23.0 1.6 %copy-start.5 = (bf16[3,3,256,256]{3,2,1,0:T(8,128)(2,1)S(1)}, bf16[3,3,256,256]{3,2,1,0:T(8,128)(2,1)}, u32[]{:S(2)}) copy-start(bf16[3,3,256,256]{3,2,1,0:T(8,128)(2,1)} %refs_4_.2) | copy-start | bytes 3538948
  23.0 1.6 %copy-start.7 = (bf16[3,256,256]{2,1,0:T(8,128)(2,1)S(1)}, bf16[3,256,256]{2,1,0:T(8,128)(2,1)}, u32[]{:S(2)}) copy-start(bf16[3,256,256]{2,1,0:T(8,128)(2,1)} %k_ref.9) | copy-start | bytes 1179652
  23.0 1.7 %copy-start.8 = (f32[256]{0:T(256)S(1)}, f32[256]{0:T(256)}, u32[]{:S(2)}) copy-start(f32[256]{0:T(256)} %param.11) | copy-start | bytes 3076
  24.6 3.6 %collective-permute-start.5 = (bf16[2,2,128,256]{3,2,1,0:T(8,128)(2,1)S(1)}, bf16[2,2,128,256]{3,2,1,0:T(8,128)(2,1)S(1)}, u32[]{:S(2)}, u32[]{:S(2)}) collective-permute-start(bf16[2,2,128,256]{3,2,1,0:T(8,128)(2,1)S(1)} %get-tuple-element.38), channel_id=1, source_target_pairs={{0,1},{1,0},{2,3},{3,2},{4,5},{5,4},{6,7},{7,6},{8,9},{9,8},{10,11... | collective-permute-start | bytes 786440 | tf_op jit(solution)/shard_map/ppermute | solution.py:318
  30.3 1.6 %collective-permute-start.8 = (bf16[2,2,128,256]{3,2,1,0:T(8,128)(2,1)S(1)}, bf16[2,2,128,256]{3,2,1,0:T(8,128)(2,1)S(1)}, u32[]{:S(2)}, u32[]{:S(2)}) collective-permute-start(bf16[2,2,128,256]{3,2,1,0:T(8,128)(2,1)S(1)} %get-tuple-element.43), channel_id=1, source_target_pairs={{1,0},{0,1},{3,2},{2,3},{5,4},{4,5},{7,6},{6,7},{9,8},{8,9},{11,10... | collective-permute-start | bytes 786440 | tf_op jit(solution)/shard_map/ppermute | solution.py:321
  30.3 6.3 %collective-permute-start.4 = (bf16[2,2,128,256]{3,2,1,0:T(8,128)(2,1)S(1)}, bf16[2,2,128,256]{3,2,1,0:T(8,128)(2,1)S(1)}, u32[]{:S(2)}, u32[]{:S(2)}) collective-permute-start(bf16[2,2,128,256]{3,2,1,0:T(8,128)(2,1)S(1)} %get-tuple-element.37), channel_id=1, source_target_pairs={{1,0},{0,1},{3,2},{2,3},{5,4},{4,5},{7,6},{6,7},{9,8},{8,9},{11,10... | collective-permute-start | bytes 786440 | tf_op jit(solution)/shard_map/ppermute | solution.py:321
  32.6 14.0 %collective-permute-start.9 = (bf16[4,128,256]{2,1,0:T(8,128)(2,1)S(1)}, bf16[4,128,256]{2,1,0:T(8,128)(2,1)S(1)}, u32[]{:S(2)}, u32[]{:S(2)}) collective-permute-start(bf16[4,128,256]{2,1,0:T(8,128)(2,1)S(1)} %get-tuple-element.45), channel_id=1, source_target_pairs={{0,2},{2,0},{4,6},{6,4},{8,10},{10,8},{12,14},{14,12},{1,3},{3,1},... | collective-permute-start | bytes 786440 | tf_op jit(solution)/shard_map/ppermute | solution.py:312
  32.7 14.0 %collective-permute-start.10 = (bf16[4,128,256]{2,1,0:T(8,128)(2,1)S(1)}, bf16[4,128,256]{2,1,0:T(8,128)(2,1)S(1)}, u32[]{:S(2)}, u32[]{:S(2)}) collective-permute-start(bf16[4,128,256]{2,1,0:T(8,128)(2,1)S(1)} %get-tuple-element.46), channel_id=1, source_target_pairs={{0,0},{2,4},{4,2},{6,8},{8,6},{10,12},{12,10},{14,14},{1,1},{3,5},... | collective-permute-start | bytes 786440 | tf_op jit(solution)/shard_map/ppermute | solution.py:312

commit v4 on v3

v4 whole, which is shorter than its diff:
```python
import functools

import jax
import jax.numpy as jnp
from jax import lax
from jax.experimental import pallas as pl
from jax.experimental.pallas import tpu as pltpu
from jax.sharding import PartitionSpec as P

EPS = 1e-06
F32 = jnp.float32
BF16 = jnp.bfloat16
VMEM = pl.BlockSpec(memory_space=pltpu.VMEM)
ANY = pl.BlockSpec(memory_space=pl.ANY)


def shape_of(*shape, dtype=BF16):
    return jax.ShapeDtypeStruct(shape, dtype)


def call(kernel, outs, flops, *args, aliases=None, scratch=(), any_in=(), any_out=(), vmem=40, name=None):
    moved = sum(a.size * a.dtype.itemsize for a in (*args, *outs))
    return pl.pallas_call(
        kernel,
        out_shape=tuple(outs),
        in_specs=[ANY if i in any_in else VMEM for i in range(len(args))],
        out_specs=tuple(ANY if i in any_out else VMEM for i in range(len(outs))),
        scratch_shapes=scratch,
        input_output_aliases=aliases or {},
        compiler_params=pltpu.CompilerParams(vmem_limit_bytes=vmem * 2**20),
        cost_estimate=pl.CostEstimate(flops=flops, bytes_accessed=moved, transcendentals=0),
        name=name,
    )(*args)


def dot_nn(lhs, rhs):
    return lax.dot_general(lhs, rhs, (((1,), (0,)), ((), ())), preferred_element_type=F32)


def dot_nt(lhs, rhs):
    return lax.dot_general(lhs, rhs, (((1,), (1,)), ((), ())), preferred_element_type=F32)


def flat(block):
    return block.reshape(-1, block.shape[-1])


def mean_last(values):
    return jnp.mean(values, axis=-1, keepdims=True)


def logistic(values):
    return 0.5 + 0.5 * jnp.tanh(0.5 * values)


def unit_of(values):
    inv = lax.rsqrt(mean_last(values * values) + EPS)
    return inv, values * inv


def silu_of(values, gain):
    _, unit = unit_of(values)
    normed = unit * gain
    return (normed * logistic(normed)).astype(BF16)


def slope_of(values, gain):
    inv, unit = unit_of(values)
    normed = unit * gain
    sig = logistic(normed)
    return (sig * (1.0 + normed * (1.0 - sig))) * (gain * inv), unit


def back_of(upstream, slope, unit):
    scaled = upstream * slope
    return scaled - unit * mean_last(scaled * unit)


def mixed(before, centre, after_it, cols):
    rows = before.shape[0]
    at = lax.rem(lax.broadcasted_iota(jnp.int32, (rows, 1), 0), cols)
    down = jnp.where(at == 0, 0.0, pltpu.roll(before, 1, 0))
    up = jnp.where(at == cols - 1, 0.0, pltpu.roll(after_it, rows - 1, 0))
    return centre + down + up


def spatial(rows, kernel_ref, cols):
    lhs = jnp.concatenate(rows, axis=1)
    width = kernel_ref.shape[2]
    parts = [dot_nn(lhs, kernel_ref[:, dj].reshape(3 * width, -1)) for dj in range(3)]
    return mixed(*parts, cols)


def spatial_back(rows, taps, kernel_ref, cols):
    lhs = jnp.concatenate(rows, axis=1) if len(rows) > 1 else rows[0]
    parts = []
    for dj in range(3):
        weights = [kernel_ref[2 - di, 2 - dj] for di in taps]
        parts.append(dot_nt(lhs, jnp.concatenate(weights, axis=1) if len(taps) > 1 else weights[0]))
    return mixed(*parts, cols)


def time_back(padded, kernel_ref):
    head = (lax.axis_index("tm") == 0).astype(F32)
    weights = jnp.concatenate([kernel_ref[2], kernel_ref[1], kernel_ref[0]], axis=1)
    out = []
    for f in range(len(padded) - 2):
        part = dot_nt(jnp.concatenate(padded[f : f + 3], axis=1), weights)
        if f == 0:
            extra = jnp.concatenate([kernel_ref[0], kernel_ref[0], kernel_ref[1]], axis=1)
            part += head * dot_nt(jnp.concatenate([padded[0], padded[1], padded[0]], axis=1), extra)
        out.append(part.astype(BF16))
    return out


def later_of(block):
    last = lax.axis_index("tm") == lax.axis_size("tm") - 1
    return jnp.where(last, jnp.zeros_like(block), block)


def is_odd():
    return lax.rem(lax.axis_index("tile"), 2) == 1


def to_send(top, low):
    odd = is_odd()
    return jnp.where(odd, top, low), jnp.where(odd, low, top)


def neighbours(own, other):
    tile, odd = lax.axis_index("tile"), is_odd()
    above = jnp.where(tile == 0, jnp.zeros_like(own), jnp.where(odd, own, other))
    below = jnp.where(tile == lax.axis_size("tile") - 1, jnp.zeros_like(own), jnp.where(odd, other, own))
    return above, below


def run_all(copies):
    for copy in copies:
        copy.start()
    for copy in copies:
        copy.wait()


def rims_kernel(x_ref, own_ref, other_ref, sems):
    nrows = x_ref.shape[1]
    odd = lax.rem(lax.axis_index("tile"), 2)
    run_all(
        [
            pltpu.make_async_copy(x_ref.at[:, (1 - odd) * (nrows - 1)], own_ref, sems.at[0]),
            pltpu.make_async_copy(x_ref.at[:, odd * (nrows - 1)], other_ref, sems.at[1]),
        ]
    )


def act_kernel(x_ref, gain_ref, k_ref, a_ref, s_ref, tail_ref):
    frames, nrows, cols, width = x_ref.shape
    gain = gain_ref[...]
    for r in range(nrows):
        values = flat(x_ref[:, r]).astype(F32)
        a_ref[r] = silu_of(values, gain).reshape(frames, cols, width)
    for r in range(1, nrows - 1):
        rows = [flat(a_ref[r + d]) for d in (-1, 0, 1)]
        out = spatial(rows, k_ref, cols).astype(BF16).reshape(frames, cols, width)
        s_ref[r - 1] = out
        tail_ref[r - 1] = out[frames - 2 :]


def act_rim_kernel(own_ref, other_ref, a_ref, gain_ref, k_ref, s_ref, *tail_refs):
    nrows, frames, cols, width = a_ref.shape
    gain = gain_ref[...]
    above, below = neighbours(flat(own_ref[...]), flat(other_ref[...]))
    above = silu_of(above.astype(F32), gain)
    below = silu_of(below.astype(F32), gain)
    last = nrows - 1
    for at, rows in enumerate(
        [[above, flat(a_ref[0]), flat(a_ref[1])], [flat(a_ref[last - 1]), flat(a_ref[last]), below]]
    ):
        out = spatial(rows, k_ref, cols).astype(BF16).reshape(frames, cols, width)
        s_ref[at] = out
        tail_refs[at][...] = out[frames - 2 :]


def grad_time_kernel(g_ref, later_ref, k_ref, d_ref, own_ref, other_ref):
    frames, nrows, cols, width = g_ref.shape
    padded = [flat(g_ref[f]) for f in range(frames)] + [later_of(flat(later_ref[f])) for f in range(2)]
    for f, out in enumerate(time_back(padded, k_ref)):
        out = out.reshape(nrows, cols, width)
        d_ref[:, f] = out
        own_ref[f], other_ref[f] = to_send(out[0], out[nrows - 1])


def hidden_of(at, s_ref, early_ref, kt_ref):
    frames, cols, width = s_ref.shape[1:]
    at_start = lax.axis_index("tm") == 0
    line = [jnp.where(at_start, s_ref[at, 0], early_ref[f]) for f in range(2)]
    line += [s_ref[at, f] for f in range(frames)]
    lhs = jnp.concatenate([jnp.concatenate(line[k : k + frames], axis=0) for k in range(3)], axis=1)
    return dot_nn(lhs, kt_ref[...].reshape(3 * width, width))


def hidden_kernel(s_ref, early_ref, d_ref, gain_ref, kt_ref, ks_ref, o_ref, head_ref):
    nrows, frames, cols, width = d_ref.shape
    for r in range(1, nrows - 1):
        slope, unit = slope_of(hidden_of(r - 1, s_ref, early_ref.at[r - 1], kt_ref), gain_ref[...])
        grad = spatial_back([flat(d_ref[r + d]) for d in (-1, 0, 1)], [0, 1, 2], ks_ref, cols)
        out = back_of(grad, slope, unit).astype(BF16).reshape(frames, cols, width)
        o_ref[r - 1] = out
        head_ref[r - 1] = out[:2]


def store(refs, at, arrays):
    for ref, array in zip(refs, arrays):
        ref[at] = array.reshape(ref.shape[1:])


def hidden_own_kernel(s_ref, first_ref, last_ref, d_ref, gain_ref, kt_ref, ks_ref, *o_refs):
    nrows, _, cols, _ = d_ref.shape
    for at, (rows, taps) in enumerate([((0, 1), (1, 2)), ((nrows - 2, nrows - 1), (0, 1))]):
        slope, unit = slope_of(hidden_of(at, s_ref, (first_ref, last_ref)[at], kt_ref), gain_ref[...])
        grad = spatial_back([flat(d_ref[r]) for r in rows], taps, ks_ref, cols)
        store(o_refs, at, (grad, slope, unit))


def edges(own_ref, other_ref, k_ref, part_refs):
    cols = own_ref.shape[1]
    for at, row in enumerate(neighbours(flat(own_ref[...]), flat(other_ref[...]))):
        grad, slope, unit = [flat(ref[at]) for ref in part_refs]
        yield at, back_of(grad + spatial_back([row], [2 * at], k_ref, cols), slope, unit)


def hidden_rim_kernel(own_ref, other_ref, ks_ref, grad_ref, slope_ref, unit_ref, o_ref, head_ref):
    for at, out in edges(own_ref, other_ref, ks_ref, (grad_ref, slope_ref, unit_ref)):
        out = out.astype(BF16).reshape(o_ref.shape[1:])
        o_ref[at] = out
        head_ref[at] = out[:2]


def back_time_kernel(dh_ref, later_ref, k_ref, d_ref, *send_refs):
    rows, frames, cols, width = dh_ref.shape
    padded = [flat(dh_ref[:, f]) for f in range(frames)] + [later_of(flat(later_ref[:, f])) for f in range(2)]
    for f, out in enumerate(time_back(padded, k_ref)):
        out = out.reshape(rows, cols, width)
        d_ref[:, f] = out
        if send_refs:
            send_refs[0][f], send_refs[1][f] = to_send(out[0], out[rows - 1])


def lines_of(din_ref, drim_ref):
    return [flat(drim_ref[0])] + [flat(din_ref[r]) for r in range(din_ref.shape[0])] + [flat(drim_ref[1])]


def put(r, at, out, g_ref, held, o_ref, sems):
    held[at] = (flat(g_ref[:, r]).astype(F32) + out).astype(BF16).reshape(held.shape[1:])
    copy = pltpu.make_async_copy(held.at[at], o_ref.at[:, r], sems.at[at])
    copy.start()
    return copy


def out_kernel(x_ref, g_ref, din_ref, drim_ref, gain_ref, k_ref, o_ref, held, sems):
    _, nrows, cols, _ = x_ref.shape
    lines = lines_of(din_ref, drim_ref)
    copies = []
    for r in range(1, nrows - 1):
        grad = spatial_back(lines[r - 1 : r + 2], [0, 1, 2], k_ref, cols)
        out = back_of(grad, *slope_of(flat(x_ref[:, r]).astype(F32), gain_ref[...]))
        copies.append(put(r, r - 1, out, g_ref, held, o_ref, sems))
    for copy in copies:
        copy.wait()


def out_own_kernel(x_ref, din_ref, drim_ref, gain_ref, k_ref, *o_refs):
    _, nrows, cols, _ = x_ref.shape
    lines = lines_of(din_ref, drim_ref)
    for at, (r, rows, taps) in enumerate([(0, lines[:2], (1, 2)), (nrows - 1, lines[-2:], (0, 1))]):
        slope, unit = slope_of(flat(x_ref[:, r]).astype(F32), gain_ref[...])
        store(o_refs, at, (spatial_back(rows, taps, k_ref, cols), slope, unit))


def out_rim_kernel(own_ref, other_ref, k_ref, grad_ref, slope_ref, unit_ref, g_ref, _, o_ref, held, sems):
    nrows = g_ref.shape[1]
    copies = []
    for at, out in edges(own_ref, other_ref, k_ref, (grad_ref, slope_ref, unit_ref)):
        copies.append(put((0, nrows - 1)[at], at, out, g_ref, held, o_ref, sems))
    for copy in copies:
        copy.wait()


def after(value, *earlier):
    return lax.optimization_barrier((value,) + earlier)[0]


def on_device(
    frames_in,
    grad_out,
    gain_first,
    gain_second,
    spatial_first,
    temporal_first,
    spatial_second,
    temporal_second,
):
    frames, nrows, cols, width = frames_in.shape
    tiles, spans = lax.axis_size("tile"), lax.axis_size("tm")
    gain_first = gain_first.reshape(1, width)
    gain_second = gain_second.reshape(1, width)

    def swap(block, first):
        pairs = [(i, i + 1) for i in range(first, tiles - 1, 2)]
        route = dict(pairs + [(b, a) for a, b in pairs])
        return lax.ppermute(block, "tile", [(i, route.get(i, i)) for i in range(tiles)])

    def exchange(own, other):
        return [swap(own, 0), swap(other, 1)]

    def to_later(block):
        return lax.ppermute(block, "tm", [(i, (i + 1) % spans) for i in range(spans)])

    def to_earlier(block):
        return lax.ppermute(block, "tm", [((i + 1) % spans, i) for i in range(spans)])

    per_tap = 2 * frames * cols * width * width
    row = (frames, cols, width)
    inner = nrows - 2
    parts = [shape_of(2, *row, dtype=F32)] * 3
    two = lambda count: [shape_of(count, *row), shape_of(count, 2, cols, width)]
    held = lambda count: [pltpu.VMEM((count, *row), BF16), pltpu.SemaphoreType.DMA((count,))]

    x_send = call(
        rims_kernel, [shape_of(*row)] * 2, 1, frames_in,
        any_in=(0,), scratch=[pltpu.SemaphoreType.DMA((2,))], name="rims",
    )
    g_later = to_earlier(grad_out[:2])
    grads = after(grad_out, *x_send)
    x_rims = exchange(*x_send)

    d2, *d2_send = call(
        grad_time_kernel, [shape_of(nrows, *row)] + [shape_of(*row)] * 2, 4 * nrows * per_tap,
        grads, g_later, temporal_second, name="grad_time",
    )
    d2_rims = exchange(*d2_send)

    a1, s_in, s_in_tail = call(
        act_kernel, [shape_of(nrows, *row)] + two(inner), 9 * inner * per_tap,
        frames_in, after(gain_first, d2), spatial_first, name="act",
    )
    s_rim, *s_rim_tails = call(
        act_rim_kernel, [shape_of(2, *row)] + [shape_of(2, cols, width)] * 2, 18 * per_tap,
        *x_rims, a1, gain_first, spatial_first, name="act_rim",
    )
    s_rim_early = [to_later(tail) for tail in s_rim_tails]

    dh_in, dh_in_head = call(
        hidden_kernel, two(inner), 12 * inner * per_tap,
        s_in, to_later(s_in_tail), d2, after(gain_second, s_rim), temporal_first, spatial_second, name="hidden",
    )
    dh_in_later = to_earlier(dh_in_head)
    own = call(
        hidden_own_kernel, parts, 18 * per_tap,
        s_rim, *s_rim_early, d2, after(gain_second, dh_in), temporal_first, spatial_second, name="hidden_own",
    )
    dh_rim, dh_rim_head = call(
        hidden_rim_kernel, two(2), 6 * per_tap,
        *d2_rims, spatial_second, *own, name="hidden_rim",
    )

    def back_time(dh, later, sends, name):
        return call(
            back_time_kernel, [shape_of(*dh.shape)] + [shape_of(*row)] * sends, 4 * dh.shape[0] * per_tap,
            dh, later, temporal_first, name=name,
        )

    d1_rim, *d1_send = back_time(dh_rim, to_earlier(dh_rim_head), 2, "back_time_rim")
    d1_rims = exchange(*d1_send)
    (d1_in,) = back_time(dh_in, dh_in_later, 0, "back_time")

    own = call(
        out_own_kernel, parts, 12 * per_tap,
        frames_in, d1_in, d1_rim, gain_first, spatial_first, name="out_own",
    )
    (out,) = call(
        out_kernel, [shape_of(*frames_in.shape)], 9 * inner * per_tap,
        frames_in, grads, d1_in, d1_rim, gain_first, spatial_first,
        any_out=(0,), scratch=held(inner), name="out",
    )
    return call(
        out_rim_kernel, [shape_of(*frames_in.shape)], 6 * per_tap,
        *d1_rims, spatial_first, *own, grads, out,
        any_in=(7,), any_out=(0,), aliases={7: 0}, scratch=held(2), name="out_rim",
    )[0]


def solution(mesh):
    return jax.shard_map(
        on_device,
        mesh=mesh,
        in_specs=(
            P(("clip", "tm"), "tile", None, None),
            P(("clip", "tm"), "tile", None, None),
            P(),
            P(),
            P(),
            P(),
            P(),
            P(),
        ),
        out_specs=P(("clip", "tm"), "tile", None, None),
        check_vma=False,
    )
```

time: 50.1 us -> 47 us (0.938); the launches traced: 49.4 us -> 46.8 us
  waiting for transfers between devices: 18.1 us -> 14.8 us
  Pallas kernels: 15.3 us -> 16.2 us
    ppermute x6, waiting for transfers between devices: 17 us -> 13.8 us  [swap(): lax.ppermute(block, 'tile', [(i, route.get(i, i)) for i in range(tiles)])]
    unnamed x18 -> x16, local copies, waits for them, and re-layouts: 2.42 us -> 1.08 us
    slice x0 -> x1, local copies, waits for them, and re-layouts: none -> 1.22 us  [on_device(): g_later = to_earlier(grad_out[:2])]
    pallas_call x11 -> x12, Pallas kernels: 15.3 us -> 16.2 us  [call(): pl.pallas_call(kernel, out_shape=tuple(outs), in_specs=[ANY if i in any_i...]
    ppermute x6, starting transfers between devices: 12.4 us -> 11.8 us  [swap(): lax.ppermute(block, 'tile', [(i, route.get(i, i)) for i in range(tiles)])]
  transfers between devices with their start and end apart: 11 -> 12, of which waited for: 4 -> 3; matrix products, arithmetic and copies ran while one was open for 0% -> 0% of each run, Pallas kernels for 21% -> 29%
where the time goes in v4:
time: 47 us; the launch traced here: 46.8 us
  Pallas kernels  16.2 us (34%)
  waiting for transfers between devices  14.8 us (31%)
  starting transfers between devices  13 us (28%)
  local copies, waits for them, and re-layouts  2.31 us (5%)
    pallas_call x12, Pallas kernels, call(): pl.pallas_call(kernel, out_shape=tuple(outs), in_specs=[ANY if i in any_i...  16.2 us
    ppermute x6, waiting for transfers between devices, swap(): lax.ppermute(block, 'tile', [(i, route.get(i, i)) for i in range(tiles)])  13.8 us
    ppermute x6, starting transfers between devices, swap(): lax.ppermute(block, 'tile', [(i, route.get(i, i)) for i in range(tiles)])  11.8 us
    slice x1, local copies, waits for them, and re-layouts, on_device(): g_later = to_earlier(grad_out[:2])  1.22 us
    unnamed x16, local copies, waits for them, and re-layouts  1.08 us
    ppermute x3, waiting for transfers between devices, to_earlier(): lax.ppermute(block, 'tm', [((i + 1) % spans, i) for i in range(spans)])  1.03 us
  transfers between devices with their start and end apart: 12, of which 3 were waited for; matrix products, arithmetic and copies ran while one was open for 0% of the time, Pallas kernels for 29%

profile of v4, /device:TPU:24, one launch (start us, length us, event | category | flops | bytes accessed | tf_op | source)
XLA Modules:
  0.0 46.8 jit_solution(5804076699109606605)
XLA Ops:
  0.0 1.2 %slice.3 = bf16[2,4,128,256]{3,2,1,0:T(8,128)(2,1)S(1)} slice(bf16[4,4,128,256]{3,2,1,0:T(8,128)(2,1)} %g_ref.2), slice={[0:2], [0:4], [0:128], [0:256]} | slice | bytes 1048576 | tf_op jit(solution)/shard_map/slice | solution.py:332
  1.2 0.1 collective-permute-start
  1.4 1.6 %collective-permute-start.3 = (bf16[4,128,256]{2,1,0:T(8,128)(2,1)S(1)}, bf16[4,128,256]{2,1,0:T(8,128)(2,1)S(1)}, u32[]{:S(2)}, u32[]{:S(2)}) collective-permute-start(bf16[4,128,256]{2,1,0:T(8,128)(2,1)S(1)} %get-tuple-element.33), channel_id=1, source_target_pairs={{0,2},{2,0},{4,6},{6,4},{8,10},{10,8},{12,14},{14,12},{1,3},{3,1},... | collective-permute-start | bytes 786440 | tf_op jit(solution)/shard_map/ppermute | solution.py:310
  3.0 2.4 %collective-permute-start.4 = (bf16[4,128,256]{2,1,0:T(8,128)(2,1)S(1)}, bf16[4,128,256]{2,1,0:T(8,128)(2,1)S(1)}, u32[]{:S(2)}, u32[]{:S(2)}) collective-permute-start(bf16[4,128,256]{2,1,0:T(8,128)(2,1)S(1)} %get-tuple-element.34), channel_id=1, source_target_pairs={{0,0},{2,4},{4,2},{6,8},{8,6},{10,12},{12,10},{14,14},{1,1},{3,5},... | collective-permute-start | bytes 786440 | tf_op jit(solution)/shard_map/ppermute | solution.py:310
  5.5 1.0 %copy-done.5 = bf16[3,256,256]{2,1,0:T(8,128)(2,1)S(1)} copy-done((bf16[3,256,256]{2,1,0:T(8,128)(2,1)S(1)}, bf16[3,256,256]{2,1,0:T(8,128)(2,1)}, u32[]{:S(2)}) %copy-start.5) | copy-done | bytes 393240
  6.5 1.2 %grad_time.1 = (bf16[4,4,128,256]{3,2,1,0:T(8,128)(2,1)S(1)}, bf16[4,128,256]{2,1,0:T(8,128)(2,1)S(1)}, bf16[4,128,256]{2,1,0:T(8,128)(2,1)S(1)}) custom-call(bf16[4,4,128,256]{3,2,1,0:T(8,128)(2,1)S(1)} %copy-done.2, bf16[2,4,128,256]{3,2,1,0:T(8,128)(2,1)S(1)} %collective-permute-done.later_ref, bf16[3,256,256]{2,1,0:T(8,128)(2,1)S(1)} %copy-done.5), custom_call_target="tpu_custom_call" | custom-call | flops 1073741824 | bytes 3538944 | tf_op jit(solution)/shard_map/grad_time/pallas_call | solution.py:23
  7.7 1.7 %act.1 = (bf16[4,4,128,256]{3,2,1,0:T(8,128)(2,1)S(1)}, bf16[2,4,128,256]{3,2,1,0:T(8,128)(2,1)S(1)}, bf16[2,2,128,256]{3,2,1,0:T(8,128)(2,1)S(1)}) custom-call(bf16[4,4,128,256]{3,2,1,0:T(8,128)(2,1)S(1)} %copy-done.1, f32[1,256]{1,0:T(1,128)S(1)} %bitcast.2, bf16[3,3,256,256]{3,2,1,0:T(8,128)(2,1)S(1)} %copy-done), custom_call_target="tpu_custom_call" | custom-call | flops 1207959552 | bytes 4064256 | tf_op jit(solution)/shard_map/act/pallas_call | solution.py:23
  9.6 4.4 %collective-permute-start.2 = (bf16[4,128,256]{2,1,0:T(8,128)(2,1)S(1)}, bf16[4,128,256]{2,1,0:T(8,128)(2,1)S(1)}, u32[]{:S(2)}, u32[]{:S(2)}) collective-permute-start(bf16[4,128,256]{2,1,0:T(8,128)(2,1)S(1)} %get-tuple-element.37), channel_id=1, source_target_pairs={{0,0},{2,4},{4,2},{6,8},{8,6},{10,12},{12,10},{14,14},{1,1},{3,5},... | collective-permute-start | bytes 786440 | tf_op jit(solution)/shard_map/ppermute | solution.py:310
  14.1 7.8 %collective-permute-done.3.own_ref = bf16[4,128,256]{2,1,0:T(8,128)(2,1)S(1)} collective-permute-done((bf16[4,128,256]{2,1,0:T(8,128)(2,1)S(1)}, bf16[4,128,256]{2,1,0:T(8,128)(2,1)S(1)}, u32[]{:S(2)}, u32[]{:S(2)}) %collective-permute-start.3) | collective-permute-done | bytes 262176 | tf_op jit(solution)/shard_map/ppermute | solution.py:310
  21.9 1.5 %act_rim.1 = (bf16[2,4,128,256]{3,2,1,0:T(8,128)(2,1)S(1)}, bf16[2,128,256]{2,1,0:T(8,128)(2,1)S(1)}, bf16[2,128,256]{2,1,0:T(8,128)(2,1)S(1)}) custom-call(bf16[4,128,256]{2,1,0:T(8,128)(2,1)S(1)} %collective-permute-done.3.own_ref, bf16[4,128,256]{2,1,0:T(8,128)(2,1)S(1)} %collective-permute-done.4.other_ref, ...), custom_call_target="tpu_custom_call" | custom-call | flops 1207959552 | bytes 3539968 | tf_op jit(solution)/shard_map/act_rim/pallas_call | solution.py:23
  23.5 0.5 %collective-permute-start.6 = (bf16[2,128,256]{2,1,0:T(8,128)(2,1)S(1)}, bf16[2,128,256]{2,1,0:T(8,128)(2,1)S(1)}, u32[]{:S(2)}, u32[]{:S(2)}) collective-permute-start(bf16[2,128,256]{2,1,0:T(8,128)(2,1)S(1)} %get-tuple-element.43), channel_id=1, source_target_pairs={{0,1},{1,0},{2,3},{3,2},{4,5},{5,4},{6,7},{7,6},{8,9},{9,8},{10,11... | collective-permute-start | bytes 393224 | tf_op jit(solution)/shard_map/ppermute | solution.py:316
  24.0 2.1 %hidden.1 = (bf16[2,4,128,256]{3,2,1,0:T(8,128)(2,1)S(1)}, bf16[2,2,128,256]{3,2,1,0:T(8,128)(2,1)S(1)}) custom-call(bf16[2,4,128,256]{3,2,1,0:T(8,128)(2,1)S(1)} %get-tuple-element.44.s_ref, bf16[2,2,128,256]{3,2,1,0:T(8,128)(2,1)S(1)} %collective-permute-done.7.early_ref, bf16[4,4,128,256]{3,2,1,0:T(8,128)(2,1)S(1)} %get-tuple-element.38.d_ref, ...), custom_call_target="tpu_custom_call" | custom-call | flops 1610612736 | bytes 4195328 | tf_op jit(solution)/shard_map/hidden/pallas_call | solution.py:23
  26.1 1.7 %hidden_own.1 = (f32[2,4,128,256]{3,2,1,0:T(8,128)S(1)}, f32[2,4,128,256]{3,2,1,0:T(8,128)S(1)}, f32[2,4,128,256]{3,2,1,0:T(8,128)S(1)}) custom-call(bf16[2,4,128,256]{3,2,1,0:T(8,128)(2,1)S(1)} %get-tuple-element.41.s_ref, bf16[2,128,256]{2,1,0:T(8,128)(2,1)S(1)} %collective-permute-done.5.first_ref, ...), custom_call_target="tpu_custom_call" | custom-call | flops 1207959552 | bytes 6554624 | tf_op jit(solution)/shard_map/hidden_own/pallas_call | solution.py:23
  27.8 0.9 %hidden_rim.1 = (bf16[2,4,128,256]{3,2,1,0:T(8,128)(2,1)S(1)}, bf16[2,2,128,256]{3,2,1,0:T(8,128)(2,1)S(1)}) custom-call(bf16[4,128,256]{2,1,0:T(8,128)(2,1)S(1)} %collective-permute-done.1.own_ref, bf16[4,128,256]{2,1,0:T(8,128)(2,1)S(1)} %collective-permute-done.2.other_ref, bf16[3,3,256,256]{3,2,1,0:T(8,128)(2,1)S(1)} %copy-done.3, ...), custom_call_target="tpu_custom_call" | custom-call | flops 402653184 | bytes 5636096 | tf_op jit(solution)/shard_map/hidden_rim/pallas_call | solution.py:23
  28.7 0.1 collective-permute-start.8
  28.8 0.4 collective-permute-start.11
  29.3 1.0 %collective-permute-done.8.later_ref = bf16[2,2,128,256]{3,2,1,0:T(8,128)(2,1)S(1)} collective-permute-done((bf16[2,2,128,256]{3,2,1,0:T(8,128)(2,1)S(1)}, bf16[2,2,128,256]{3,2,1,0:T(8,128)(2,1)S(1)}, u32[]{:S(2)}, u32[]{:S(2)}) %collective-permute-start.8) | collective-permute-done | bytes 262176 | tf_op jit(solution)/shard_map/ppermute | solution.py:319
  30.3 0.7 %back_time_rim.1 = (bf16[2,4,128,256]{3,2,1,0:T(8,128)(2,1)S(1)}, bf16[4,128,256]{2,1,0:T(8,128)(2,1)S(1)}, bf16[4,128,256]{2,1,0:T(8,128)(2,1)S(1)}) custom-call(bf16[2,4,128,256]{3,2,1,0:T(8,128)(2,1)S(1)} %get-tuple-element.52.dh_ref, bf16[2,2,128,256]{3,2,1,0:T(8,128)(2,1)S(1)} %collective-permute-done.8.later_ref, bf16[3,256,256]{2,1,0:T(8,128)(2,1)S(1)} %copy-done.6), custom_call_target="tpu_custom_call" | custom-call | flops 536870912 | bytes 2228224 | tf_op jit(solution)/shard_map/back_time_rim/pallas_call | solution.py:23
  31.1 3.2 %collective-permute-start.10 = (bf16[4,128,256]{2,1,0:T(8,128)(2,1)S(1)}, bf16[4,128,256]{2,1,0:T(8,128)(2,1)S(1)}, u32[]{:S(2)}, u32[]{:S(2)}) collective-permute-start(bf16[4,128,256]{2,1,0:T(8,128)(2,1)S(1)} %get-tuple-element.55), channel_id=1, source_target_pairs={{0,0},{2,4},{4,2},{6,8},{8,6},{10,12},{12,10},{14,14},{1,1},{3,5},... | collective-permute-start | bytes 786440 | tf_op jit(solution)/shard_map/ppermute | solution.py:310
  34.3 0.7 %back_time.1.din_ref = bf16[2,4,128,256]{3,2,1,0:T(8,128)(2,1)S(1)} custom-call(bf16[2,4,128,256]{3,2,1,0:T(8,128)(2,1)S(1)} %get-tuple-element.47.dh_ref, bf16[2,2,128,256]{3,2,1,0:T(8,128)(2,1)S(1)} %collective-permute-done.11.later_ref, bf16[3,256,256]{2,1,0:T(8,128)(2,1)S(1)} %copy-done.6), custom_call_target="tpu_custom_call" | custom-call | flops 536870912 | bytes 1703936 | tf_op jit(solution)/shard_map/back_time/pallas_call | solution.py:23
  35.0 1.4 %out_own.1 = (f32[2,4,128,256]{3,2,1,0:T(8,128)S(1)}, f32[2,4,128,256]{3,2,1,0:T(8,128)S(1)}, f32[2,4,128,256]{3,2,1,0:T(8,128)S(1)}) custom-call(bf16[4,4,128,256]{3,2,1,0:T(8,128)(2,1)S(1)} %copy-done.1, bf16[2,4,128,256]{3,2,1,0:T(8,128)(2,1)S(1)} %back_time.1.din_ref, bf16[2,4,128,256]{3,2,1,0:T(8,128)(2,1)S(1)} %get-tuple-element.57.drim_ref, ...), custom_call_target="tpu_custom_call" | custom-call | flops 805306368 | bytes 6423552 | tf_op jit(solution)/shard_map/out_own/pallas_call | solution.py:23
  36.5 2.6 %out.1._ = bf16[4,4,128,256]{3,2,1,0:T(8,128)(2,1)} custom-call(bf16[4,4,128,256]{3,2,1,0:T(8,128)(2,1)S(1)} %copy-done.1, bf16[4,4,128,256]{3,2,1,0:T(8,128)(2,1)S(1)} %copy-done.2, bf16[2,4,128,256]{3,2,1,0:T(8,128)(2,1)S(1)} %back_time.1.din_ref, bf16[2,4,128,256]{3,2,1,0:T(8,128)(2,1)S(1)} %get-tuple-element.57.drim_ref, f32[1,256]{1,0:T(1,128)S(1)} %bitcast.5, ...), custom_call_target="tpu_custom_call" | custom-call | flops 1207959552 | bytes 5374976 | tf_op jit(solution)/shard_map/out/pallas_call | solution.py:23
  39.1 6.0 %collective-permute-done.9.own_ref = bf16[4,128,256]{2,1,0:T(8,128)(2,1)S(1)} collective-permute-done((bf16[4,128,256]{2,1,0:T(8,128)(2,1)S(1)}, bf16[4,128,256]{2,1,0:T(8,128)(2,1)S(1)}, u32[]{:S(2)}, u32[]{:S(2)}) %collective-permute-start.9) | collective-permute-done | bytes 262176 | tf_op jit(solution)/shard_map/ppermute | solution.py:310
  45.1 1.6 %out_rim.1 = bf16[4,4,128,256]{3,2,1,0:T(8,128)(2,1)} custom-call(bf16[4,128,256]{2,1,0:T(8,128)(2,1)S(1)} %collective-permute-done.9.own_ref, bf16[4,128,256]{2,1,0:T(8,128)(2,1)S(1)} %collective-permute-done.10.other_ref, bf16[3,3,256,256]{3,2,1,0:T(8,128)(2,1)S(1)} %copy-done, ...), custom_call_target="tpu_custom_call", output_to_operand_aliasing={{}: (7, {})} | custom-call | flops 402653184 | bytes 7995392 | tf_op jit(solution)/shard_map/out_rim/pallas_call | solution.py:23
  (29 shorter events, 0.5 us)
Async XLA Ops:
  0.0 1.4 %copy-start.1 = (bf16[4,4,128,256]{3,2,1,0:T(8,128)(2,1)S(1)}, bf16[4,4,128,256]{3,2,1,0:T(8,128)(2,1)}, u32[]{:S(2)}) copy-start(bf16[4,4,128,256]{3,2,1,0:T(8,128)(2,1)} %x_ref.7) | copy-start | bytes 3145732
  0.0 5.5 %copy-start.2 = (bf16[4,4,128,256]{3,2,1,0:T(8,128)(2,1)S(1)}, bf16[4,4,128,256]{3,2,1,0:T(8,128)(2,1)}, u32[]{:S(2)}) copy-start(bf16[4,4,128,256]{3,2,1,0:T(8,128)(2,1)} %g_ref.2) | copy-start | bytes 3145732
  1.2 4.2 %collective-permute-start = (bf16[2,4,128,256]{3,2,1,0:T(8,128)(2,1)S(1)}, bf16[2,4,128,256]{3,2,1,0:T(8,128)(2,1)S(1)}, u32[]{:S(2)}, u32[]{:S(2)}) collective-permute-start(bf16[2,4,128,256]{3,2,1,0:T(8,128)(2,1)S(1)} %slice.3), channel_id=1, source_target_pairs={{1,0},{0,1},{3,2},{2,3},{5,4},{4,5},{7,6},{6,7},{9,8},{8,9},{11,10... | collective-permute-start | bytes 1572872 | tf_op jit(solution)/shard_map/ppermute | solution.py:319
  1.4 20.4 %collective-permute-start.3 = (bf16[4,128,256]{2,1,0:T(8,128)(2,1)S(1)}, bf16[4,128,256]{2,1,0:T(8,128)(2,1)S(1)}, u32[]{:S(2)}, u32[]{:S(2)}) collective-permute-start(bf16[4,128,256]{2,1,0:T(8,128)(2,1)S(1)} %get-tuple-element.33), channel_id=1, source_target_pairs={{0,2},{2,0},{4,6},{6,4},{8,10},{10,8},{12,14},{14,12},{1,3},{3,1},... | collective-permute-start | bytes 786440 | tf_op jit(solution)/shard_map/ppermute | solution.py:310
  3.0 4.7 %copy-start = (bf16[3,3,256,256]{3,2,1,0:T(8,128)(2,1)S(1)}, bf16[3,3,256,256]{3,2,1,0:T(8,128)(2,1)}, u32[]{:S(2)}) copy-start(bf16[3,3,256,256]{3,2,1,0:T(8,128)(2,1)} %k_ref.15) | copy-start | bytes 3538948
  3.0 4.7 %copy-start.4 = (f32[256]{0:T(256)S(1)}, f32[256]{0:T(256)}, u32[]{:S(2)}) copy-start(f32[256]{0:T(256)} %param.10) | copy-start | bytes 3076
  3.0 18.8 %collective-permute-start.4 = (bf16[4,128,256]{2,1,0:T(8,128)(2,1)S(1)}, bf16[4,128,256]{2,1,0:T(8,128)(2,1)S(1)}, u32[]{:S(2)}, u32[]{:S(2)}) collective-permute-start(bf16[4,128,256]{2,1,0:T(8,128)(2,1)S(1)} %get-tuple-element.34), channel_id=1, source_target_pairs={{0,0},{2,4},{4,2},{6,8},{8,6},{10,12},{12,10},{14,14},{1,1},{3,5},... | collective-permute-start | bytes 786440 | tf_op jit(solution)/shard_map/ppermute | solution.py:310
  5.5 1.0 %copy-start.5 = (bf16[3,256,256]{2,1,0:T(8,128)(2,1)S(1)}, bf16[3,256,256]{2,1,0:T(8,128)(2,1)}, u32[]{:S(2)}) copy-start(bf16[3,256,256]{2,1,0:T(8,128)(2,1)} %k_ref.8) | copy-start | bytes 1179652
  9.5 14.5 %collective-permute-start.7 = (bf16[2,2,128,256]{3,2,1,0:T(8,128)(2,1)S(1)}, bf16[2,2,128,256]{3,2,1,0:T(8,128)(2,1)S(1)}, u32[]{:S(2)}, u32[]{:S(2)}) collective-permute-start(bf16[2,2,128,256]{3,2,1,0:T(8,128)(2,1)S(1)} %get-tuple-element.45), channel_id=1, source_target_pairs={{0,1},{1,0},{2,3},{3,2},{4,5},{5,4},{6,7},{7,6},{8,9},{9,8},{10,11... | collective-permute-start | bytes 786440 | tf_op jit(solution)/shard_map/ppermute | solution.py:316
  9.6 18.2 %collective-permute-start.1 = (bf16[4,128,256]{2,1,0:T(8,128)(2,1)S(1)}, bf16[4,128,256]{2,1,0:T(8,128)(2,1)S(1)}, u32[]{:S(2)}, u32[]{:S(2)}) collective-permute-start(bf16[4,128,256]{2,1,0:T(8,128)(2,1)S(1)} %get-tuple-element.36), channel_id=1, source_target_pairs={{0,2},{2,0},{4,6},{6,4},{8,10},{10,8},{12,14},{14,12},{1,3},{3,1},... | collective-permute-start | bytes 786440 | tf_op jit(solution)/shard_map/ppermute | solution.py:310
  9.6 18.2 %collective-permute-start.2 = (bf16[4,128,256]{2,1,0:T(8,128)(2,1)S(1)}, bf16[4,128,256]{2,1,0:T(8,128)(2,1)S(1)}, u32[]{:S(2)}, u32[]{:S(2)}) collective-permute-start(bf16[4,128,256]{2,1,0:T(8,128)(2,1)S(1)} %get-tuple-element.37), channel_id=1, source_target_pairs={{0,0},{2,4},{4,2},{6,8},{8,6},{10,12},{12,10},{14,14},{1,1},{3,5},... | collective-permute-start | bytes 786440 | tf_op jit(solution)/shard_map/ppermute | solution.py:310
  21.9 2.1 %copy-start.3 = (bf16[3,3,256,256]{3,2,1,0:T(8,128)(2,1)S(1)}, bf16[3,3,256,256]{3,2,1,0:T(8,128)(2,1)}, u32[]{:S(2)}) copy-start(bf16[3,3,256,256]{3,2,1,0:T(8,128)(2,1)} %ks_ref.5) | copy-start | bytes 3538948
  21.9 2.1 %copy-start.6 = (bf16[3,256,256]{2,1,0:T(8,128)(2,1)S(1)}, bf16[3,256,256]{2,1,0:T(8,128)(2,1)}, u32[]{:S(2)}) copy-start(bf16[3,256,256]{2,1,0:T(8,128)(2,1)} %k_ref.12) | copy-start | bytes 1179652
  21.9 2.1 %copy-start.7 = (f32[256]{0:T(256)S(1)}, f32[256]{0:T(256)}, u32[]{:S(2)}) copy-start(f32[256]{0:T(256)} %param.11) | copy-start | bytes 3076
  23.4 2.7 %collective-permute-start.5 = (bf16[2,128,256]{2,1,0:T(8,128)(2,1)S(1)}, bf16[2,128,256]{2,1,0:T(8,128)(2,1)S(1)}, u32[]{:S(2)}, u32[]{:S(2)}) collective-permute-start(bf16[2,128,256]{2,1,0:T(8,128)(2,1)S(1)} %get-tuple-element.42), channel_id=1, source_target_pairs={{0,1},{1,0},{2,3},{3,2},{4,5},{5,4},{6,7},{7,6},{8,9},{9,8},{10,11... | collective-permute-start | bytes 393224 | tf_op jit(solution)/shard_map/ppermute | solution.py:316
  23.5 2.6 %collective-permute-start.6 = (bf16[2,128,256]{2,1,0:T(8,128)(2,1)S(1)}, bf16[2,128,256]{2,1,0:T(8,128)(2,1)S(1)}, u32[]{:S(2)}, u32[]{:S(2)}) collective-permute-start(bf16[2,128,256]{2,1,0:T(8,128)(2,1)S(1)} %get-tuple-element.43), channel_id=1, source_target_pairs={{0,1},{1,0},{2,3},{3,2},{4,5},{5,4},{6,7},{7,6},{8,9},{9,8},{10,11... | collective-permute-start | bytes 393224 | tf_op jit(solution)/shard_map/ppermute | solution.py:316
  28.7 1.6 %collective-permute-start.8 = (bf16[2,2,128,256]{3,2,1,0:T(8,128)(2,1)S(1)}, bf16[2,2,128,256]{3,2,1,0:T(8,128)(2,1)S(1)}, u32[]{:S(2)}, u32[]{:S(2)}) collective-permute-start(bf16[2,2,128,256]{3,2,1,0:T(8,128)(2,1)S(1)} %get-tuple-element.53), channel_id=1, source_target_pairs={{1,0},{0,1},{3,2},{2,3},{5,4},{4,5},{7,6},{6,7},{9,8},{8,9},{11,10... | collective-permute-start | bytes 786440 | tf_op jit(solution)/shard_map/ppermute | solution.py:319
  28.8 5.5 %collective-permute-start.11 = (bf16[2,2,128,256]{3,2,1,0:T(8,128)(2,1)S(1)}, bf16[2,2,128,256]{3,2,1,0:T(8,128)(2,1)S(1)}, u32[]{:S(2)}, u32[]{:S(2)}) collective-permute-start(bf16[2,2,128,256]{3,2,1,0:T(8,128)(2,1)S(1)} %get-tuple-element.56), channel_id=1, source_target_pairs={{1,0},{0,1},{3,2},{2,3},{5,4},{4,5},{7,6},{6,7},{9,8},{8,9},{11,10... | collective-permute-start | bytes 786440 | tf_op jit(solution)/shard_map/ppermute | solution.py:319
  31.0 14.0 %collective-permute-start.9 = (bf16[4,128,256]{2,1,0:T(8,128)(2,1)S(1)}, bf16[4,128,256]{2,1,0:T(8,128)(2,1)S(1)}, u32[]{:S(2)}, u32[]{:S(2)}) collective-permute-start(bf16[4,128,256]{2,1,0:T(8,128)(2,1)S(1)} %get-tuple-element.54), channel_id=1, source_target_pairs={{0,2},{2,0},{4,6},{6,4},{8,10},{10,8},{12,14},{14,12},{1,3},{3,1},... | collective-permute-start | bytes 786440 | tf_op jit(solution)/shard_map/ppermute | solution.py:310
  31.1 13.9 %collective-permute-start.10 = (bf16[4,128,256]{2,1,0:T(8,128)(2,1)S(1)}, bf16[4,128,256]{2,1,0:T(8,128)(2,1)S(1)}, u32[]{:S(2)}, u32[]{:S(2)}) collective-permute-start(bf16[4,128,256]{2,1,0:T(8,128)(2,1)S(1)} %get-tuple-element.55), channel_id=1, source_target_pairs={{0,0},{2,4},{4,2},{6,8},{8,6},{10,12},{12,10},{14,14},{1,1},{3,5},... | collective-permute-start | bytes 786440 | tf_op jit(solution)/shard_map/ppermute | solution.py:310

commit v5 on v4

--- a/solution.py
+++ b/solution.py
@@ -100,13 +100,13 @@
     return mixed(*parts, cols)
 
 
-def time_back(padded, kernel_ref):
+def time_back(padded, kernel_ref, starts=True):
     head = (lax.axis_index("tm") == 0).astype(F32)
     weights = jnp.concatenate([kernel_ref[2], kernel_ref[1], kernel_ref[0]], axis=1)
     out = []
     for f in range(len(padded) - 2):
         part = dot_nt(jnp.concatenate(padded[f : f + 3], axis=1), weights)
-        if f == 0:
+        if f == 0 and starts:
             extra = jnp.concatenate([kernel_ref[0], kernel_ref[0], kernel_ref[1]], axis=1)
             part += head * dot_nt(jnp.concatenate([padded[0], padded[1], padded[0]], axis=1), extra)
         out.append(part.astype(BF16))
@@ -213,36 +213,54 @@
         ref[at] = array.reshape(ref.shape[1:])
 
 
-def hidden_own_kernel(s_ref, first_ref, last_ref, d_ref, gain_ref, kt_ref, ks_ref, *o_refs):
+def grad_own_kernel(d_ref, ks_ref, o_ref):
     nrows, _, cols, _ = d_ref.shape
     for at, (rows, taps) in enumerate([((0, 1), (1, 2)), ((nrows - 2, nrows - 1), (0, 1))]):
-        slope, unit = slope_of(hidden_of(at, s_ref, (first_ref, last_ref)[at], kt_ref), gain_ref[...])
         grad = spatial_back([flat(d_ref[r]) for r in rows], taps, ks_ref, cols)
-        store(o_refs, at, (grad, slope, unit))
-
-
-def edges(own_ref, other_ref, k_ref, part_refs):
+        store((o_ref,), at, (grad,))
+
+
+def hidden_own_kernel(s_ref, first_ref, last_ref, gain_ref, kt_ref, *o_refs):
+    for at, early_ref in enumerate((first_ref, last_ref)):
+        store(o_refs, at, slope_of(hidden_of(at, s_ref, early_ref, kt_ref), gain_ref[...]))
+
+
+def edges(own_ref, other_ref, k_ref, part_refs, f0, f1):
     cols = own_ref.shape[1]
-    for at, row in enumerate(neighbours(flat(own_ref[...]), flat(other_ref[...]))):
-        grad, slope, unit = [flat(ref[at]) for ref in part_refs]
+    for at, row in enumerate(neighbours(flat(own_ref[f0:f1]), flat(other_ref[f0:f1]))):
+        grad, slope, unit = [flat(ref[at, f0:f1]) for ref in part_refs]
         yield at, back_of(grad + spatial_back([row], [2 * at], k_ref, cols), slope, unit)
 
 
-def hidden_rim_kernel(own_ref, other_ref, ks_ref, grad_ref, slope_ref, unit_ref, o_ref, head_ref):
-    for at, out in edges(own_ref, other_ref, ks_ref, (grad_ref, slope_ref, unit_ref)):
-        out = out.astype(BF16).reshape(o_ref.shape[1:])
-        o_ref[at] = out
-        head_ref[at] = out[:2]
-
-
-def back_time_kernel(dh_ref, later_ref, k_ref, d_ref, *send_refs):
-    rows, frames, cols, width = dh_ref.shape
-    padded = [flat(dh_ref[:, f]) for f in range(frames)] + [later_of(flat(later_ref[:, f])) for f in range(2)]
+def hidden_rim_kernel(f0, f1, own_ref, other_ref, ks_ref, grad_ref, slope_ref, unit_ref, o_ref):
+    for at, out in edges(own_ref, other_ref, ks_ref, (grad_ref, slope_ref, unit_ref), f0, f1):
+        o_ref[at] = out.astype(BF16).reshape(o_ref.shape[1:])
+
+
+def frames_of(*refs):
+    return [flat(ref[:, f]) for ref in refs for f in range(ref.shape[1])]
+
+
+def back_time_kernel(dh_ref, later_ref, k_ref, d_ref):
+    rows, _, cols, width = dh_ref.shape
+    padded = frames_of(dh_ref) + [later_of(block) for block in frames_of(later_ref)]
     for f, out in enumerate(time_back(padded, k_ref)):
-        out = out.reshape(rows, cols, width)
+        d_ref[:, f] = out.reshape(rows, cols, width)
+
+
+def back_first_kernel(dh_ref, next_ref, k_ref, d_ref):
+    rows, _, cols, width = dh_ref.shape
+    for f, out in enumerate(time_back((frames_of(dh_ref, next_ref))[:4], k_ref)):
+        d_ref[:, f] = out.reshape(rows, cols, width)
+
+
+def back_last_kernel(dh_ref, later_ref, first_ref, k_ref, d_ref, own_ref, other_ref):
+    rows, frames, cols, width = d_ref.shape
+    padded = frames_of(dh_ref) + [later_of(block) for block in frames_of(later_ref)]
+    last = [out.reshape(rows, cols, width) for out in time_back(padded, k_ref, starts=False)]
+    for f, out in enumerate([first_ref[:, f] for f in range(2)] + last):
         d_ref[:, f] = out
-        if send_refs:
-            send_refs[0][f], send_refs[1][f] = to_send(out[0], out[rows - 1])
+        own_ref[f], other_ref[f] = to_send(out[0], out[rows - 1])
 
 
 def lines_of(din_ref, drim_ref):
@@ -279,7 +297,7 @@
 def out_rim_kernel(own_ref, other_ref, k_ref, grad_ref, slope_ref, unit_ref, g_ref, _, o_ref, held, sems):
     nrows = g_ref.shape[1]
     copies = []
-    for at, out in edges(own_ref, other_ref, k_ref, (grad_ref, slope_ref, unit_ref)):
+    for at, out in edges(own_ref, other_ref, k_ref, (grad_ref, slope_ref, unit_ref), 0, g_ref.shape[0]):
         copies.append(put((0, nrows - 1)[at], at, out, g_ref, held, o_ref, sems))
     for copy in copies:
         copy.wait()
@@ -343,9 +361,13 @@
         act_kernel, [shape_of(nrows, *row)] + two(inner), 9 * inner * per_tap,
         frames_in, after(gain_first, d2), spatial_first, name="act",
     )
+    (grad_own,) = call(
+        grad_own_kernel, parts[:1], 12 * per_tap,
+        d2, after(spatial_second, s_in), name="grad_own",
+    )
     s_rim, *s_rim_tails = call(
         act_rim_kernel, [shape_of(2, *row)] + [shape_of(2, cols, width)] * 2, 18 * per_tap,
-        *x_rims, a1, gain_first, spatial_first, name="act_rim",
+        *x_rims, a1, after(gain_first, grad_own), spatial_first, name="act_rim",
     )
     s_rim_early = [to_later(tail) for tail in s_rim_tails]
 
@@ -355,23 +377,30 @@
     )
     dh_in_later = to_earlier(dh_in_head)
     own = call(
-        hidden_own_kernel, parts, 18 * per_tap,
-        s_rim, *s_rim_early, d2, after(gain_second, dh_in), temporal_first, spatial_second, name="hidden_own",
-    )
-    dh_rim, dh_rim_head = call(
-        hidden_rim_kernel, two(2), 6 * per_tap,
-        *d2_rims, spatial_second, *own, name="hidden_rim",
-    )
-
-    def back_time(dh, later, sends, name):
-        return call(
-            back_time_kernel, [shape_of(*dh.shape)] + [shape_of(*row)] * sends, 4 * dh.shape[0] * per_tap,
-            dh, later, temporal_first, name=name,
+        hidden_own_kernel, parts[:2], 6 * per_tap,
+        s_rim, *s_rim_early, after(gain_second, dh_in), temporal_first, name="hidden_own",
+    )
+    dh_rim, gate = [], spatial_second
+    for f0, f1 in [(0, 2), (2, frames)]:
+        dh_rim += call(
+            functools.partial(hidden_rim_kernel, f0, f1), [shape_of(2, f1 - f0, cols, width)], 3 * per_tap,
+            *d2_rims, gate, grad_own, *own, name="hidden_rim",
         )
-
-    d1_rim, *d1_send = back_time(dh_rim, to_earlier(dh_rim_head), 2, "back_time_rim")
+        gate = after(spatial_second, dh_rim[0])
+
+    (first,) = call(
+        back_first_kernel, [shape_of(2, 2, cols, width)], 4 * per_tap,
+        *dh_rim, temporal_first, name="back_first",
+    )
+    d1_rim, *d1_send = call(
+        back_last_kernel, [shape_of(2, *row)] + [shape_of(*row)] * 2, 4 * per_tap,
+        dh_rim[1], to_earlier(dh_rim[0]), first, temporal_first, name="back_last",
+    )
     d1_rims = exchange(*d1_send)
-    (d1_in,) = back_time(dh_in, dh_in_later, 0, "back_time")
+    (d1_in,) = call(
+        back_time_kernel, [shape_of(*dh_in.shape)], 4 * inner * per_tap,
+        dh_in, dh_in_later, temporal_first, name="back_time",
+    )
 
     own = call(
         out_own_kernel, parts, 12 * per_tap,

time: 47 us -> 46.1 us (0.981)
  waiting for transfers between devices: 14.8 us -> 12 us
  starting transfers between devices: 13 us -> 13.8 us
  Pallas kernels: 16.2 us -> 16.9 us
    ppermute x6, waiting for transfers between devices: 13.8 us -> 12 us  [swap(): lax.ppermute(block, 'tile', [(i, route.get(i, i)) for i in range(tiles)])]
    ppermute x3, waiting for transfers between devices: 1.03 us -> 0.01 us  [to_earlier(): lax.ppermute(block, 'tm', [((i + 1) % spans, i) for i in range(spans)])]
    ppermute x6, starting transfers between devices: 11.8 us -> 12.5 us  [swap(): lax.ppermute(block, 'tile', [(i, route.get(i, i)) for i in range(tiles)])]
    pallas_call x12 -> x15, Pallas kernels: 16.2 us -> 16.9 us  [call(): pl.pallas_call(kernel, out_shape=tuple(outs), in_specs=[ANY if i in any_i...]
  transfers between devices with their start and end apart: 12 -> 12, of which waited for: 3 -> 2; matrix products, arithmetic and copies ran while one was open for 0% -> 0% of each run, Pallas kernels for 29% -> 32%
where the time goes in v5:
time: 46.1 us; the launch traced here: 45.5 us
  Pallas kernels  16.9 us (37%)
  starting transfers between devices  13.8 us (30%)
  waiting for transfers between devices  12 us (26%)
  local copies, waits for them, and re-layouts  2.31 us (5%)
    pallas_call x15, Pallas kernels, call(): pl.pallas_call(kernel, out_shape=tuple(outs), in_specs=[ANY if i in any_i...  16.9 us
    ppermute x6, starting transfers between devices, swap(): lax.ppermute(block, 'tile', [(i, route.get(i, i)) for i in range(tiles)])  12.5 us
    ppermute x6, waiting for transfers between devices, swap(): lax.ppermute(block, 'tile', [(i, route.get(i, i)) for i in range(tiles)])  12 us
    slice x1, local copies, waits for them, and re-layouts, on_device(): g_later = to_earlier(grad_out[:2])  1.22 us
    unnamed x16, local copies, waits for them, and re-layouts  1.09 us
  transfers between devices with their start and end apart: 12, of which 2 were waited for; matrix products, arithmetic and copies ran while one was open for 0% of the time, Pallas kernels for 32%

profile of v5, /device:TPU:24, one launch (start us, length us, event | category | flops | bytes accessed | tf_op | source)
XLA Modules:
  0.0 45.5 jit_solution(417497892030790039)
XLA Ops:
  0.0 1.2 %slice.3 = bf16[2,4,128,256]{3,2,1,0:T(8,128)(2,1)S(1)} slice(bf16[4,4,128,256]{3,2,1,0:T(8,128)(2,1)} %g_ref.2), slice={[0:2], [0:4], [0:128], [0:256]} | slice | bytes 1048576 | tf_op jit(solution)/shard_map/slice | solution.py:350
  1.4 1.6 %collective-permute-start.3 = (bf16[4,128,256]{2,1,0:T(8,128)(2,1)S(1)}, bf16[4,128,256]{2,1,0:T(8,128)(2,1)S(1)}, u32[]{:S(2)}, u32[]{:S(2)}) collective-permute-start(bf16[4,128,256]{2,1,0:T(8,128)(2,1)S(1)} %get-tuple-element.33), channel_id=1, source_target_pairs={{0,2},{2,0},{4,6},{6,4},{8,10},{10,8},{12,14},{14,12},{1,3},{3,1},... | collective-permute-start | bytes 786440 | tf_op jit(solution)/shard_map/ppermute | solution.py:328
  3.0 2.4 %collective-permute-start.4 = (bf16[4,128,256]{2,1,0:T(8,128)(2,1)S(1)}, bf16[4,128,256]{2,1,0:T(8,128)(2,1)S(1)}, u32[]{:S(2)}, u32[]{:S(2)}) collective-permute-start(bf16[4,128,256]{2,1,0:T(8,128)(2,1)S(1)} %get-tuple-element.34), channel_id=1, source_target_pairs={{0,0},{2,4},{4,2},{6,8},{8,6},{10,12},{12,10},{14,14},{1,1},{3,5},... | collective-permute-start | bytes 786440 | tf_op jit(solution)/shard_map/ppermute | solution.py:328
  5.5 1.0 %copy-done.6 = bf16[3,256,256]{2,1,0:T(8,128)(2,1)S(1)} copy-done((bf16[3,256,256]{2,1,0:T(8,128)(2,1)S(1)}, bf16[3,256,256]{2,1,0:T(8,128)(2,1)}, u32[]{:S(2)}) %copy-start.6) | copy-done | bytes 393240
  6.5 1.2 %grad_time.1 = (bf16[4,4,128,256]{3,2,1,0:T(8,128)(2,1)S(1)}, bf16[4,128,256]{2,1,0:T(8,128)(2,1)S(1)}, bf16[4,128,256]{2,1,0:T(8,128)(2,1)S(1)}) custom-call(bf16[4,4,128,256]{3,2,1,0:T(8,128)(2,1)S(1)} %copy-done.3, bf16[2,4,128,256]{3,2,1,0:T(8,128)(2,1)S(1)} %collective-permute-done.later_ref, bf16[3,256,256]{2,1,0:T(8,128)(2,1)S(1)} %copy-done.6), custom_call_target="tpu_custom_call" | custom-call | flops 1073741824 | bytes 3538944 | tf_op jit(solution)/shard_map/grad_time/pallas_call | solution.py:23
  7.8 1.7 %act.1 = (bf16[4,4,128,256]{3,2,1,0:T(8,128)(2,1)S(1)}, bf16[2,4,128,256]{3,2,1,0:T(8,128)(2,1)S(1)}, bf16[2,2,128,256]{3,2,1,0:T(8,128)(2,1)S(1)}) custom-call(bf16[4,4,128,256]{3,2,1,0:T(8,128)(2,1)S(1)} %copy-done.2, f32[1,256]{1,0:T(1,128)S(1)} %bitcast.2, bf16[3,3,256,256]{3,2,1,0:T(8,128)(2,1)S(1)} %copy-done.1), custom_call_target="tpu_custom_call" | custom-call | flops 1207959552 | bytes 4064256 | tf_op jit(solution)/shard_map/act/pallas_call | solution.py:23
  9.6 4.4 %collective-permute-start.2 = (bf16[4,128,256]{2,1,0:T(8,128)(2,1)S(1)}, bf16[4,128,256]{2,1,0:T(8,128)(2,1)S(1)}, u32[]{:S(2)}, u32[]{:S(2)}) collective-permute-start(bf16[4,128,256]{2,1,0:T(8,128)(2,1)S(1)} %get-tuple-element.37), channel_id=1, source_target_pairs={{0,0},{2,4},{4,2},{6,8},{8,6},{10,12},{12,10},{14,14},{1,1},{3,5},... | collective-permute-start | bytes 786440 | tf_op jit(solution)/shard_map/ppermute | solution.py:328
  14.1 1.0 %grad_own.1.grad_ref = f32[2,4,128,256]{3,2,1,0:T(8,128)S(1)} custom-call(bf16[4,4,128,256]{3,2,1,0:T(8,128)(2,1)S(1)} %get-tuple-element.38.d_ref, bf16[3,3,256,256]{3,2,1,0:T(8,128)(2,1)S(1)} %copy-done), custom_call_target="tpu_custom_call" | custom-call | flops 805306368 | bytes 3276800 | tf_op jit(solution)/shard_map/grad_own/pallas_call | solution.py:23
  15.1 6.8 %collective-permute-done.3.own_ref = bf16[4,128,256]{2,1,0:T(8,128)(2,1)S(1)} collective-permute-done((bf16[4,128,256]{2,1,0:T(8,128)(2,1)S(1)}, bf16[4,128,256]{2,1,0:T(8,128)(2,1)S(1)}, u32[]{:S(2)}, u32[]{:S(2)}) %collective-permute-start.3) | collective-permute-done | bytes 262176 | tf_op jit(solution)/shard_map/ppermute | solution.py:328
  21.9 1.5 %act_rim.1 = (bf16[2,4,128,256]{3,2,1,0:T(8,128)(2,1)S(1)}, bf16[2,128,256]{2,1,0:T(8,128)(2,1)S(1)}, bf16[2,128,256]{2,1,0:T(8,128)(2,1)S(1)}) custom-call(bf16[4,128,256]{2,1,0:T(8,128)(2,1)S(1)} %collective-permute-done.3.own_ref, bf16[4,128,256]{2,1,0:T(8,128)(2,1)S(1)} %collective-permute-done.4.other_ref, ...), custom_call_target="tpu_custom_call" | custom-call | flops 1207959552 | bytes 3539968 | tf_op jit(solution)/shard_map/act_rim/pallas_call | solution.py:23
  23.5 0.5 %collective-permute-start.6 = (bf16[2,128,256]{2,1,0:T(8,128)(2,1)S(1)}, bf16[2,128,256]{2,1,0:T(8,128)(2,1)S(1)}, u32[]{:S(2)}, u32[]{:S(2)}) collective-permute-start(bf16[2,128,256]{2,1,0:T(8,128)(2,1)S(1)} %get-tuple-element.46), channel_id=1, source_target_pairs={{0,1},{1,0},{2,3},{3,2},{4,5},{5,4},{6,7},{7,6},{8,9},{9,8},{10,11... | collective-permute-start | bytes 393224 | tf_op jit(solution)/shard_map/ppermute | solution.py:334
  24.0 2.0 %hidden.1 = (bf16[2,4,128,256]{3,2,1,0:T(8,128)(2,1)S(1)}, bf16[2,2,128,256]{3,2,1,0:T(8,128)(2,1)S(1)}) custom-call(bf16[2,4,128,256]{3,2,1,0:T(8,128)(2,1)S(1)} %get-tuple-element.40.s_ref, bf16[2,2,128,256]{3,2,1,0:T(8,128)(2,1)S(1)} %collective-permute-done.7.early_ref, bf16[4,4,128,256]{3,2,1,0:T(8,128)(2,1)S(1)} %get-tuple-element.38.d_ref, ...), custom_call_target="tpu_custom_call" | custom-call | flops 1610612736 | bytes 4195328 | tf_op jit(solution)/shard_map/hidden/pallas_call | solution.py:23
  26.1 1.0 %hidden_own.1 = (f32[2,4,128,256]{3,2,1,0:T(8,128)S(1)}, f32[2,4,128,256]{3,2,1,0:T(8,128)S(1)}) custom-call(bf16[2,4,128,256]{3,2,1,0:T(8,128)(2,1)S(1)} %get-tuple-element.44.s_ref, bf16[2,128,256]{2,1,0:T(8,128)(2,1)S(1)} %collective-permute-done.5.first_ref, bf16[2,128,256]{2,1,0:T(8,128)(2,1)S(1)} %collective-permute-done.6.last_ref, ...), custom_call_target="tpu_custom_call" | custom-call | flops 402653184 | bytes 3277824 | tf_op jit(solution)/shard_map/hidden_own/pallas_call | solution.py:23
  27.1 0.5 %hidden_rim.2.dh_ref = bf16[2,2,128,256]{3,2,1,0:T(8,128)(2,1)S(1)} custom-call(bf16[4,128,256]{2,1,0:T(8,128)(2,1)S(1)} %collective-permute-done.1.own_ref, bf16[4,128,256]{2,1,0:T(8,128)(2,1)S(1)} %collective-permute-done.2.other_ref, bf16[3,3,256,256]{3,2,1,0:T(8,128)(2,1)S(1)} %copy-done, f32[2,4,128,256]{3,2,1,0:T(8,128)S(1)} %grad_own.1.grad_ref, ...), custom_call_target="tpu_custom_call" | custom-call | flops 201326592 | bytes 5111808 | tf_op jit(solution)/shard_map/hidden_rim/pallas_call | solution.py:23
  27.8 0.4 collective-permute-start.11
  28.2 0.5 %hidden_rim.3.next_ref.dh_ref = bf16[2,2,128,256]{3,2,1,0:T(8,128)(2,1)S(1)} custom-call(bf16[4,128,256]{2,1,0:T(8,128)(2,1)S(1)} %collective-permute-done.1.own_ref, bf16[4,128,256]{2,1,0:T(8,128)(2,1)S(1)} %collective-permute-done.2.other_ref, bf16[3,3,256,256]{3,2,1,0:T(8,128)(2,1)S(1)} %copy-done, f32[2,4,128,256]{3,2,1,0:T(8,128)S(1)} %grad_own.1.grad_ref, ...), custom_call_target="tpu_custom_call" | custom-call | flops 201326592 | bytes 5111808 | tf_op jit(solution)/shard_map/hidden_rim/pallas_call | solution.py:23
  28.8 0.5 %back_first.1.first_ref = bf16[2,2,128,256]{3,2,1,0:T(8,128)(2,1)S(1)} custom-call(bf16[2,2,128,256]{3,2,1,0:T(8,128)(2,1)S(1)} %hidden_rim.2.dh_ref, bf16[2,2,128,256]{3,2,1,0:T(8,128)(2,1)S(1)} %hidden_rim.3.next_ref.dh_ref, bf16[3,256,256]{2,1,0:T(8,128)(2,1)S(1)} %copy-done.4), custom_call_target="tpu_custom_call" | custom-call | flops 268435456 | bytes 1179648 | tf_op jit(solution)/shard_map/back_first/pallas_call | solution.py:23
  29.3 0.4 back_last.1
  29.8 3.9 %collective-permute-start.10 = (bf16[4,128,256]{2,1,0:T(8,128)(2,1)S(1)}, bf16[4,128,256]{2,1,0:T(8,128)(2,1)S(1)}, u32[]{:S(2)}, u32[]{:S(2)}) collective-permute-start(bf16[4,128,256]{2,1,0:T(8,128)(2,1)S(1)} %get-tuple-element.55), channel_id=1, source_target_pairs={{0,0},{2,4},{4,2},{6,8},{8,6},{10,12},{12,10},{14,14},{1,1},{3,5},... | collective-permute-start | bytes 786440 | tf_op jit(solution)/shard_map/ppermute | solution.py:328
  33.7 0.7 %back_time.1.din_ref = bf16[2,4,128,256]{3,2,1,0:T(8,128)(2,1)S(1)} custom-call(bf16[2,4,128,256]{3,2,1,0:T(8,128)(2,1)S(1)} %get-tuple-element.49.dh_ref, bf16[2,2,128,256]{3,2,1,0:T(8,128)(2,1)S(1)} %collective-permute-done.11.later_ref, bf16[3,256,256]{2,1,0:T(8,128)(2,1)S(1)} %copy-done.4), custom_call_target="tpu_custom_call" | custom-call | flops 536870912 | bytes 1703936 | tf_op jit(solution)/shard_map/back_time/pallas_call | solution.py:23
  34.4 1.4 %out_own.1 = (f32[2,4,128,256]{3,2,1,0:T(8,128)S(1)}, f32[2,4,128,256]{3,2,1,0:T(8,128)S(1)}, f32[2,4,128,256]{3,2,1,0:T(8,128)S(1)}) custom-call(bf16[4,4,128,256]{3,2,1,0:T(8,128)(2,1)S(1)} %copy-done.2, bf16[2,4,128,256]{3,2,1,0:T(8,128)(2,1)S(1)} %back_time.1.din_ref, bf16[2,4,128,256]{3,2,1,0:T(8,128)(2,1)S(1)} %get-tuple-element.57.drim_ref, ...), custom_call_target="tpu_custom_call" | custom-call | flops 805306368 | bytes 6423552 | tf_op jit(solution)/shard_map/out_own/pallas_call | solution.py:23
  35.8 2.6 %out.1._ = bf16[4,4,128,256]{3,2,1,0:T(8,128)(2,1)} custom-call(bf16[4,4,128,256]{3,2,1,0:T(8,128)(2,1)S(1)} %copy-done.2, bf16[4,4,128,256]{3,2,1,0:T(8,128)(2,1)S(1)} %copy-done.3, bf16[2,4,128,256]{3,2,1,0:T(8,128)(2,1)S(1)} %back_time.1.din_ref, bf16[2,4,128,256]{3,2,1,0:T(8,128)(2,1)S(1)} %get-tuple-element.57.drim_ref, f32[1,256]{1,0:T(1,128)S(1)} %bitcast.5, ...), custom_call_target="tpu_custom_call" | custom-call | flops 1207959552 | bytes 5374976 | tf_op jit(solution)/shard_map/out/pallas_call | solution.py:23
  38.4 5.3 %collective-permute-done.9.own_ref = bf16[4,128,256]{2,1,0:T(8,128)(2,1)S(1)} collective-permute-done((bf16[4,128,256]{2,1,0:T(8,128)(2,1)S(1)}, bf16[4,128,256]{2,1,0:T(8,128)(2,1)S(1)}, u32[]{:S(2)}, u32[]{:S(2)}) %collective-permute-start.9) | collective-permute-done | bytes 262176 | tf_op jit(solution)/shard_map/ppermute | solution.py:328
  43.7 1.6 %out_rim.1 = bf16[4,4,128,256]{3,2,1,0:T(8,128)(2,1)} custom-call(bf16[4,128,256]{2,1,0:T(8,128)(2,1)S(1)} %collective-permute-done.9.own_ref, bf16[4,128,256]{2,1,0:T(8,128)(2,1)S(1)} %collective-permute-done.10.other_ref, bf16[3,3,256,256]{3,2,1,0:T(8,128)(2,1)S(1)} %copy-done.1, ...), custom_call_target="tpu_custom_call", output_to_operand_aliasing={{}: (7, {})} | custom-call | flops 402653184 | bytes 7995392 | tf_op jit(solution)/shard_map/out_rim/pallas_call | solution.py:23
  (32 shorter events, 0.7 us)
Async XLA Ops:
  0.0 1.4 %copy-start.2 = (bf16[4,4,128,256]{3,2,1,0:T(8,128)(2,1)S(1)}, bf16[4,4,128,256]{3,2,1,0:T(8,128)(2,1)}, u32[]{:S(2)}) copy-start(bf16[4,4,128,256]{3,2,1,0:T(8,128)(2,1)} %x_ref.7) | copy-start | bytes 3145732
  0.0 5.5 %copy-start.3 = (bf16[4,4,128,256]{3,2,1,0:T(8,128)(2,1)S(1)}, bf16[4,4,128,256]{3,2,1,0:T(8,128)(2,1)}, u32[]{:S(2)}) copy-start(bf16[4,4,128,256]{3,2,1,0:T(8,128)(2,1)} %g_ref.2) | copy-start | bytes 3145732
  1.2 4.2 %collective-permute-start = (bf16[2,4,128,256]{3,2,1,0:T(8,128)(2,1)S(1)}, bf16[2,4,128,256]{3,2,1,0:T(8,128)(2,1)S(1)}, u32[]{:S(2)}, u32[]{:S(2)}) collective-permute-start(bf16[2,4,128,256]{3,2,1,0:T(8,128)(2,1)S(1)} %slice.3), channel_id=1, source_target_pairs={{1,0},{0,1},{3,2},{2,3},{5,4},{4,5},{7,6},{6,7},{9,8},{8,9},{11,10... | collective-permute-start | bytes 1572872 | tf_op jit(solution)/shard_map/ppermute | solution.py:337
  1.4 20.4 %collective-permute-start.3 = (bf16[4,128,256]{2,1,0:T(8,128)(2,1)S(1)}, bf16[4,128,256]{2,1,0:T(8,128)(2,1)S(1)}, u32[]{:S(2)}, u32[]{:S(2)}) collective-permute-start(bf16[4,128,256]{2,1,0:T(8,128)(2,1)S(1)} %get-tuple-element.33), channel_id=1, source_target_pairs={{0,2},{2,0},{4,6},{6,4},{8,10},{10,8},{12,14},{14,12},{1,3},{3,1},... | collective-permute-start | bytes 786440 | tf_op jit(solution)/shard_map/ppermute | solution.py:328
  3.0 4.7 %copy-start.1 = (bf16[3,3,256,256]{3,2,1,0:T(8,128)(2,1)S(1)}, bf16[3,3,256,256]{3,2,1,0:T(8,128)(2,1)}, u32[]{:S(2)}) copy-start(bf16[3,3,256,256]{3,2,1,0:T(8,128)(2,1)} %k_ref.17) | copy-start | bytes 3538948
  3.0 4.7 %copy-start.5 = (f32[256]{0:T(256)S(1)}, f32[256]{0:T(256)}, u32[]{:S(2)}) copy-start(f32[256]{0:T(256)} %param.10) | copy-start | bytes 3076
  3.0 18.8 %collective-permute-start.4 = (bf16[4,128,256]{2,1,0:T(8,128)(2,1)S(1)}, bf16[4,128,256]{2,1,0:T(8,128)(2,1)S(1)}, u32[]{:S(2)}, u32[]{:S(2)}) collective-permute-start(bf16[4,128,256]{2,1,0:T(8,128)(2,1)S(1)} %get-tuple-element.34), channel_id=1, source_target_pairs={{0,0},{2,4},{4,2},{6,8},{8,6},{10,12},{12,10},{14,14},{1,1},{3,5},... | collective-permute-start | bytes 786440 | tf_op jit(solution)/shard_map/ppermute | solution.py:328
  5.5 1.0 %copy-start.6 = (bf16[3,256,256]{2,1,0:T(8,128)(2,1)S(1)}, bf16[3,256,256]{2,1,0:T(8,128)(2,1)}, u32[]{:S(2)}) copy-start(bf16[3,256,256]{2,1,0:T(8,128)(2,1)} %k_ref.9) | copy-start | bytes 1179652
  7.7 6.3 %copy-start = (bf16[3,3,256,256]{3,2,1,0:T(8,128)(2,1)S(1)}, bf16[3,3,256,256]{3,2,1,0:T(8,128)(2,1)}, u32[]{:S(2)}) copy-start(bf16[3,3,256,256]{3,2,1,0:T(8,128)(2,1)} %ks_ref.5) | copy-start | bytes 3538948
  9.5 14.5 %collective-permute-start.7 = (bf16[2,2,128,256]{3,2,1,0:T(8,128)(2,1)S(1)}, bf16[2,2,128,256]{3,2,1,0:T(8,128)(2,1)S(1)}, u32[]{:S(2)}, u32[]{:S(2)}) collective-permute-start(bf16[2,2,128,256]{3,2,1,0:T(8,128)(2,1)S(1)} %get-tuple-element.47), channel_id=1, source_target_pairs={{0,1},{1,0},{2,3},{3,2},{4,5},{5,4},{6,7},{7,6},{8,9},{9,8},{10,11... | collective-permute-start | bytes 786440 | tf_op jit(solution)/shard_map/ppermute | solution.py:334
  9.6 17.5 %collective-permute-start.1 = (bf16[4,128,256]{2,1,0:T(8,128)(2,1)S(1)}, bf16[4,128,256]{2,1,0:T(8,128)(2,1)S(1)}, u32[]{:S(2)}, u32[]{:S(2)}) collective-permute-start(bf16[4,128,256]{2,1,0:T(8,128)(2,1)S(1)} %get-tuple-element.36), channel_id=1, source_target_pairs={{0,2},{2,0},{4,6},{6,4},{8,10},{10,8},{12,14},{14,12},{1,3},{3,1},... | collective-permute-start | bytes 786440 | tf_op jit(solution)/shard_map/ppermute | solution.py:328
  9.6 17.5 %collective-permute-start.2 = (bf16[4,128,256]{2,1,0:T(8,128)(2,1)S(1)}, bf16[4,128,256]{2,1,0:T(8,128)(2,1)S(1)}, u32[]{:S(2)}, u32[]{:S(2)}) collective-permute-start(bf16[4,128,256]{2,1,0:T(8,128)(2,1)S(1)} %get-tuple-element.37), channel_id=1, source_target_pairs={{0,0},{2,4},{4,2},{6,8},{8,6},{10,12},{12,10},{14,14},{1,1},{3,5},... | collective-permute-start | bytes 786440 | tf_op jit(solution)/shard_map/ppermute | solution.py:328
  21.9 2.1 %copy-start.4 = (bf16[3,256,256]{2,1,0:T(8,128)(2,1)S(1)}, bf16[3,256,256]{2,1,0:T(8,128)(2,1)}, u32[]{:S(2)}) copy-start(bf16[3,256,256]{2,1,0:T(8,128)(2,1)} %k_ref.14) | copy-start | bytes 1179652
  21.9 2.1 %copy-start.7 = (f32[256]{0:T(256)S(1)}, f32[256]{0:T(256)}, u32[]{:S(2)}) copy-start(f32[256]{0:T(256)} %param.11) | copy-start | bytes 3076
  23.4 2.6 %collective-permute-start.5 = (bf16[2,128,256]{2,1,0:T(8,128)(2,1)S(1)}, bf16[2,128,256]{2,1,0:T(8,128)(2,1)S(1)}, u32[]{:S(2)}, u32[]{:S(2)}) collective-permute-start(bf16[2,128,256]{2,1,0:T(8,128)(2,1)S(1)} %get-tuple-element.45), channel_id=1, source_target_pairs={{0,1},{1,0},{2,3},{3,2},{4,5},{5,4},{6,7},{7,6},{8,9},{9,8},{10,11... | collective-permute-start | bytes 393224 | tf_op jit(solution)/shard_map/ppermute | solution.py:334
  23.5 2.6 %collective-permute-start.6 = (bf16[2,128,256]{2,1,0:T(8,128)(2,1)S(1)}, bf16[2,128,256]{2,1,0:T(8,128)(2,1)S(1)}, u32[]{:S(2)}, u32[]{:S(2)}) collective-permute-start(bf16[2,128,256]{2,1,0:T(8,128)(2,1)S(1)} %get-tuple-element.46), channel_id=1, source_target_pairs={{0,1},{1,0},{2,3},{3,2},{4,5},{5,4},{6,7},{7,6},{8,9},{9,8},{10,11... | collective-permute-start | bytes 393224 | tf_op jit(solution)/shard_map/ppermute | solution.py:334
  27.7 1.6 %collective-permute-start.8 = (bf16[2,2,128,256]{3,2,1,0:T(8,128)(2,1)S(1)}, bf16[2,2,128,256]{3,2,1,0:T(8,128)(2,1)S(1)}, u32[]{:S(2)}, u32[]{:S(2)}) collective-permute-start(bf16[2,2,128,256]{3,2,1,0:T(8,128)(2,1)S(1)} %hidden_rim.2.dh_ref), channel_id=1, source_target_pairs={{1,0},{0,1},{3,2},{2,3},{5,4},{4,5},{7,6},{6,7},{9,8},{8,9},{11,10... | collective-permute-start | bytes 786440 | tf_op jit(solution)/shard_map/ppermute | solution.py:337
  27.8 5.9 %collective-permute-start.11 = (bf16[2,2,128,256]{3,2,1,0:T(8,128)(2,1)S(1)}, bf16[2,2,128,256]{3,2,1,0:T(8,128)(2,1)S(1)}, u32[]{:S(2)}, u32[]{:S(2)}) collective-permute-start(bf16[2,2,128,256]{3,2,1,0:T(8,128)(2,1)S(1)} %get-tuple-element.56), channel_id=1, source_target_pairs={{1,0},{0,1},{3,2},{2,3},{5,4},{4,5},{7,6},{6,7},{9,8},{8,9},{11,10... | collective-permute-start | bytes 786440 | tf_op jit(solution)/shard_map/ppermute | solution.py:337
  29.7 14.0 %collective-permute-start.9 = (bf16[4,128,256]{2,1,0:T(8,128)(2,1)S(1)}, bf16[4,128,256]{2,1,0:T(8,128)(2,1)S(1)}, u32[]{:S(2)}, u32[]{:S(2)}) collective-permute-start(bf16[4,128,256]{2,1,0:T(8,128)(2,1)S(1)} %get-tuple-element.54), channel_id=1, source_target_pairs={{0,2},{2,0},{4,6},{6,4},{8,10},{10,8},{12,14},{14,12},{1,3},{3,1},... | collective-permute-start | bytes 786440 | tf_op jit(solution)/shard_map/ppermute | solution.py:328
  29.8 13.9 %collective-permute-start.10 = (bf16[4,128,256]{2,1,0:T(8,128)(2,1)S(1)}, bf16[4,128,256]{2,1,0:T(8,128)(2,1)S(1)}, u32[]{:S(2)}, u32[]{:S(2)}) collective-permute-start(bf16[4,128,256]{2,1,0:T(8,128)(2,1)S(1)} %get-tuple-element.55), channel_id=1, source_target_pairs={{0,0},{2,4},{4,2},{6,8},{8,6},{10,12},{12,10},{14,14},{1,1},{3,5},... | collective-permute-start | bytes 786440 | tf_op jit(solution)/shard_map/ppermute | solution.py:328

commit v6 on v5

--- a/solution.py
+++ b/solution.py
@@ -8,6 +8,7 @@
 from jax.sharding import PartitionSpec as P
 
 EPS = 1e-06
+PAD = 16
 F32 = jnp.float32
 BF16 = jnp.bfloat16
 VMEM = pl.BlockSpec(memory_space=pltpu.VMEM)
@@ -28,7 +29,7 @@
         scratch_shapes=scratch,
         input_output_aliases=aliases or {},
         compiler_params=pltpu.CompilerParams(vmem_limit_bytes=vmem * 2**20),
-        cost_estimate=pl.CostEstimate(flops=flops, bytes_accessed=moved, transcendentals=0),
+        cost_estimate=pl.CostEstimate(flops=flops, bytes_accessed=moved if flops else 0, transcendentals=0),
         name=name,
     )(*args)
 
@@ -100,17 +101,37 @@
     return mixed(*parts, cols)
 
 
+def one_tap(row, di, kernel_ref, cols):
+    rows = row.shape[0]
+    wide = row.astype(F32)
+    at = lax.rem(lax.broadcasted_iota(jnp.int32, (rows, 1), 0), cols)
+    before = jnp.where(at == 0, 0.0, pltpu.roll(wide, 1, 0)).astype(BF16)
+    after_it = jnp.where(at == cols - 1, 0.0, pltpu.roll(wide, rows - 1, 0)).astype(BF16)
+    weights = jnp.concatenate([kernel_ref[2 - di, 2 - dj] for dj in range(3)], axis=1)
+    return dot_nt(jnp.concatenate([before, row, after_it], axis=1), weights)
+
+
+def one_tap(row, di, kernel_ref, cols):
+    rows = row.shape[0]
+    wide = row.astype(F32)
+    at = lax.rem(lax.broadcasted_iota(jnp.int32, (rows, 1), 0), cols)
+    before = jnp.where(at == 0, 0.0, pltpu.roll(wide, 1, 0)).astype(BF16)
+    after_it = jnp.where(at == cols - 1, 0.0, pltpu.roll(wide, rows - 1, 0)).astype(BF16)
+    weights = jnp.concatenate([kernel_ref[2 - di, 2 - dj] for dj in range(3)], axis=1)
+    return dot_nt(jnp.concatenate([before, row, after_it], axis=1), weights)
+
+
 def time_back(padded, kernel_ref, starts=True):
     head = (lax.axis_index("tm") == 0).astype(F32)
     weights = jnp.concatenate([kernel_ref[2], kernel_ref[1], kernel_ref[0]], axis=1)
-    out = []
-    for f in range(len(padded) - 2):
-        part = dot_nt(jnp.concatenate(padded[f : f + 3], axis=1), weights)
-        if f == 0 and starts:
-            extra = jnp.concatenate([kernel_ref[0], kernel_ref[0], kernel_ref[1]], axis=1)
-            part += head * dot_nt(jnp.concatenate([padded[0], padded[1], padded[0]], axis=1), extra)
-        out.append(part.astype(BF16))
-    return out
+    count, rows = len(padded) - 2, padded[0].shape[0]
+    lhs = jnp.concatenate([jnp.concatenate(padded[k : k + count], axis=0) for k in range(3)], axis=1)
+    every = dot_nt(lhs, weights)
+    out = [every[f * rows : (f + 1) * rows] for f in range(count)]
+    if starts:
+        extra = jnp.concatenate([kernel_ref[0], kernel_ref[0], kernel_ref[1]], axis=1)
+        out[0] += head * dot_nt(jnp.concatenate([padded[0], padded[1], padded[0]], axis=1), extra)
+    return [part.astype(BF16) for part in out]
 
 
 def later_of(block):
@@ -229,7 +250,7 @@
     cols = own_ref.shape[1]
     for at, row in enumerate(neighbours(flat(own_ref[f0:f1]), flat(other_ref[f0:f1]))):
         grad, slope, unit = [flat(ref[at, f0:f1]) for ref in part_refs]
-        yield at, back_of(grad + spatial_back([row], [2 * at], k_ref, cols), slope, unit)
+        yield at, back_of(grad + one_tap(row, 2 * at, k_ref, cols), slope, unit)
 
 
 def hidden_rim_kernel(f0, f1, own_ref, other_ref, ks_ref, grad_ref, slope_ref, unit_ref, o_ref):
@@ -260,15 +281,15 @@
     last = [out.reshape(rows, cols, width) for out in time_back(padded, k_ref, starts=False)]
     for f, out in enumerate([first_ref[:, f] for f in range(2)] + last):
         d_ref[:, f] = out
-        own_ref[f], other_ref[f] = to_send(out[0], out[rows - 1])
+        own_ref[pl.ds(f * cols, cols)], other_ref[f] = to_send(out[0], out[rows - 1])
 
 
 def lines_of(din_ref, drim_ref):
     return [flat(drim_ref[0])] + [flat(din_ref[r]) for r in range(din_ref.shape[0])] + [flat(drim_ref[1])]
 
 
-def put(r, at, out, g_ref, held, o_ref, sems):
-    held[at] = (flat(g_ref[:, r]).astype(F32) + out).astype(BF16).reshape(held.shape[1:])
+def put(r, at, out, passed, held, o_ref, sems):
+    held[at] = (flat(passed).astype(F32) + out).astype(BF16).reshape(held.shape[1:])
     copy = pltpu.make_async_copy(held.at[at], o_ref.at[:, r], sems.at[at])
     copy.start()
     return copy
@@ -281,26 +302,31 @@
     for r in range(1, nrows - 1):
         grad = spatial_back(lines[r - 1 : r + 2], [0, 1, 2], k_ref, cols)
         out = back_of(grad, *slope_of(flat(x_ref[:, r]).astype(F32), gain_ref[...]))
-        copies.append(put(r, r - 1, out, g_ref, held, o_ref, sems))
+        copies.append(put(r, r - 1, out, g_ref[:, r], held, o_ref, sems))
     for copy in copies:
         copy.wait()
 
 
-def out_own_kernel(x_ref, din_ref, drim_ref, gain_ref, k_ref, *o_refs):
+def out_own_kernel(x_ref, g_ref, din_ref, drim_ref, gain_ref, k_ref, passed_ref, *o_refs):
     _, nrows, cols, _ = x_ref.shape
     lines = lines_of(din_ref, drim_ref)
     for at, (r, rows, taps) in enumerate([(0, lines[:2], (1, 2)), (nrows - 1, lines[-2:], (0, 1))]):
         slope, unit = slope_of(flat(x_ref[:, r]).astype(F32), gain_ref[...])
         store(o_refs, at, (spatial_back(rows, taps, k_ref, cols), slope, unit))
-
-
-def out_rim_kernel(own_ref, other_ref, k_ref, grad_ref, slope_ref, unit_ref, g_ref, _, o_ref, held, sems):
-    nrows = g_ref.shape[1]
-    copies = []
-    for at, out in edges(own_ref, other_ref, k_ref, (grad_ref, slope_ref, unit_ref), 0, g_ref.shape[0]):
-        copies.append(put((0, nrows - 1)[at], at, out, g_ref, held, o_ref, sems))
-    for copy in copies:
-        copy.wait()
+        passed_ref[at] = g_ref[:, r]
+
+
+def out_rim_kernel(own, halo_ref, k_ref, passed_ref, grad_ref, slope_ref, unit_ref, _, o_ref, held, sems):
+    nrows, cols = o_ref.shape[1:3]
+    tile = lax.axis_index("tile")
+    odd = lax.rem(tile, 2)
+    at = 1 - odd if own else odd
+    missing = tile == at * (lax.axis_size("tile") - 1)
+    row = halo_ref[: grad_ref.shape[1] * cols] if own else flat(halo_ref[...])
+    row = jnp.where(missing, jnp.zeros_like(row), row)
+    grad, slope, unit = [flat(ref[at]) for ref in (grad_ref, slope_ref, unit_ref)]
+    out = back_of(grad + one_tap(row, 2 * at, k_ref, cols), slope, unit)
+    put(at * (nrows - 1), 0, out, passed_ref[at], held, o_ref, sems).wait()
 
 
 def after(value, *earlier):
@@ -393,7 +419,7 @@
         *dh_rim, temporal_first, name="back_first",
     )
     d1_rim, *d1_send = call(
-        back_last_kernel, [shape_of(2, *row)] + [shape_of(*row)] * 2, 4 * per_tap,
+        back_last_kernel, [shape_of(2, *row), shape_of(frames * cols + PAD, width), shape_of(*row)], 4 * per_tap,
         dh_rim[1], to_earlier(dh_rim[0]), first, temporal_first, name="back_last",
     )
     d1_rims = exchange(*d1_send)
@@ -403,19 +429,21 @@
     )
 
     own = call(
-        out_own_kernel, parts, 12 * per_tap,
-        frames_in, d1_in, d1_rim, gain_first, spatial_first, name="out_own",
+        out_own_kernel, [shape_of(2, *row)] + parts, 12 * per_tap,
+        frames_in, grads, d1_in, d1_rim, gain_first, spatial_first, name="out_own",
     )
     (out,) = call(
         out_kernel, [shape_of(*frames_in.shape)], 9 * inner * per_tap,
         frames_in, grads, d1_in, d1_rim, gain_first, spatial_first,
         any_out=(0,), scratch=held(inner), name="out",
     )
-    return call(
-        out_rim_kernel, [shape_of(*frames_in.shape)], 6 * per_tap,
-        *d1_rims, spatial_first, *own, grads, out,
-        any_in=(7,), any_out=(0,), aliases={7: 0}, scratch=held(2), name="out_rim",
-    )[0]
+    for own_side, halo in ((False, d1_rims[1]), (True, d1_rims[0])):
+        (out,) = call(
+            functools.partial(out_rim_kernel, own_side), [shape_of(*frames_in.shape)], 0,
+            halo, spatial_first, *own, out,
+            any_in=(6,), any_out=(0,), aliases={6: 0}, scratch=held(1), name="out_rim",
+        )
+    return out
 
 
 def solution(mesh):

time: 46.1 us -> 45.9 us (level)
  waiting for transfers between devices: 12 us -> 10.9 us
  Pallas kernels: 16.9 us -> 17.9 us
    ppermute x6, waiting for transfers between devices: 12 us -> 10.8 us  [swap(): lax.ppermute(block, 'tile', [(i, route.get(i, i)) for i in range(tiles)])]
    pallas_call x15 -> x16, Pallas kernels: 16.9 us -> 17.9 us  [call(): pl.pallas_call(kernel, out_shape=tuple(outs), in_specs=[ANY if i in any_i...]
  transfers between devices with their start and end apart: 12 -> 12, of which waited for: 2 -> 3; matrix products, arithmetic and copies ran while one was open for 0% -> 0% of each run, Pallas kernels for 32% -> 36%
where the time goes in v6:
time: 45.9 us; the launch traced here: 45.2 us
  Pallas kernels  17.9 us (39%)
  starting transfers between devices  13.8 us (30%)
  waiting for transfers between devices  10.9 us (24%)
  local copies, waits for them, and re-layouts  2.31 us (5%)
    pallas_call x16, Pallas kernels, call(): pl.pallas_call(kernel, out_shape=tuple(outs), in_specs=[ANY if i in any_i...  17.9 us
    ppermute x6, starting transfers between devices, swap(): lax.ppermute(block, 'tile', [(i, route.get(i, i)) for i in range(tiles)])  12.5 us
    ppermute x6, waiting for transfers between devices, swap(): lax.ppermute(block, 'tile', [(i, route.get(i, i)) for i in range(tiles)])  10.8 us
    slice x1, local copies, waits for them, and re-layouts, on_device(): g_later = to_earlier(grad_out[:2])  1.22 us
    unnamed x16, local copies, waits for them, and re-layouts  1.09 us
  transfers between devices with their start and end apart: 12, of which 3 were waited for; matrix products, arithmetic and copies ran while one was open for 0% of the time, Pallas kernels for 36%

profile of v6, /device:TPU:24, one launch (start us, length us, event | category | flops | bytes accessed | tf_op | source)
XLA Modules:
  0.0 45.2 jit_solution(15072775905793702121)
XLA Ops:
  0.0 1.2 %slice.3 = bf16[2,4,128,256]{3,2,1,0:T(8,128)(2,1)S(1)} slice(bf16[4,4,128,256]{3,2,1,0:T(8,128)(2,1)} %g_ref.2), slice={[0:2], [0:4], [0:128], [0:256]} | slice | bytes 1048576 | tf_op jit(solution)/shard_map/slice | solution.py:376
  1.4 1.6 %collective-permute-start.3 = (bf16[4,128,256]{2,1,0:T(8,128)(2,1)S(1)}, bf16[4,128,256]{2,1,0:T(8,128)(2,1)S(1)}, u32[]{:S(2)}, u32[]{:S(2)}) collective-permute-start(bf16[4,128,256]{2,1,0:T(8,128)(2,1)S(1)} %get-tuple-element.34), channel_id=1, source_target_pairs={{0,2},{2,0},{4,6},{6,4},{8,10},{10,8},{12,14},{14,12},{1,3},{3,1},... | collective-permute-start | bytes 786440 | tf_op jit(solution)/shard_map/ppermute | solution.py:354
  3.0 2.4 %collective-permute-start.4 = (bf16[4,128,256]{2,1,0:T(8,128)(2,1)S(1)}, bf16[4,128,256]{2,1,0:T(8,128)(2,1)S(1)}, u32[]{:S(2)}, u32[]{:S(2)}) collective-permute-start(bf16[4,128,256]{2,1,0:T(8,128)(2,1)S(1)} %get-tuple-element.35), channel_id=1, source_target_pairs={{0,0},{2,4},{4,2},{6,8},{8,6},{10,12},{12,10},{14,14},{1,1},{3,5},... | collective-permute-start | bytes 786440 | tf_op jit(solution)/shard_map/ppermute | solution.py:354
  5.5 1.0 %copy-done.6 = bf16[3,256,256]{2,1,0:T(8,128)(2,1)S(1)} copy-done((bf16[3,256,256]{2,1,0:T(8,128)(2,1)S(1)}, bf16[3,256,256]{2,1,0:T(8,128)(2,1)}, u32[]{:S(2)}) %copy-start.6) | copy-done | bytes 393240
  6.5 1.2 %grad_time.1 = (bf16[4,4,128,256]{3,2,1,0:T(8,128)(2,1)S(1)}, bf16[4,128,256]{2,1,0:T(8,128)(2,1)S(1)}, bf16[4,128,256]{2,1,0:T(8,128)(2,1)S(1)}) custom-call(bf16[4,4,128,256]{3,2,1,0:T(8,128)(2,1)S(1)} %copy-done.3, bf16[2,4,128,256]{3,2,1,0:T(8,128)(2,1)S(1)} %collective-permute-done.later_ref, bf16[3,256,256]{2,1,0:T(8,128)(2,1)S(1)} %copy-done.6), custom_call_target="tpu_custom_call" | custom-call | flops 1073741824 | bytes 3538944 | tf_op jit(solution)/shard_map/grad_time/pallas_call | solution.py:24
  7.8 1.7 %act.1 = (bf16[4,4,128,256]{3,2,1,0:T(8,128)(2,1)S(1)}, bf16[2,4,128,256]{3,2,1,0:T(8,128)(2,1)S(1)}, bf16[2,2,128,256]{3,2,1,0:T(8,128)(2,1)S(1)}) custom-call(bf16[4,4,128,256]{3,2,1,0:T(8,128)(2,1)S(1)} %copy-done.2, f32[1,256]{1,0:T(1,128)S(1)} %bitcast.2, bf16[3,3,256,256]{3,2,1,0:T(8,128)(2,1)S(1)} %copy-done), custom_call_target="tpu_custom_call" | custom-call | flops 1207959552 | bytes 4064256 | tf_op jit(solution)/shard_map/act/pallas_call | solution.py:24
  9.7 4.4 %collective-permute-start.2 = (bf16[4,128,256]{2,1,0:T(8,128)(2,1)S(1)}, bf16[4,128,256]{2,1,0:T(8,128)(2,1)S(1)}, u32[]{:S(2)}, u32[]{:S(2)}) collective-permute-start(bf16[4,128,256]{2,1,0:T(8,128)(2,1)S(1)} %get-tuple-element.38), channel_id=1, source_target_pairs={{0,0},{2,4},{4,2},{6,8},{8,6},{10,12},{12,10},{14,14},{1,1},{3,5},... | collective-permute-start | bytes 786440 | tf_op jit(solution)/shard_map/ppermute | solution.py:354
  14.1 1.0 %grad_own.1.grad_ref = f32[2,4,128,256]{3,2,1,0:T(8,128)S(1)} custom-call(bf16[4,4,128,256]{3,2,1,0:T(8,128)(2,1)S(1)} %get-tuple-element.39.d_ref, bf16[3,3,256,256]{3,2,1,0:T(8,128)(2,1)S(1)} %copy-done.1), custom_call_target="tpu_custom_call" | custom-call | flops 805306368 | bytes 3276800 | tf_op jit(solution)/shard_map/grad_own/pallas_call | solution.py:24
  15.1 6.8 %collective-permute-done.3.own_ref = bf16[4,128,256]{2,1,0:T(8,128)(2,1)S(1)} collective-permute-done((bf16[4,128,256]{2,1,0:T(8,128)(2,1)S(1)}, bf16[4,128,256]{2,1,0:T(8,128)(2,1)S(1)}, u32[]{:S(2)}, u32[]{:S(2)}) %collective-permute-start.3) | collective-permute-done | bytes 262176 | tf_op jit(solution)/shard_map/ppermute | solution.py:354
  21.9 1.5 %act_rim.1 = (bf16[2,4,128,256]{3,2,1,0:T(8,128)(2,1)S(1)}, bf16[2,128,256]{2,1,0:T(8,128)(2,1)S(1)}, bf16[2,128,256]{2,1,0:T(8,128)(2,1)S(1)}) custom-call(bf16[4,128,256]{2,1,0:T(8,128)(2,1)S(1)} %collective-permute-done.3.own_ref, bf16[4,128,256]{2,1,0:T(8,128)(2,1)S(1)} %collective-permute-done.4.other_ref, ...), custom_call_target="tpu_custom_call" | custom-call | flops 1207959552 | bytes 3539968 | tf_op jit(solution)/shard_map/act_rim/pallas_call | solution.py:24
  23.5 0.5 %collective-permute-start.6 = (bf16[2,128,256]{2,1,0:T(8,128)(2,1)S(1)}, bf16[2,128,256]{2,1,0:T(8,128)(2,1)S(1)}, u32[]{:S(2)}, u32[]{:S(2)}) collective-permute-start(bf16[2,128,256]{2,1,0:T(8,128)(2,1)S(1)} %get-tuple-element.47), channel_id=1, source_target_pairs={{0,1},{1,0},{2,3},{3,2},{4,5},{5,4},{6,7},{7,6},{8,9},{9,8},{10,11... | collective-permute-start | bytes 393224 | tf_op jit(solution)/shard_map/ppermute | solution.py:360
  24.0 2.0 %hidden.1 = (bf16[2,4,128,256]{3,2,1,0:T(8,128)(2,1)S(1)}, bf16[2,2,128,256]{3,2,1,0:T(8,128)(2,1)S(1)}) custom-call(bf16[2,4,128,256]{3,2,1,0:T(8,128)(2,1)S(1)} %get-tuple-element.41.s_ref, bf16[2,2,128,256]{3,2,1,0:T(8,128)(2,1)S(1)} %collective-permute-done.7.early_ref, bf16[4,4,128,256]{3,2,1,0:T(8,128)(2,1)S(1)} %get-tuple-element.39.d_ref, ...), custom_call_target="tpu_custom_call" | custom-call | flops 1610612736 | bytes 4195328 | tf_op jit(solution)/shard_map/hidden/pallas_call | solution.py:24
  26.0 1.0 %hidden_own.1 = (f32[2,4,128,256]{3,2,1,0:T(8,128)S(1)}, f32[2,4,128,256]{3,2,1,0:T(8,128)S(1)}) custom-call(bf16[2,4,128,256]{3,2,1,0:T(8,128)(2,1)S(1)} %get-tuple-element.45.s_ref, bf16[2,128,256]{2,1,0:T(8,128)(2,1)S(1)} %collective-permute-done.5.first_ref, bf16[2,128,256]{2,1,0:T(8,128)(2,1)S(1)} %collective-permute-done.6.last_ref, ...), custom_call_target="tpu_custom_call" | custom-call | flops 402653184 | bytes 3277824 | tf_op jit(solution)/shard_map/hidden_own/pallas_call | solution.py:24
  27.1 0.5 %hidden_rim.2.dh_ref = bf16[2,2,128,256]{3,2,1,0:T(8,128)(2,1)S(1)} custom-call(bf16[4,128,256]{2,1,0:T(8,128)(2,1)S(1)} %collective-permute-done.1.own_ref, bf16[4,128,256]{2,1,0:T(8,128)(2,1)S(1)} %collective-permute-done.2.other_ref, bf16[3,3,256,256]{3,2,1,0:T(8,128)(2,1)S(1)} %copy-done.1, f32[2,4,128,256]{3,2,1,0:T(8,128)S(1)} %grad_own.1.grad_ref, ...), custom_call_target="tpu_custom_call" | custom-call | flops 201326592 | bytes 5111808 | tf_op jit(solution)/shard_map/hidden_rim/pallas_call | solution.py:24
  28.2 0.5 %hidden_rim.3.next_ref.dh_ref = bf16[2,2,128,256]{3,2,1,0:T(8,128)(2,1)S(1)} custom-call(bf16[4,128,256]{2,1,0:T(8,128)(2,1)S(1)} %collective-permute-done.1.own_ref, bf16[4,128,256]{2,1,0:T(8,128)(2,1)S(1)} %collective-permute-done.2.other_ref, bf16[3,3,256,256]{3,2,1,0:T(8,128)(2,1)S(1)} %copy-done.1, f32[2,4,128,256]{3,2,1,0:T(8,128)S(1)} %grad_own.1.grad_ref, ...), custom_call_target="tpu_custom_call" | custom-call | flops 201326592 | bytes 5111808 | tf_op jit(solution)/shard_map/hidden_rim/pallas_call | solution.py:24
  28.7 0.5 %back_first.1.first_ref = bf16[2,2,128,256]{3,2,1,0:T(8,128)(2,1)S(1)} custom-call(bf16[2,2,128,256]{3,2,1,0:T(8,128)(2,1)S(1)} %hidden_rim.2.dh_ref, bf16[2,2,128,256]{3,2,1,0:T(8,128)(2,1)S(1)} %hidden_rim.3.next_ref.dh_ref, bf16[3,256,256]{2,1,0:T(8,128)(2,1)S(1)} %copy-done.4), custom_call_target="tpu_custom_call" | custom-call | flops 268435456 | bytes 1179648 | tf_op jit(solution)/shard_map/back_first/pallas_call | solution.py:24
  29.7 3.9 %collective-permute-start.11 = (bf16[4,128,256]{2,1,0:T(8,128)(2,1)S(1)}, bf16[4,128,256]{2,1,0:T(8,128)(2,1)S(1)}, u32[]{:S(2)}, u32[]{:S(2)}) collective-permute-start(bf16[4,128,256]{2,1,0:T(8,128)(2,1)S(1)} %get-tuple-element.62), channel_id=1, source_target_pairs={{0,0},{2,4},{4,2},{6,8},{8,6},{10,12},{12,10},{14,14},{1,1},{3,5},... | collective-permute-start | bytes 786440 | tf_op jit(solution)/shard_map/ppermute | solution.py:354
  33.7 0.7 %back_time.1.din_ref = bf16[2,4,128,256]{3,2,1,0:T(8,128)(2,1)S(1)} custom-call(bf16[2,4,128,256]{3,2,1,0:T(8,128)(2,1)S(1)} %get-tuple-element.50.dh_ref, bf16[2,2,128,256]{3,2,1,0:T(8,128)(2,1)S(1)} %collective-permute-done.10.later_ref, bf16[3,256,256]{2,1,0:T(8,128)(2,1)S(1)} %copy-done.4), custom_call_target="tpu_custom_call" | custom-call | flops 536870912 | bytes 1703936 | tf_op jit(solution)/shard_map/back_time/pallas_call | solution.py:24
  34.4 1.4 %out_own.1 = (bf16[2,4,128,256]{3,2,1,0:T(8,128)(2,1)S(1)}, f32[2,4,128,256]{3,2,1,0:T(8,128)S(1)}, f32[2,4,128,256]{3,2,1,0:T(8,128)S(1)}, f32[2,4,128,256]{3,2,1,0:T(8,128)S(1)}) custom-call(bf16[4,4,128,256]{3,2,1,0:T(8,128)(2,1)S(1)} %copy-done.2, bf16[4,4,128,256]{3,2,1,0:T(8,128)(2,1)S(1)} %copy-done.3, bf16[2,4,128,256]{3,2,1,0:T(8,128)(2,1)S(1)} %back_time.1.din_ref, ...), custom_call_target="tpu_custom_call" | custom-call | flops 805306368 | bytes 7996416 | tf_op jit(solution)/shard_map/out_own/pallas_call | solution.py:24
  35.9 2.6 %out.1._ = bf16[4,4,128,256]{3,2,1,0:T(8,128)(2,1)} custom-call(bf16[4,4,128,256]{3,2,1,0:T(8,128)(2,1)S(1)} %copy-done.2, bf16[4,4,128,256]{3,2,1,0:T(8,128)(2,1)S(1)} %copy-done.3, bf16[2,4,128,256]{3,2,1,0:T(8,128)(2,1)S(1)} %back_time.1.din_ref, bf16[2,4,128,256]{3,2,1,0:T(8,128)(2,1)S(1)} %get-tuple-element.57.drim_ref, f32[1,256]{1,0:T(1,128)S(1)} %bitcast.5, ...), custom_call_target="tpu_custom_call" | custom-call | flops 1207959552 | bytes 5374976 | tf_op jit(solution)/shard_map/out/pallas_call | solution.py:24
  38.5 2.5 %collective-permute-done.11.halo_ref = bf16[4,128,256]{2,1,0:T(8,128)(2,1)S(1)} collective-permute-done((bf16[4,128,256]{2,1,0:T(8,128)(2,1)S(1)}, bf16[4,128,256]{2,1,0:T(8,128)(2,1)S(1)}, u32[]{:S(2)}, u32[]{:S(2)}) %collective-permute-start.11) | collective-permute-done | bytes 262176 | tf_op jit(solution)/shard_map/ppermute | solution.py:354
  41.0 1.3 %out_rim.2._ = bf16[4,4,128,256]{3,2,1,0:T(8,128)(2,1)} custom-call(bf16[4,128,256]{2,1,0:T(8,128)(2,1)S(1)} %collective-permute-done.11.halo_ref, bf16[3,3,256,256]{3,2,1,0:T(8,128)(2,1)S(1)} %copy-done, bf16[2,4,128,256]{3,2,1,0:T(8,128)(2,1)S(1)} %get-tuple-element.58.passed_ref, ...), custom_call_target="tpu_custom_call", output_to_operand_aliasing={{}: (6, {})} | custom-call | tf_op jit(solution)/shard_map/out_rim/pallas_call | solution.py:24
  42.2 1.6 %collective-permute-done.9.halo_ref = bf16[528,256]{1,0:T(8,128)(2,1)S(1)} collective-permute-done((bf16[528,256]{1,0:T(8,128)(2,1)S(1)}, bf16[528,256]{1,0:T(8,128)(2,1)S(1)}, u32[]{:S(2)}, u32[]{:S(2)}) %collective-permute-start.9) | collective-permute-done | bytes 270368 | tf_op jit(solution)/shard_map/ppermute | solution.py:354
  43.8 1.3 %out_rim.3 = bf16[4,4,128,256]{3,2,1,0:T(8,128)(2,1)} custom-call(bf16[528,256]{1,0:T(8,128)(2,1)S(1)} %collective-permute-done.9.halo_ref, bf16[3,3,256,256]{3,2,1,0:T(8,128)(2,1)S(1)} %copy-done, bf16[2,4,128,256]{3,2,1,0:T(8,128)(2,1)S(1)} %get-tuple-element.58.passed_ref, ...), custom_call_target="tpu_custom_call", output_to_operand_aliasing={{}: (6, {})} | custom-call | tf_op jit(solution)/shard_map/out_rim/pallas_call | solution.py:24
  (33 shorter events, 1.5 us)
Async XLA Ops:
  0.0 1.4 %copy-start.2 = (bf16[4,4,128,256]{3,2,1,0:T(8,128)(2,1)S(1)}, bf16[4,4,128,256]{3,2,1,0:T(8,128)(2,1)}, u32[]{:S(2)}) copy-start(bf16[4,4,128,256]{3,2,1,0:T(8,128)(2,1)} %x_ref.7) | copy-start | bytes 3145732
  0.0 5.5 %copy-start.3 = (bf16[4,4,128,256]{3,2,1,0:T(8,128)(2,1)S(1)}, bf16[4,4,128,256]{3,2,1,0:T(8,128)(2,1)}, u32[]{:S(2)}) copy-start(bf16[4,4,128,256]{3,2,1,0:T(8,128)(2,1)} %g_ref.2) | copy-start | bytes 3145732
  1.2 4.2 %collective-permute-start = (bf16[2,4,128,256]{3,2,1,0:T(8,128)(2,1)S(1)}, bf16[2,4,128,256]{3,2,1,0:T(8,128)(2,1)S(1)}, u32[]{:S(2)}, u32[]{:S(2)}) collective-permute-start(bf16[2,4,128,256]{3,2,1,0:T(8,128)(2,1)S(1)} %slice.3), channel_id=1, source_target_pairs={{1,0},{0,1},{3,2},{2,3},{5,4},{4,5},{7,6},{6,7},{9,8},{8,9},{11,10... | collective-permute-start | bytes 1572872 | tf_op jit(solution)/shard_map/ppermute | solution.py:363
  1.4 20.4 %collective-permute-start.3 = (bf16[4,128,256]{2,1,0:T(8,128)(2,1)S(1)}, bf16[4,128,256]{2,1,0:T(8,128)(2,1)S(1)}, u32[]{:S(2)}, u32[]{:S(2)}) collective-permute-start(bf16[4,128,256]{2,1,0:T(8,128)(2,1)S(1)} %get-tuple-element.34), channel_id=1, source_target_pairs={{0,2},{2,0},{4,6},{6,4},{8,10},{10,8},{12,14},{14,12},{1,3},{3,1},... | collective-permute-start | bytes 786440 | tf_op jit(solution)/shard_map/ppermute | solution.py:354
  3.0 4.7 %copy-start = (bf16[3,3,256,256]{3,2,1,0:T(8,128)(2,1)S(1)}, bf16[3,3,256,256]{3,2,1,0:T(8,128)(2,1)}, u32[]{:S(2)}) copy-start(bf16[3,3,256,256]{3,2,1,0:T(8,128)(2,1)} %k_ref.19) | copy-start | bytes 3538948
  3.0 4.7 %copy-start.5 = (f32[256]{0:T(256)S(1)}, f32[256]{0:T(256)}, u32[]{:S(2)}) copy-start(f32[256]{0:T(256)} %param.10) | copy-start | bytes 3076
  3.0 18.9 %collective-permute-start.4 = (bf16[4,128,256]{2,1,0:T(8,128)(2,1)S(1)}, bf16[4,128,256]{2,1,0:T(8,128)(2,1)S(1)}, u32[]{:S(2)}, u32[]{:S(2)}) collective-permute-start(bf16[4,128,256]{2,1,0:T(8,128)(2,1)S(1)} %get-tuple-element.35), channel_id=1, source_target_pairs={{0,0},{2,4},{4,2},{6,8},{8,6},{10,12},{12,10},{14,14},{1,1},{3,5},... | collective-permute-start | bytes 786440 | tf_op jit(solution)/shard_map/ppermute | solution.py:354
  5.5 1.0 %copy-start.6 = (bf16[3,256,256]{2,1,0:T(8,128)(2,1)S(1)}, bf16[3,256,256]{2,1,0:T(8,128)(2,1)}, u32[]{:S(2)}) copy-start(bf16[3,256,256]{2,1,0:T(8,128)(2,1)} %k_ref.10) | copy-start | bytes 1179652
  7.8 6.3 %copy-start.1 = (bf16[3,3,256,256]{3,2,1,0:T(8,128)(2,1)S(1)}, bf16[3,3,256,256]{3,2,1,0:T(8,128)(2,1)}, u32[]{:S(2)}) copy-start(bf16[3,3,256,256]{3,2,1,0:T(8,128)(2,1)} %ks_ref.5) | copy-start | bytes 3538948
  9.5 14.5 %collective-permute-start.7 = (bf16[2,2,128,256]{3,2,1,0:T(8,128)(2,1)S(1)}, bf16[2,2,128,256]{3,2,1,0:T(8,128)(2,1)S(1)}, u32[]{:S(2)}, u32[]{:S(2)}) collective-permute-start(bf16[2,2,128,256]{3,2,1,0:T(8,128)(2,1)S(1)} %get-tuple-element.48), channel_id=1, source_target_pairs={{0,1},{1,0},{2,3},{3,2},{4,5},{5,4},{6,7},{7,6},{8,9},{9,8},{10,11... | collective-permute-start | bytes 786440 | tf_op jit(solution)/shard_map/ppermute | solution.py:360
  9.6 17.5 %collective-permute-start.1 = (bf16[4,128,256]{2,1,0:T(8,128)(2,1)S(1)}, bf16[4,128,256]{2,1,0:T(8,128)(2,1)S(1)}, u32[]{:S(2)}, u32[]{:S(2)}) collective-permute-start(bf16[4,128,256]{2,1,0:T(8,128)(2,1)S(1)} %get-tuple-element.37), channel_id=1, source_target_pairs={{0,2},{2,0},{4,6},{6,4},{8,10},{10,8},{12,14},{14,12},{1,3},{3,1},... | collective-permute-start | bytes 786440 | tf_op jit(solution)/shard_map/ppermute | solution.py:354
  9.7 17.4 %collective-permute-start.2 = (bf16[4,128,256]{2,1,0:T(8,128)(2,1)S(1)}, bf16[4,128,256]{2,1,0:T(8,128)(2,1)S(1)}, u32[]{:S(2)}, u32[]{:S(2)}) collective-permute-start(bf16[4,128,256]{2,1,0:T(8,128)(2,1)S(1)} %get-tuple-element.38), channel_id=1, source_target_pairs={{0,0},{2,4},{4,2},{6,8},{8,6},{10,12},{12,10},{14,14},{1,1},{3,5},... | collective-permute-start | bytes 786440 | tf_op jit(solution)/shard_map/ppermute | solution.py:354
  21.9 2.1 %copy-start.4 = (bf16[3,256,256]{2,1,0:T(8,128)(2,1)S(1)}, bf16[3,256,256]{2,1,0:T(8,128)(2,1)}, u32[]{:S(2)}) copy-start(bf16[3,256,256]{2,1,0:T(8,128)(2,1)} %k_ref.15) | copy-start | bytes 1179652
  21.9 2.1 %copy-start.7 = (f32[256]{0:T(256)S(1)}, f32[256]{0:T(256)}, u32[]{:S(2)}) copy-start(f32[256]{0:T(256)} %param.11) | copy-start | bytes 3076
  23.4 2.6 %collective-permute-start.5 = (bf16[2,128,256]{2,1,0:T(8,128)(2,1)S(1)}, bf16[2,128,256]{2,1,0:T(8,128)(2,1)S(1)}, u32[]{:S(2)}, u32[]{:S(2)}) collective-permute-start(bf16[2,128,256]{2,1,0:T(8,128)(2,1)S(1)} %get-tuple-element.46), channel_id=1, source_target_pairs={{0,1},{1,0},{2,3},{3,2},{4,5},{5,4},{6,7},{7,6},{8,9},{9,8},{10,11... | collective-permute-start | bytes 393224 | tf_op jit(solution)/shard_map/ppermute | solution.py:360
  23.5 2.5 %collective-permute-start.6 = (bf16[2,128,256]{2,1,0:T(8,128)(2,1)S(1)}, bf16[2,128,256]{2,1,0:T(8,128)(2,1)S(1)}, u32[]{:S(2)}, u32[]{:S(2)}) collective-permute-start(bf16[2,128,256]{2,1,0:T(8,128)(2,1)S(1)} %get-tuple-element.47), channel_id=1, source_target_pairs={{0,1},{1,0},{2,3},{3,2},{4,5},{5,4},{6,7},{7,6},{8,9},{9,8},{10,11... | collective-permute-start | bytes 393224 | tf_op jit(solution)/shard_map/ppermute | solution.py:360
  27.6 1.6 %collective-permute-start.8 = (bf16[2,2,128,256]{3,2,1,0:T(8,128)(2,1)S(1)}, bf16[2,2,128,256]{3,2,1,0:T(8,128)(2,1)S(1)}, u32[]{:S(2)}, u32[]{:S(2)}) collective-permute-start(bf16[2,2,128,256]{3,2,1,0:T(8,128)(2,1)S(1)} %hidden_rim.2.dh_ref), channel_id=1, source_target_pairs={{1,0},{0,1},{3,2},{2,3},{5,4},{4,5},{7,6},{6,7},{9,8},{8,9},{11,10... | collective-permute-start | bytes 786440 | tf_op jit(solution)/shard_map/ppermute | solution.py:363
  27.8 5.9 %collective-permute-start.10 = (bf16[2,2,128,256]{3,2,1,0:T(8,128)(2,1)S(1)}, bf16[2,2,128,256]{3,2,1,0:T(8,128)(2,1)S(1)}, u32[]{:S(2)}, u32[]{:S(2)}) collective-permute-start(bf16[2,2,128,256]{3,2,1,0:T(8,128)(2,1)S(1)} %get-tuple-element.56), channel_id=1, source_target_pairs={{1,0},{0,1},{3,2},{2,3},{5,4},{4,5},{7,6},{6,7},{9,8},{8,9},{11,10... | collective-permute-start | bytes 786440 | tf_op jit(solution)/shard_map/ppermute | solution.py:363
  29.7 14.2 %collective-permute-start.9 = (bf16[528,256]{1,0:T(8,128)(2,1)S(1)}, bf16[528,256]{1,0:T(8,128)(2,1)S(1)}, u32[]{:S(2)}, u32[]{:S(2)}) collective-permute-start(bf16[528,256]{1,0:T(8,128)(2,1)S(1)} %get-tuple-element.55), channel_id=1, source_target_pairs={{0,2},{2,0},{4,6},{6,4},{8,10},{10,8},{12,14},{14,12},{1,3},{3,1},... | collective-permute-start | bytes 811016 | tf_op jit(solution)/shard_map/ppermute | solution.py:354
  29.7 11.2 %collective-permute-start.11 = (bf16[4,128,256]{2,1,0:T(8,128)(2,1)S(1)}, bf16[4,128,256]{2,1,0:T(8,128)(2,1)S(1)}, u32[]{:S(2)}, u32[]{:S(2)}) collective-permute-start(bf16[4,128,256]{2,1,0:T(8,128)(2,1)S(1)} %get-tuple-element.62), channel_id=1, source_target_pairs={{0,0},{2,4},{4,2},{6,8},{8,6},{10,12},{12,10},{14,14},{1,1},{3,5},... | collective-permute-start | bytes 786440 | tf_op jit(solution)/shard_map/ppermute | solution.py:354
